TPU v7x, 32 devices: a whole 2x2x4 slice. The times are simulated.
32 devices in a mesh: lon: 8 (over y, x, core), lat: 2 (over z_hi), depth: 2 (over z_lo).
Axes of the slice: x: 2, y: 2, z: 4 (z_hi: 2, z_lo: 2; z = z_hi * 2 + z_lo), core: 2. Of those that a mesh axis runs over, the one named last changes fastest.
Arguments:
- adj_temp: float32 [96, 16, 1024], P('depth', 'lat', 'lon'), may hold values from -6 to 6
- adj_salt: float32 [96, 16, 1024], P('depth', 'lat', 'lon'), may hold values from -6 to 6
- adj_zonal: float32 [96, 16, 1024], P('depth', 'lat', 'lon'), may hold values from -6 to 6
- adj_merid: float32 [96, 16, 1024], P('depth', 'lat', 'lon'), may hold values from -6 to 6
- east_speed: float32 [96, 16, 1024], P('depth', 'lat', 'lon'), may hold values from -4 to 4
- north_speed: float32 [96, 16, 1024], P('depth', 'lat', 'lon'), may hold values from -4 to 4
- branch_flags: int32 [2, 96, 16, 1024], P(None, 'depth', 'lat', 'lon'), may hold values from 0 to 8
- sea_mask: int32 [96, 16, 1024], P('depth', 'lat', 'lon'), may hold values 0 or 1
- block_inverse: float32 [16, 96, 48], P('lat', 'depth'), may hold values from -1 to 1, as said below
- coupling: float32 [16], P('lat'), may hold values from 0.3 to 0.9
Outputs:
- grad_temp: float32 [96, 16, 1024], P('depth', 'lat', 'lon')
- grad_salt: float32 [96, 16, 1024], P('depth', 'lat', 'lon')
- grad_zonal: float32 [96, 16, 1024], P('depth', 'lat', 'lon')
- grad_merid: float32 [96, 16, 1024], P('depth', 'lat', 'lon')
Inputs may be any that keep to these rules, and one draw needn't show every extreme that they name: `branch_flags`: a flag is 3 times the branch of the north face plus the branch of the east face. `sea_mask`: 1 marks a sea cell. `block_inverse`: the diagonal entries of every 48 x 48 block lie between 0.4 and 1, the other entries between -0.5 / 48 and 0.5 / 48.
All inputs are finite; a program needn't handle non-finite values. No bound on the sum of `sea_mask` on one device may be relied on, other than what follows from the above.
Results may differ from a plain program's by a relative error of at most 0.00016.
Values sent between devices are 32-bit elements; how exact they have to be, the bound alone decides.
No kernel may reach another device: no remote copies, remote signals or barrier semaphores. Data moves between devices by JAX's collectives and lax.ppermute only.
A program may use at most 64 MiB of HBM per device.

v0:
```python
import jax
import jax.numpy as jnp
from jax import lax
from jax.sharding import PartitionSpec as P

STEPS = 2


advect_scale = 0.25
diffusion = 0.5
gravity = 0.1
pressure_scale = 1.0
viscosity = 0.1
haline = 0.8


def partner(value, axis, apart):
    mask = 2**apart
    pairs = [(source, source ^ mask) for source in range(lax.axis_size(axis))]
    return lax.ppermute(value, axis, pairs)


def with_halo(block, sides, width, periodic):
    for axis, dim in sides:
        count = lax.axis_size(axis)
        forward = [(i, i + 1) for i in range(count - 1)]
        if periodic:
            forward.append((count - 1, 0))
        backward = [(target, source) for source, target in forward]
        low = lax.ppermute(
            lax.slice_in_dim(block, block.shape[dim] - width, None, axis=dim), axis, forward
        )
        high = lax.ppermute(lax.slice_in_dim(block, 0, width, axis=dim), axis, backward)
        block = jnp.concatenate([low, block, high], axis=dim)
    return block


def entering(part, axis, combine, identity):
    count = lax.axis_size(axis)
    place = lax.axis_index(axis)
    ahead = count - 1 - place
    gathered = lax.all_gather(part, axis)
    state = jnp.zeros_like(part) + jnp.asarray(identity, part.dtype)

    def one(hop, state):
        source = count - 1 - hop
        return combine(state, lax.dynamic_index_in_dim(gathered, source, 0, False))

    return lax.fori_loop(0, ahead, one, state)


def project(stack, inverse):
    return jnp.einsum("yjk,fjyx->fkyx", inverse, stack, precision=lax.Precision.HIGHEST)


def interface(projected, inverse, edge):
    spike_row = lax.dynamic_index_in_dim(inverse, edge, 1, keepdims=False)
    corner = lax.dynamic_index_in_dim(spike_row, edge, 1, keepdims=False)
    plane = lax.dynamic_index_in_dim(projected, edge, 1, keepdims=False)
    return (spike_row, corner, plane)


def finish(projected, spike_row, corner, plane, other_corner, other_plane, coupling):
    divisor = 1.0 - coupling * coupling * corner * other_corner
    carried = (other_plane + (coupling * other_corner)[:, None] * plane) / divisor[:, None]
    return projected + (coupling[:, None] * spike_row).T[None, :, :, None] * carried[:, None]


def face_terms(lon_extra, lat_extra, east_self, north_self, sea):
    sea_lon = lon_extra[0]
    sea_lat = lat_extra[0]
    east_own = east_self * sea_lon[..., 2:][None]
    west_own = lon_extra[1:, ..., :-2] * sea[None]
    north_own = north_self * sea_lat[:, 2:, :][None]
    south_own = lat_extra[1:, :, :-2, :] * sea[None]
    return (east_own, west_own, north_own, south_own, sea_lon, sea_lat)


def add_sums(earlier, later):
    return earlier + later


def on_device(
    adj_temp,
    adj_salt,
    adj_zonal,
    adj_merid,
    east_speed,
    north_speed,
    branch_flags,
    sea_mask,
    block_inverse,
    coupling,
):
    levels, rows, cols = adj_temp.shape
    sea = sea_mask.astype(jnp.float32)
    zonal_branch = (branch_flags % 3).astype(jnp.float32) * 0.5
    merid_branch = (branch_flags // 3).astype(jnp.float32) * 0.5
    east_self = sea[None] * (east_speed[None] * (1.0 - zonal_branch) + diffusion)
    east_next = sea[None] * (east_speed[None] * zonal_branch - diffusion)
    north_self = sea[None] * (north_speed[None] * (1.0 - merid_branch) + diffusion)
    north_next = sea[None] * (north_speed[None] * merid_branch - diffusion)
    lon_coef = jnp.concatenate([sea[None], east_next], axis=0)
    lat_coef = jnp.concatenate([sea[None], north_next], axis=0)
    global_rows = rows * lax.axis_size("lat")
    row_index = lax.axis_index("lat") * rows + jnp.arange(rows)
    coriolis = (0.2 + 0.6 * (row_index.astype(jnp.float32) + 0.5) / global_rows)[None, :, None]
    edge = (levels - 1) * (1 - lax.axis_index("depth"))
    scale = jnp.array([advect_scale, advect_scale, 1.0, 1.0], jnp.float32)[:, None, None, None]
    triangle = (jnp.arange(levels)[None, :] >= jnp.arange(levels)[:, None]).astype(jnp.float32)
    state = jnp.stack([adj_temp, adj_salt, adj_zonal, adj_merid])
    for step_index in reversed(range(STEPS)):
        first = step_index == STEPS - 1
        projected = project(state, block_inverse)
        spike_row, corner, plane = interface(projected, block_inverse, edge)
        other_plane, other_corner = partner((plane, corner), "depth", 0)
        solved = finish(projected, spike_row, corner, plane, other_corner, other_plane, coupling)
        weighted = sea[None] * solved
        outgoing = scale * weighted
        lon_payload = jnp.concatenate([outgoing, lon_coef], axis=0) if first else outgoing
        lat_payload = jnp.concatenate([outgoing, lat_coef], axis=0) if first else outgoing
        lon_wide = with_halo(lon_payload, (("lon", 3),), 1, True)
        lat_wide = with_halo(lat_payload, (("lat", 2),), 1, False)
        if first:
            faces = face_terms(lon_wide[4:], lat_wide[4:], east_self, north_self, sea)
        east_own, west_own, north_own, south_own, sea_lon, sea_lat = faces
        lon_rims = lon_wide[:4]
        lat_rims = lat_wide[:4]
        east_part = east_own[step_index] * (
            lon_rims[:2, ..., 2:] - lon_rims[:2, ..., 1:-1]
        ) + west_own[step_index] * (lon_rims[:2, ..., 1:-1] - lon_rims[:2, ..., :-2])
        north_part = north_own[step_index] * (
            lat_rims[:2, :, 2:] - lat_rims[:2, :, 1:-1]
        ) + south_own[step_index] * (lat_rims[:2, :, 1:-1] - lat_rims[:2, :, :-2])
        tracers = weighted[:2] + east_part + north_part
        beside_all = (
            lon_rims[2:, ..., 2:]
            + lon_rims[2:, ..., :-2]
            + lat_rims[2:, :, 2:]
            + lat_rims[2:, :, :-2]
            - 4.0 * weighted[2:]
        )
        zonal = weighted[2] - coriolis * weighted[3] + viscosity * beside_all[0]
        merid = weighted[3] + coriolis * weighted[2] + viscosity * beside_all[1]
        pressure = (
            -0.5
            * pressure_scale
            * (
                lon_rims[2, ..., :-2]
                - lon_rims[2, ..., 2:]
                + lat_rims[3, :, :-2]
                - lat_rims[3, :, 2:]
            )
        )
        below = jnp.einsum("kj,jyx->kyx", triangle, pressure, precision=lax.Precision.HIGHEST)
        deeper = entering(below[0], "depth", add_sums, jnp.zeros_like(below[0]))
        buoyancy = gravity * (below + deeper[None])
        state = jnp.stack([tracers[0] + buoyancy, tracers[1] - haline * buoyancy, zonal, merid])
    return (state[0], state[1], state[2], state[3])


def solution(mesh):
    in_specs = (
        P("depth", "lat", "lon"),
        P("depth", "lat", "lon"),
        P("depth", "lat", "lon"),
        P("depth", "lat", "lon"),
        P("depth", "lat", "lon"),
        P("depth", "lat", "lon"),
        P(None, "depth", "lat", "lon"),
        P("depth", "lat", "lon"),
        P("lat", "depth", None),
        P("lat"),
    )
    out_specs = (
        P("depth", "lat", "lon"),
        P("depth", "lat", "lon"),
        P("depth", "lat", "lon"),
        P("depth", "lat", "lon"),
    )
    return jax.shard_map(
        on_device, mesh=mesh, in_specs=in_specs, out_specs=out_specs, check_vma=False
    )
```

profile of v0, /device:TPU:0, one launch (start us, length us, event | category | flops | bytes accessed | tf_op | source)
XLA Modules:
  0.0 84.6 jit_solution(15763508087434768798)
XLA Ops:
  0.7 1.1 %copy_bitcast_fusion = (f32[1,48,8,128]{3,1,0,2:T(8,128)S(1)}, f32[1,48,8,128]{3,1,0,2:T(8,128)S(1)}) fusion(f32[48,8,128]{2,1,0:T(8,128)} %param.18, f32[48,8,128]{2,1,0:T(8,128)} %param.17), kind=kLoop, calls=%fused_computation.187 | loop fusion | bytes 786432 | tf_op jit(solution)/shard_map/stack | solution.py:111
  1.8 1.1 %copy_bitcast_fusion.2 = (f32[1,48,8,128]{3,1,0,2:T(8,128)S(1)}, f32[1,48,8,128]{3,1,0,2:T(8,128)S(1)}) fusion(f32[48,8,128]{2,1,0:T(8,128)} %param.16, f32[48,8,128]{2,1,0:T(8,128)} %param.15), kind=kLoop, calls=%fused_computation.189 | loop fusion | bytes 786432 | tf_op jit(solution)/shard_map/stack | solution.py:111
  3.0 0.8 fusion
  3.9 3.1 %collective-permute-start = (f32[4,8,128]{2,0,1:T(4,128)S(1)}, f32[4,8,128]{2,0,1:T(4,128)S(1)}, u32[]{:S(2)}, u32[]{:S(2)}) collective-permute-start(f32[4,8,128]{2,0,1:T(4,128)S(1)} %bitcast.136), channel_id=1, source_target_pairs={{0,1},{1,0},{2,3},{3,2},{4,5},{5,4},{6,7},{7,6},{8,9},{9,8},{10,11... | collective-permute-start | bytes 49160 | tf_op jit(solution)/shard_map/ppermute | solution.py:20
  7.0 0.2 dynamic-slice_reduce_fusion
  7.6 0.5 add_multiply_fusion.1
  8.1 2.7 %collective-permute-done.1 = f32[8]{0:T(128)S(1)} collective-permute-done((f32[8]{0:T(128)S(1)}, f32[8]{0:T(128)S(1)}, u32[]{:S(2)}, u32[]{:S(2)}) %collective-permute-start.1) | collective-permute-done | bytes 64 | tf_op jit(solution)/shard_map/ppermute | solution.py:20
  10.9 0.2 fusion.17
  11.1 1.1 %fusion.126 = (f32[4,48,8,128]{3,1,2,0:T(8,128)}, f32[4,48,8,128]{3,1,2,0:T(8,128)S(1)}) fusion(f32[4,48,8,128]{3,1,0,2:T(8,128)S(1)} %fusion.17, f32[4]{0:T(128)S(1)} %copy-done.29), kind=kLoop, calls=%fused_computation.218 | loop fusion | flops 196608 | bytes 2359312 | tf_op jit(solution)/shard_map/mul | solution.py:118
  12.3 0.3 pad_maximum_fusion
  12.6 0.8 fusion.123
  13.3 5.2 %collective-permute-start.4 = (f32[7,48,1,128]{3,1,2,0:T(8,128)}, f32[7,48,1,128]{3,1,2,0:T(8,128)}, u32[]{:S(2)}, u32[]{:S(2)}) collective-permute-start(f32[7,48,1,128]{3,1,2,0:T(8,128)} %get-tuple-element.167), channel_id=1, source_target_pairs={{0,2},{1,3},{4,6},{5,7},{8,10},{9,11},{12,14},{13,15},{16,18},{17,... | collective-permute-start | bytes 516104 | tf_op jit(solution)/shard_map/ppermute | solution.py:30
  18.5 1.3 %collective-permute-start.5 = (f32[7,48,1,128]{3,1,2,0:T(8,128)}, f32[7,48,1,128]{3,1,2,0:T(8,128)}, u32[]{:S(2)}, u32[]{:S(2)}) collective-permute-start(f32[7,48,1,128]{3,1,2,0:T(8,128)} %get-tuple-element.166), channel_id=1, source_target_pairs={{2,0},{3,1},{6,4},{7,5},{10,8},{11,9},{14,12},{15,13},{18,16},{19,... | collective-permute-start | bytes 516104 | tf_op jit(solution)/shard_map/ppermute | solution.py:33
  19.8 1.6 %fusion.122 = (f32[7,48,8,1]{3,1,2,0:T(8,128)S(1)}, f32[7,48,8,1]{3,1,2,0:T(8,128)}) fusion(f32[7,48,8,128]{3,1,2,0:T(8,128)S(1)} %get-tuple-element.172), kind=kLoop, calls=%fused_computation.214 | loop fusion | bytes 43008 | tf_op jit(solution)/shard_map/slice | solution.py:33
  21.3 2.4 %copy.97 = f32[7,48,8,1]{1,2,3,0:T(8,128)} copy(f32[7,48,8,1]{3,1,2,0:T(8,128)} %get-tuple-element.165) | data formatting | bytes 21504 | tf_op jit(solution)/shard_map/slice | solution.py:31
  23.8 1.1 %copy.98 = f32[7,48,8,1]{1,2,3,0:T(8,128)} copy(f32[7,48,8,1]{3,1,2,0:T(8,128)S(1)} %get-tuple-element.164) | data formatting | bytes 21504 | tf_op jit(solution)/shard_map/slice | solution.py:33
  24.9 2.6 %collective-permute-start.3 = (f32[7,48,8,1]{1,2,3,0:T(8,128)}, f32[7,48,8,1]{1,2,3,0:T(8,128)}, u32[]{:S(2)}, u32[]{:S(2)}) collective-permute-start(f32[7,48,8,1]{1,2,3,0:T(8,128)} %copy.98), channel_id=1, source_target_pairs={{4,0},{8,4},{12,8},{16,12},{20,16},{24,20},{28,24},{0,28},{5,1},{9... | collective-permute-start | bytes 32264 | tf_op jit(solution)/shard_map/ppermute | solution.py:33
  27.5 0.5 multiply_add_fusion
  28.1 1.6 %copy.93 = f32[48,8,128]{2,0,1:T(8,128)} copy(f32[48,8,128]{2,1,0:T(8,128)} %param.19) | data formatting | bytes 393216 | tf_op args[4]
  29.7 1.6 %copy.103 = f32[48,8,128]{2,0,1:T(8,128)} copy(f32[48,8,128]{2,1,0:T(8,128)} %param.20) | data formatting | bytes 393216 | tf_op args[5]
  31.3 1.2 %copy.99 = f32[7,48,8,1]{3,1,2,0:T(8,128)S(1)} copy(f32[7,48,8,1]{1,2,3,0:T(8,128)} %collective-permute-done.2) | data formatting | bytes 21504 | tf_op jit(solution)/shard_map/ppermute | solution.py:30
  32.6 2.3 %copy.100 = f32[7,48,8,1]{3,1,2,0:T(8,128)} copy(f32[7,48,8,1]{1,2,3,0:T(8,128)} %collective-permute-done.3) | data formatting | bytes 21504 | tf_op jit(solution)/shard_map/ppermute | solution.py:33
  34.9 1.1 %fusion.47 = f32[48,8,130]{2,0,1:T(8,128)S(1)} fusion(f32[7,48,8,1]{3,1,2,0:T(8,128)} %copy.100, f32[7,48,8,1]{3,1,2,0:T(8,128)S(1)} %copy.99, f32[2,48,8,128]{3,1,2,0:T(8,128)S(1)} %get-tuple-element.186, f32[1,48,8,128]{3,1,2,0:T(8,128)S(1)} %get-tuple-element.198, f32[4,48,8,128]{3,1,2,0:T(8,128)S(1)} %get-tuple-element.179), kind=kLoop, calls=%fused_computation.90 | loop fusion | flops 199680 | bytes 1597440 | tf_op jit(solution)/shard_map/squeeze | solution.py:70
  36.2 0.8 fusion.50
  37.1 1.1 %maximum_maximum_fusion = f32[7,48,9,128]{3,1,2,0:T(8,128)S(1)} fusion(f32[2,48,8,128]{3,1,2,0:T(8,128)S(1)} %get-tuple-element.187, f32[1,48,8,128]{3,1,2,0:T(8,128)S(1)} %get-tuple-element.198, f32[4,48,8,128]{3,1,2,0:T(8,128)S(1)} %get-tuple-element.179, f32[7,48,1,128]{3,1,2,0:T(8,128)} %collective-permute-done.4), kind=kLoop, calls=%fused_computation.2 | loop fusion | flops 1161216 | bytes 3096576 | tf_op jit(solution)/shard_map/concatenate | solution.py:34
  38.3 0.6 multiply_multiply_fusion.1
  38.9 0.5 copy-done.5
  39.4 0.8 slice_bitcast_fusion.5
  40.2 0.8 slice_bitcast_fusion.6
  41.0 0.8 slice_bitcast_fusion.7
  41.8 0.8 slice_bitcast_fusion.8
  42.5 1.2 %fusion.78 = f32[48,8,128]{2,0,1:T(8,128)S(1)} fusion(f32[7,48,1,128]{3,1,2,0:T(8,128)} %collective-permute-done.5, f32[2,48,8,128]{3,1,2,0:T(8,128)S(1)} %get-tuple-element.187, f32[1,48,8,128]{3,1,2,0:T(8,128)S(1)} %get-tuple-element.198, f32[4,48,8,128]{3,1,2,0:T(8,128)S(1)} %get-tuple-element.179, f32[7,48,1,128]{3,1,2,0:T(8,128)} %collective-permute-done.4, ...), kind=kOutput, calls=%fused_computation.150 | convolution fusion | flops 29100288 | bytes 2331648 | tf_op jit(solution)/shard_map/kj,jyx->kyx/dot_general | solution.py:155
  43.8 0.7 copy-done.9
  44.4 4.3 %all_gather.6 = f32[2,8,128]{2,1,0:T(8,128)S(1)} all-gather(f32[1,8,128]{2,1,0:T(8,128)S(1)} %bitcast.140), channel_id=1, replica_groups=mesh['lon'=8,'lat'=2,'depth'=2] {'depth'}, dimensions={0}, use_global_device_ids=true | all-gather | bytes 12288 | tf_op jit(solution)/shard_map/all_gather | solution.py:42
  48.9 1.7 %fusion.36 = f32[2,48,8,128]{3,1,0,2:T(8,128)S(1)} fusion(f32[4,48,8,128]{3,1,0,2:T(8,128)} %copy-done.3, f32[7,48,1,128]{3,1,2,0:T(8,128)} %collective-permute-done.4, f32[2,48,8,128]{3,1,2,0:T(8,128)S(1)} %get-tuple-element.187, f32[1,48,8,128]{3,1,2,0:T(8,128)S(1)} %get-tuple-element.198, f32[4,48,8,128]{3,1,2,0:T(8,128)S(1)} %get-tuple-element.179, ...), kind=kLoop, calls=%fused_computation.62 | loop fusion | flops 1671168 | bytes 2921472 | tf_op jit(solution)/shard_map/sub | solution.py:137
  50.6 0.1 fusion.73
  50.9 1.0 %copy-done.6 = f32[4,48,8,128]{3,1,2,0:T(8,128)S(1)} copy-done((f32[4,48,8,128]{3,1,2,0:T(8,128)S(1)}, f32[4,48,8,128]{3,1,2,0:T(8,128)}, u32[]{:S(2)}) %copy-start.6) | copy-done | bytes 786456
  51.8 1.4 %fusion.41 = f32[2,48,8,128]{3,1,2,0:T(8,128)S(1)} fusion(f32[7,48,9,128]{3,1,2,0:T(8,128)} %copy-done.5, f32[7,48,1,128]{3,1,2,0:T(8,128)} %collective-permute-done.5, f32[2,48,8,128]{3,1,2,0:T(8,128)S(1)} %get-tuple-element.187, f32[1,48,8,128]{3,1,2,0:T(8,128)S(1)} %get-tuple-element.198, f32[4,48,8,128]{3,1,2,0:T(8,128)S(1)} %get-tuple-element.179, ...), kind=kLoop, calls=%fused_computation.78 | loop fusion | flops 2064384 | bytes 7053312 | tf_op jit(solution)/shard_map/add | solution.py:135
  53.3 0.8 fusion.8
  54.2 0.5 collective-permute-start.6
  54.7 3.3 %collective-permute-done.6 = f32[4,8,128]{2,0,1:T(4,128)S(1)} collective-permute-done((f32[4,8,128]{2,0,1:T(4,128)S(1)}, f32[4,8,128]{2,0,1:T(4,128)S(1)}, u32[]{:S(2)}, u32[]{:S(2)}) %collective-permute-start.6) | collective-permute-done | bytes 16416 | tf_op jit(solution)/shard_map/ppermute | solution.py:20
  58.1 0.2 broadcast_multiply_fusion
  58.4 0.7 fusion.125
  59.1 6.1 %collective-permute-start.10 = (f32[4,48,1,128]{3,1,2,0:T(8,128)}, f32[4,48,1,128]{3,1,2,0:T(8,128)S(1)}, u32[]{:S(2)}, u32[]{:S(2)}) collective-permute-start(f32[4,48,1,128]{3,1,2,0:T(8,128)} %get-tuple-element.177), channel_id=1, source_target_pairs={{0,2},{1,3},{4,6},{5,7},{8,10},{9,11},{12,14},{13,15},{16,18},{17,... | collective-permute-start | bytes 294920 | tf_op jit(solution)/shard_map/ppermute | solution.py:30
  65.2 1.3 %collective-permute-start.9 = (f32[4,48,1,128]{3,1,2,0:T(8,128)}, f32[4,48,1,128]{3,1,2,0:T(8,128)S(1)}, u32[]{:S(2)}, u32[]{:S(2)}) collective-permute-start(f32[4,48,1,128]{3,1,2,0:T(8,128)} %get-tuple-element.176), channel_id=1, source_target_pairs={{2,0},{3,1},{6,4},{7,5},{10,8},{11,9},{14,12},{15,13},{18,16},{19,... | collective-permute-start | bytes 294920 | tf_op jit(solution)/shard_map/ppermute | solution.py:33
  66.5 0.3 fusion.124
  66.7 0.3 copy.118
  67.1 0.3 copy.116
  67.4 2.7 %collective-permute-start.7 = (f32[4,48,8,1]{1,2,3,0:T(8,128)S(1)}, f32[4,48,8,1]{1,2,3,0:T(8,128)}, u32[]{:S(2)}, u32[]{:S(2)}) collective-permute-start(f32[4,48,8,1]{1,2,3,0:T(8,128)S(1)} %copy.116), channel_id=1, source_target_pairs={{4,0},{8,4},{12,8},{16,12},{20,16},{24,20},{28,24},{0,28},{5,1},{9... | collective-permute-start | bytes 18440 | tf_op jit(solution)/shard_map/ppermute | solution.py:33
  70.1 1.1 %collective-permute-done.8 = f32[4,48,8,1]{1,2,3,0:T(8,128)S(1)} collective-permute-done((f32[4,48,8,1]{1,2,3,0:T(8,128)S(1)}, f32[4,48,8,1]{1,2,3,0:T(8,128)S(1)}, u32[]{:S(2)}, u32[]{:S(2)}) %collective-permute-start.8) | collective-permute-done | bytes 6176 | tf_op jit(solution)/shard_map/ppermute | solution.py:30
  71.1 0.3 copy.119
  71.5 1.0 %copy.117 = f32[4,48,8,1]{3,1,2,0:T(8,128)S(1)} copy(f32[4,48,8,1]{1,2,3,0:T(8,128)} %collective-permute-done.7) | data formatting | bytes 12288 | tf_op jit(solution)/shard_map/ppermute | solution.py:33
  72.6 1.1 %collective-permute-done.9 = f32[4,48,1,128]{3,1,2,0:T(8,128)S(1)} collective-permute-done((f32[4,48,1,128]{3,1,2,0:T(8,128)}, f32[4,48,1,128]{3,1,2,0:T(8,128)S(1)}, u32[]{:S(2)}, u32[]{:S(2)}) %collective-permute-start.9) | collective-permute-done | bytes 98336 | tf_op jit(solution)/shard_map/ppermute | solution.py:33
  73.7 0.4 fusion.56
  74.1 0.7 copy-done.11
  74.8 4.3 %all_gather.7 = f32[2,8,128]{2,1,0:T(8,128)S(1)} all-gather(f32[1,8,128]{2,1,0:T(8,128)S(1)} %bitcast.141), channel_id=1, replica_groups=mesh['lon'=8,'lat'=2,'depth'=2] {'depth'}, dimensions={0}, use_global_device_ids=true | all-gather | bytes 12288 | tf_op jit(solution)/shard_map/all_gather | solution.py:42
  79.2 1.6 %fusion.24 = f32[2,48,8,128]{3,1,2,0:T(8,128)S(1)} fusion(f32[4,48,8,128]{3,1,2,0:T(8,128)S(1)} %get-tuple-element.162, f32[4,48,1,128]{3,1,2,0:T(8,128)S(1)} %collective-permute-done.10, f32[4,48,1,128]{3,1,2,0:T(8,128)S(1)} %collective-permute-done.9, f32[4,48,8,1]{3,1,2,0:T(8,128)S(1)} %copy.119, f32[4,48,8,1]{3,1,2,0:T(8,128)S(1)} %copy.117, ...), kind=kLoop, calls=%fused_computation.42 | loop fusion | flops 1572864 | bytes 4521984 | tf_op jit(solution)/shard_map/add | solution.py:135
  80.9 0.7 copy.123
  81.6 0.7 copy.124
  82.4 0.4 fusion.28
  82.8 0.2 copy-done.27
  83.0 0.1 fusion.62
  83.1 0.7 copy.125
  83.8 0.7 copy.126
  (93 shorter events, 1.3 us)
Async XLA Ops:
  0.6 2.3 %copy-start = (f32[8,48,48]{2,1,0:T(8,128)S(1)}, f32[8,48,48]{2,1,0:T(8,128)}, u32[]{:S(2)}) copy-start(f32[8,48,48]{2,1,0:T(8,128)} %param.23) | copy-start | bytes 221188
  1.8 5.5 %copy-start.21 = (s32[48,8,128]{2,1,0:T(8,128)S(1)}, s32[48,8,128]{2,1,0:T(8,128)}, u32[]{:S(2)}) copy-start(s32[48,8,128]{2,1,0:T(8,128)} %param.22) | copy-start | bytes 589828
  2.9 4.4 %copy-start.19 = (f32[48,8,128]{2,1,0:T(8,128)S(1)}, f32[48,8,128]{2,1,0:T(8,128)}, u32[]{:S(2)}) copy-start(f32[48,8,128]{2,1,0:T(8,128)} %param.19) | copy-start | bytes 589828
  3.0 4.5 %copy-start.20 = (f32[48,8,128]{2,1,0:T(8,128)S(1)}, f32[48,8,128]{2,1,0:T(8,128)}, u32[]{:S(2)}) copy-start(f32[48,8,128]{2,1,0:T(8,128)} %param.20) | copy-start | bytes 589828
  3.8 3.7 %copy-start.28 = (f32[8]{0:T(128)S(1)}, f32[8]{0:T(128)}, u32[]{:S(2)}) copy-start(f32[8]{0:T(128)} %param.24) | copy-start | bytes 100
  3.8 3.8 %copy-start.7 = (s32[2,48,8,128]{3,2,1,0:T(8,128)S(1)}, s32[2,48,8,128]{3,2,1,0:T(8,128)}, u32[]{:S(2)}) copy-start(s32[2,48,8,128]{3,2,1,0:T(8,128)} %param.21) | copy-start | bytes 1179652
  3.9 7.0 %collective-permute-start = (f32[4,8,128]{2,0,1:T(4,128)S(1)}, f32[4,8,128]{2,0,1:T(4,128)S(1)}, u32[]{:S(2)}, u32[]{:S(2)}) collective-permute-start(f32[4,8,128]{2,0,1:T(4,128)S(1)} %bitcast.136), channel_id=1, source_target_pairs={{0,1},{1,0},{2,3},{3,2},{4,5},{5,4},{6,7},{7,6},{8,9},{9,8},{10,11... | collective-permute-start | bytes 49160 | tf_op jit(solution)/shard_map/ppermute | solution.py:20
  7.2 3.6 %collective-permute-start.1 = (f32[8]{0:T(128)S(1)}, f32[8]{0:T(128)S(1)}, u32[]{:S(2)}, u32[]{:S(2)}) collective-permute-start(f32[8]{0:T(128)S(1)} %dynamic-slice_reduce_fusion), channel_id=1, source_target_pairs={{0,1},{1,0},{2,3},{3,2},{4,5},{5,4},{6,7},{7,6},{8,9},{9,8},{10,11... | collective-permute-start | bytes 104 | tf_op jit(solution)/shard_map/ppermute | solution.py:20
  8.1 3.0 %copy-start.29 = (f32[4]{0:T(128)S(1)}, f32[4]{0:T(128)}, u32[]{:S(2)}) copy-start(f32[4]{0:T(128)} %constant.132.clone) | copy-start | bytes 52
  10.8 1.4 %copy-start.22 = (f32[8]{0:T(128)}, f32[8]{0:T(128)S(1)}, u32[]{:S(2)}) copy-start(f32[8]{0:T(128)S(1)} %get-tuple-element.200) | copy-start | bytes 100
  10.8 1.4 %copy-start.24 = (f32[8]{0:T(128)}, f32[8]{0:T(128)S(1)}, u32[]{:S(2)}) copy-start(f32[8]{0:T(128)S(1)} %get-tuple-element.201) | copy-start | bytes 100
  11.1 1.2 %copy-start.3 = (f32[4,48,8,128]{3,1,0,2:T(8,128)}, f32[4,48,8,128]{3,1,0,2:T(8,128)S(1)}, u32[]{:S(2)}) copy-start(f32[4,48,8,128]{3,1,0,2:T(8,128)S(1)} %fusion.17) | copy-start | bytes 2359300
  13.3 22.9 %collective-permute-start.4 = (f32[7,48,1,128]{3,1,2,0:T(8,128)}, f32[7,48,1,128]{3,1,2,0:T(8,128)}, u32[]{:S(2)}, u32[]{:S(2)}) collective-permute-start(f32[7,48,1,128]{3,1,2,0:T(8,128)} %get-tuple-element.167), channel_id=1, source_target_pairs={{0,2},{1,3},{4,6},{5,7},{8,10},{9,11},{12,14},{13,15},{16,18},{17,... | collective-permute-start | bytes 516104 | tf_op jit(solution)/shard_map/ppermute | solution.py:30
  18.5 17.7 %collective-permute-start.5 = (f32[7,48,1,128]{3,1,2,0:T(8,128)}, f32[7,48,1,128]{3,1,2,0:T(8,128)}, u32[]{:S(2)}, u32[]{:S(2)}) collective-permute-start(f32[7,48,1,128]{3,1,2,0:T(8,128)} %get-tuple-element.166), channel_id=1, source_target_pairs={{2,0},{3,1},{6,4},{7,5},{10,8},{11,9},{14,12},{15,13},{18,16},{19,... | collective-permute-start | bytes 516104 | tf_op jit(solution)/shard_map/ppermute | solution.py:33
  23.8 7.6 %collective-permute-start.2 = (f32[7,48,8,1]{1,2,3,0:T(8,128)}, f32[7,48,8,1]{1,2,3,0:T(8,128)}, u32[]{:S(2)}, u32[]{:S(2)}) collective-permute-start(f32[7,48,8,1]{1,2,3,0:T(8,128)} %copy.97), channel_id=1, source_target_pairs={{0,4},{4,8},{8,12},{12,16},{16,20},{20,24},{24,28},{28,0},{1,5},{5... | collective-permute-start | bytes 32264 | tf_op jit(solution)/shard_map/ppermute | solution.py:30
  24.9 7.7 %collective-permute-start.3 = (f32[7,48,8,1]{1,2,3,0:T(8,128)}, f32[7,48,8,1]{1,2,3,0:T(8,128)}, u32[]{:S(2)}, u32[]{:S(2)}) collective-permute-start(f32[7,48,8,1]{1,2,3,0:T(8,128)} %copy.98), channel_id=1, source_target_pairs={{4,0},{8,4},{12,8},{16,12},{20,16},{24,20},{28,24},{0,28},{5,1},{9... | collective-permute-start | bytes 32264 | tf_op jit(solution)/shard_map/ppermute | solution.py:33
  37.0 1.2 %copy-start.8 = (s32[2,48,8,128]{3,2,1,0:T(8,128)S(1)}, s32[2,48,8,128]{3,2,1,0:T(8,128)}, u32[]{:S(2)}) copy-start(s32[2,48,8,128]{3,2,1,0:T(8,128)} %param.21) | copy-start | bytes 1179652
  37.0 1.2 %copy-start.13 = (f32[48,8,128]{2,0,1:T(8,128)S(1)}, f32[48,8,128]{2,0,1:T(8,128)}, u32[]{:S(2)}) copy-start(f32[48,8,128]{2,0,1:T(8,128)} %copy.93) | copy-start | bytes 589828
  37.1 1.2 %copy-start.14 = (f32[48,8,128]{2,0,1:T(8,128)S(1)}, f32[48,8,128]{2,0,1:T(8,128)}, u32[]{:S(2)}) copy-start(f32[48,8,128]{2,0,1:T(8,128)} %copy.103) | copy-start | bytes 589828
  38.3 1.2 %copy-start.5 = (f32[7,48,9,128]{3,1,2,0:T(8,128)}, f32[7,48,9,128]{3,1,2,0:T(8,128)S(1)}, u32[]{:S(2)}) copy-start(f32[7,48,9,128]{3,1,2,0:T(8,128)S(1)} %maximum_maximum_fusion) | copy-start | bytes 4644868
  40.2 2.4 %copy-start.1 = (f32[7,48,8,1]{3,1,2,0:T(8,128)S(1)}, f32[7,48,8,1]{3,1,2,0:T(8,128)}, u32[]{:S(2)}) copy-start(f32[7,48,8,1]{3,1,2,0:T(8,128)} %copy.100) | copy-start | bytes 32260
  43.8 0.7 copy-start.9
  48.8 1.8 %copy-start.4 = (f32[4,48,8,128]{3,1,0,2:T(8,128)S(1)}, f32[4,48,8,128]{3,1,0,2:T(8,128)}, u32[]{:S(2)}) copy-start(f32[4,48,8,128]{3,1,0,2:T(8,128)} %copy-done.3) | copy-start | bytes 2359300
  48.8 1.8 %copy-start.26 = (f32[8]{0:T(128)S(1)}, f32[8]{0:T(128)}, u32[]{:S(2)}) copy-start(f32[8]{0:T(128)} %multiply_add_fusion) | copy-start | bytes 100
  48.8 1.9 %copy-start.2 = (f32[7,48,8,1]{3,1,2,0:T(8,128)S(1)}, f32[7,48,8,1]{3,1,2,0:T(8,128)}, u32[]{:S(2)}) copy-start(f32[7,48,8,1]{3,1,2,0:T(8,128)} %copy.100) | copy-start | bytes 32260
  48.8 1.9 %copy-start.15 = (f32[48,8,128]{2,0,1:T(8,128)S(1)}, f32[48,8,128]{2,0,1:T(8,128)}, u32[]{:S(2)}) copy-start(f32[48,8,128]{2,0,1:T(8,128)} %get-tuple-element.195) | copy-start | bytes 589828
  48.8 1.9 %copy-start.16 = (f32[48,8,128]{2,0,1:T(8,128)S(1)}, f32[48,8,128]{2,0,1:T(8,128)}, u32[]{:S(2)}) copy-start(f32[48,8,128]{2,0,1:T(8,128)} %get-tuple-element.193) | copy-start | bytes 589828
  48.9 1.9 %copy-start.17 = (f32[48,8,128]{2,0,1:T(8,128)S(1)}, f32[48,8,128]{2,0,1:T(8,128)}, u32[]{:S(2)}) copy-start(f32[48,8,128]{2,0,1:T(8,128)} %get-tuple-element.191) | copy-start | bytes 589828
  48.9 2.0 %copy-start.18 = (f32[48,8,128]{2,0,1:T(8,128)S(1)}, f32[48,8,128]{2,0,1:T(8,128)}, u32[]{:S(2)}) copy-start(f32[48,8,128]{2,0,1:T(8,128)} %get-tuple-element.189) | copy-start | bytes 589828
  50.6 1.2 %copy-start.6 = (f32[4,48,8,128]{3,1,2,0:T(8,128)S(1)}, f32[4,48,8,128]{3,1,2,0:T(8,128)}, u32[]{:S(2)}) copy-start(f32[4,48,8,128]{3,1,2,0:T(8,128)} %get-tuple-element.178) | copy-start | bytes 2359300
  51.8 1.4 %copy-start.10 = (f32[48,8,128]{2,0,1:T(8,128)S(1)}, f32[48,8,128]{2,0,1:T(8,128)}, u32[]{:S(2)}) copy-start(f32[48,8,128]{2,0,1:T(8,128)} %copy-done.9) | copy-start | bytes 589828
  53.3 4.8 %copy-start.23 = (f32[8]{0:T(128)S(1)}, f32[8]{0:T(128)}, u32[]{:S(2)}) copy-start(f32[8]{0:T(128)} %copy-done.22) | copy-start | bytes 100
  53.3 4.8 %copy-start.25 = (f32[8]{0:T(128)S(1)}, f32[8]{0:T(128)}, u32[]{:S(2)}) copy-start(f32[8]{0:T(128)} %copy-done.24) | copy-start | bytes 100
  53.3 4.9 %copy-start.30 = (f32[4]{0:T(128)S(1)}, f32[4]{0:T(128)}, u32[]{:S(2)}) copy-start(f32[4]{0:T(128)} %constant.132.clone) | copy-start | bytes 52
  54.2 3.8 %collective-permute-start.6 = (f32[4,8,128]{2,0,1:T(4,128)S(1)}, f32[4,8,128]{2,0,1:T(4,128)S(1)}, u32[]{:S(2)}, u32[]{:S(2)}) collective-permute-start(f32[4,8,128]{2,0,1:T(4,128)S(1)} %bitcast.138), channel_id=1, source_target_pairs={{0,1},{1,0},{2,3},{3,2},{4,5},{5,4},{6,7},{7,6},{8,9},{9,8},{10,11... | collective-permute-start | bytes 49160 | tf_op jit(solution)/shard_map/ppermute | solution.py:20
  59.1 13.5 %collective-permute-start.10 = (f32[4,48,1,128]{3,1,2,0:T(8,128)}, f32[4,48,1,128]{3,1,2,0:T(8,128)S(1)}, u32[]{:S(2)}, u32[]{:S(2)}) collective-permute-start(f32[4,48,1,128]{3,1,2,0:T(8,128)} %get-tuple-element.177), channel_id=1, source_target_pairs={{0,2},{1,3},{4,6},{5,7},{8,10},{9,11},{12,14},{13,15},{16,18},{17,... | collective-permute-start | bytes 294920 | tf_op jit(solution)/shard_map/ppermute | solution.py:30
  65.2 8.5 %collective-permute-start.9 = (f32[4,48,1,128]{3,1,2,0:T(8,128)}, f32[4,48,1,128]{3,1,2,0:T(8,128)S(1)}, u32[]{:S(2)}, u32[]{:S(2)}) collective-permute-start(f32[4,48,1,128]{3,1,2,0:T(8,128)} %get-tuple-element.176), channel_id=1, source_target_pairs={{2,0},{3,1},{6,4},{7,5},{10,8},{11,9},{14,12},{15,13},{18,16},{19,... | collective-permute-start | bytes 294920 | tf_op jit(solution)/shard_map/ppermute | solution.py:33
  67.0 4.1 %collective-permute-start.8 = (f32[4,48,8,1]{1,2,3,0:T(8,128)S(1)}, f32[4,48,8,1]{1,2,3,0:T(8,128)S(1)}, u32[]{:S(2)}, u32[]{:S(2)}) collective-permute-start(f32[4,48,8,1]{1,2,3,0:T(8,128)S(1)} %copy.118), channel_id=1, source_target_pairs={{0,4},{4,8},{8,12},{12,16},{16,20},{20,24},{24,28},{28,0},{1,5},{5... | collective-permute-start | bytes 18440 | tf_op jit(solution)/shard_map/ppermute | solution.py:30
  67.4 4.1 %collective-permute-start.7 = (f32[4,48,8,1]{1,2,3,0:T(8,128)S(1)}, f32[4,48,8,1]{1,2,3,0:T(8,128)}, u32[]{:S(2)}, u32[]{:S(2)}) collective-permute-start(f32[4,48,8,1]{1,2,3,0:T(8,128)S(1)} %copy.116), channel_id=1, source_target_pairs={{4,0},{8,4},{12,8},{16,12},{20,16},{24,20},{28,24},{0,28},{5,1},{9... | collective-permute-start | bytes 18440 | tf_op jit(solution)/shard_map/ppermute | solution.py:33
  74.1 0.7 copy-start.11
  79.2 1.6 %copy-start.12 = (f32[48,8,128]{2,0,1:T(8,128)S(1)}, f32[48,8,128]{2,0,1:T(8,128)}, u32[]{:S(2)}) copy-start(f32[48,8,128]{2,0,1:T(8,128)} %copy-done.11) | copy-start | bytes 589828
  82.4 0.6 copy-start.27
where the time goes:
time: 85.4 us; the launch traced here: 84.6 us
  local copies, waits for them, and re-layouts  27.9 us (33%)
  starting transfers between devices  22.9 us (27%)
  other arithmetic  12.2 us (14%)
  blocking collectives  8.69 us (10%)
  waiting for transfers between devices  8.27 us (10%)
  matrix products  3.3 us (4%)
  between operations  1.32 us (2%)
    ppermute x4, starting transfers between devices, with_halo(): lax.ppermute(lax.slice_in_dim(block, block.shape[dim] - width, None, axis...  11.3 us
    unnamed x68, local copies, waits for them, and re-layouts  9.62 us
    all_gather x2, blocking collectives, entering(): gathered = lax.all_gather(part, axis)  8.69 us
    ppermute x4, starting transfers between devices, with_halo(): lax.ppermute(lax.slice_in_dim(block, 0, width, axis=dim), axis, backward)  7.9 us
    ppermute x3, waiting for transfers between devices, partner(): return lax.ppermute(value, axis, pairs)  6.04 us
    slice x6, local copies, waits for them, and re-layouts, with_halo(): lax.slice_in_dim(block, 0, width, axis=dim)  4.68 us
    ppermute x3, starting transfers between devices, partner(): return lax.ppermute(value, axis, pairs)  3.67 us
    ppermute x2, local copies, waits for them, and re-layouts, with_halo(): lax.ppermute(lax.slice_in_dim(block, 0, width, axis=dim), axis, backward)  3.39 us
  transfers between devices with their start and end apart: 11, of which 4 were waited for; matrix products, arithmetic and copies ran while one was open for 20% of the time, Pallas kernels for 0%

commit v1 on v0

v1 whole, which is shorter than its diff:
```python
import functools

import jax
import jax.numpy as jnp
from jax import lax
from jax.experimental import pallas as pl
from jax.experimental.pallas import tpu as pltpu
from jax.sharding import PartitionSpec as P

STEPS = 2

advect_scale = 0.25
diffusion = 0.5
gravity = 0.1
pressure_scale = 1.0
viscosity = 0.1
haline = 0.8

BLOCK = 8
f32 = jnp.float32
bf16 = jnp.bfloat16
CORNER_LANE = 16


def split(value):
    high = value.astype(bf16)
    return high, (value - high.astype(f32)).astype(bf16)


def dot(a, b, contract=((1,), (0,))):
    return lax.dot_general(a, b, (contract, ((), ())), preferred_element_type=f32)


def dot3(a, b):
    return dot(a[0], b[0]) + (dot(a[0], b[1]) + dot(a[1], b[0]))


def iota(shape, dim):
    return lax.broadcasted_iota(jnp.int32, shape, dim)


def branches(flags):
    one = jnp.where(flags >= 3, 1, 0) + jnp.where(flags >= 6, 1, 0)
    zonal = (flags - 3 * one).astype(f32) * 0.5
    return zonal, one.astype(f32) * 0.5


def lane_of(value, lane):
    return jnp.broadcast_to(value[:, lane : lane + 1], value.shape)


def level(ref, k, rows):
    return ref[pl.ds(pl.multiple_of(k * rows, rows), rows), :]


def take_row(ref, row, levels, rows):
    if isinstance(row, int):
        return ref[pl.ds(row, levels, stride=rows), :]
    low = ref[pl.ds(0, levels, stride=rows), :]
    high = ref[pl.ds(rows - 1, levels, stride=rows), :]
    return jnp.where(row == 0, low, high)


def row_choices(pair, rows, lat):
    return [jnp.where(lat == 0, rows - 1, 0)] if pair else [0, rows - 1]


def pack_kernel(dims, ids, t, s, u, v, sea, east, north, flags, inverse, to_east, to_west, nn_late, *lat_msgs):
    levels, rows, cols, half, pair = dims
    lane = iota((rows, cols), 1)
    fields = (t, s, u, v)

    def some(b, carry):
        accs = list(carry)
        for i in range(BLOCK):
            k = b * BLOCK + i
            here = [level(x, k, rows) for x in fields]
            wet = level(sea, k, rows).astype(f32)
            speed = level(east, k, rows)
            nexts = []
            for step in (1, 0):
                zonal, _ = branches(level(flags.at[step], k, rows))
                nexts.append(wet * (speed * zonal - diffusion))
            low, high = lane == k, lane == k + half
            last = here + [wet] + nexts
            for j, value in enumerate(last):
                place = k + (j % 2) * half
                accs[j // 2] = jnp.where(
                    high if j % 2 else low, pltpu.roll(value, (place + 1) % cols, 1), accs[j // 2]
                )
            for j, value in enumerate(here + [wet]):
                place = k + (j % 2) * half
                accs[4 + j // 2] = jnp.where(
                    high if j % 2 else low, pltpu.roll(value, place % cols, 1), accs[4 + j // 2]
                )
        return tuple(accs)

    zero = jnp.zeros((rows, cols), f32)
    accs = lax.fori_loop(0, levels // BLOCK, some, (zero,) * 7)
    for j in range(4):
        to_east[j] = accs[j]
    for j in range(3):
        to_west[j] = accs[4 + j]
    for which, row in enumerate(row_choices(pair, rows, ids[0])):
        msg = lat_msgs[which]
        for j, x in enumerate(fields):
            msg[j] = take_row(x, row, levels, rows)
        wet = take_row(sea, row, levels, rows).astype(f32)
        speed = take_row(north, row, levels, rows)
        msg[4] = wet
        for step in (1, 0):
            _, merid = branches(take_row(flags.at[step], row, levels, rows))
            value = wet * (speed * merid - diffusion)
            if step:
                msg[5] = value
            elif pair or row:
                nn_late[...] = value
        msg[6] = jnp.zeros((levels, cols), f32)
        if pair:
            block = jnp.where(row == 0, inverse[0], inverse[rows - 1])
        else:
            block = inverse[row]
        msg[6, :, pl.ds(0, levels)] = block


def project_kernel(dims, setup, ids, t, s, u, v, sea, *rest):
    levels, rows, cols, half, pair = dims
    if setup:
        inverse, coup, proj, planes, *rest = rest
        lat_out, (spike, w_high, w_low, p_high, p_low, spike_packed, cells, wide) = rest[:-8], rest[-8:]
        n = levels * rows
        for y in range(rows):
            cells[pl.ds(y, levels, stride=rows), :] = inverse[y]
        pieces = split(cells[...])
        pick = (iota((n, levels), 0) // rows == iota((n, levels), 1)).astype(bf16)
        same = (iota((n, n), 0) % rows) == (iota((n, n), 1) % rows)
        for piece, out in zip(pieces, (w_high, w_low)):
            full = dot(pick, piece, ((1,), (1,)))
            out[...] = jnp.where(same, full, 0.0).astype(bf16)
        wide[...] = jnp.zeros_like(wide)
        for y in range(rows):
            wide[y, pl.ds(0, levels), pl.ds(0, levels)] = inverse[y]
            wide[y, pl.ds(half, levels), pl.ds(half, levels)] = inverse[y]
        high, low = split(wide[...].reshape(rows * cols, cols))
        p_high[...] = high
        p_low[...] = low
        spike_packed[...] = jnp.zeros_like(spike_packed)
        for y in range(rows):
            line = inverse[y, pl.ds(ids[2], 1), :]
            spike_packed[pl.ds(y, 1), pl.ds(0, levels)] = line
            spike_packed[pl.ds(y, 1), pl.ds(half, levels)] = line
    else:
        coup, spike, w_high, w_low, proj, planes, *lat_out = rest
    w = (w_high[...], w_low[...])
    for f, x in enumerate((t, s, u, v)):
        proj[f] = dot3(w, split(x[...]))
    if setup:
        n = levels * rows
        pick = (iota((n, cols), 0) // rows == ids[2]).astype(bf16)
        spike[...] = dot(w[0], pick) + dot(w[1], pick)
    edge = pl.ds(pl.multiple_of(ids[2] * rows, rows), rows)
    for f in range(4):
        planes[f] = proj[f, edge, :]
    sums = [jnp.zeros((rows, cols), f32)] * 3
    for k in range(levels):
        here = pl.ds(k * rows, rows)
        wet = sea[here, :].astype(f32)
        sums = [
            sums[0] + wet * proj[2, here, :],
            sums[1] + wet * proj[3, here, :],
            sums[2] + wet * spike[here, :],
        ]
    for j in range(3):
        planes[4 + j] = sums[j]
    corner = spike[edge, :]
    lane_row = iota((rows, cols), 0)
    coupled = jnp.zeros((rows, cols), f32)
    for y in range(rows):
        coupled = jnp.where(lane_row == y, coup[y], coupled)
    lines = [proj[f, edge, :] for f in range(4)] + [sums[1], sums[2], corner, coupled]
    for which, row in enumerate(row_choices(pair, rows, ids[0])):
        for j, value in enumerate(lines):
            if pair:
                line = jnp.where(row == 0, value[0:1], value[rows - 1 : rows])
            else:
                line = value[row : row + 1]
            lat_out[which][pl.ds(j, 1), :] = line


def side_kernel(dims, ids, west, east, west_sea, east_sea, planes, spike, spike_packed, p_high, p_low, msg, proj):
    levels, rows, cols, half, pair = dims
    lane = iota((rows, cols), 1)
    row = iota((rows, cols), 0)
    packed = (west[0], west[1], east[0], east[1])
    chunks = []
    for y in range(rows):
        chunks.append(jnp.concatenate([jnp.where(row == y, x, 0.0) for x in packed], axis=0))
    lhs = jnp.concatenate(chunks, axis=1)
    out = dot3(split(lhs), (p_high[...], p_low[...]))
    for j in range(4):
        proj[j] = out[j * rows : (j + 1) * rows]
    for j in range(7):
        msg[j] = planes[j]
    edge = ids[2]
    misc = jnp.zeros((rows, cols), f32)
    spk = spike_packed[...]
    for side, wet in enumerate((west_sea, east_sea)):
        wet = jnp.where(lane < half, wet[2], 0.0)
        for p in range(2):
            value = out[(2 * side + p) * rows : (2 * side + p + 1) * rows]
            for i in range(2):
                column = jnp.sum(jnp.where(lane == edge + i * half, value, 0.0), axis=1, keepdims=True)
                misc = jnp.where(lane == side * 8 + 2 * p + i, column, misc)
            if p == 1:
                column = jnp.sum(wet * value, axis=1, keepdims=True)
                misc = jnp.where(lane == side * 8 + 4, column, misc)
        column = jnp.sum(wet * spk, axis=1, keepdims=True)
        misc = jnp.where(lane == side * 8 + 5, column, misc)
    corner = level(spike, edge, rows)
    msg[7] = jnp.where(lane == CORNER_LANE, corner, misc)


def stencil_kernel(dims, step, final, ids, coup, proj, spike, spike_packed, mine, theirs, side_proj,
                   west_const, east_const, sea, east, north, flags, *rest):
    levels, rows, cols, half, pair = dims
    count = 1 if pair else 2
    row_new, row_const, row_late, row_far = (rest[i * count : (i + 1) * count] for i in range(4))
    rest = rest[4 * count :]
    if final:
        outs, rest = rest[:4], rest[4:]
    else:
        late_out, rest = rest[0], rest[1:]
        outs, (to_east, to_west), rest = rest[:4], rest[4:6], rest[6:]
        lat_msgs, rest = rest[:count], rest[count:]
    north_w, south_w, north_sea, south_next, line, sides = rest
    lat, depth, edge, parts = ids[0], ids[1], ids[2], ids[3]
    lane = iota((rows, cols), 1)
    row = iota((rows, cols), 0)
    has_north = jnp.where(lat < parts - 1, 1.0, 0.0)
    has_south = jnp.where(lat > 0, 1.0, 0.0)

    row_sums = []
    for h in range(count):
        block = split(row_const[h][6][:, :levels])
        eye = (iota((levels, levels), 0) == iota((levels, levels), 1)).astype(bf16)
        turned = tuple(dot(eye, piece, ((1,), (1,))).astype(bf16) for piece in block)
        pick = (iota((levels, cols), 0) == edge).astype(bf16)
        thin = dot(turned[0], pick) + dot(turned[1], pick)
        line[4] = thin
        for f in range(4):
            line[f] = dot3(turned, split(row_new[h][f]))
        at_edge = pl.ds(edge, 1)
        far = row_far[h]
        c = far[7:8, :]
        other_corner = far[6:7, :]
        own_corner = line[4, at_edge, :]
        scaled = c / (1.0 - c * c * own_corner * other_corner)
        wet = row_const[h][4]
        if pair:
            masks = ((north_w, has_north), (south_w, has_south))
        else:
            masks = ((north_w, has_north),) if h == 0 else ((south_w, has_south),)
        for f in range(4):
            carried = scaled * (far[f : f + 1, :] + c * other_corner * line[f, at_edge, :])
            value = wet * (line[f] + thin * carried)
            for target, mask in masks:
                target[f] = value * mask
        if pair or h == 0:
            north_sea[...] = wet * has_north
        if pair or h == 1:
            late = row_const[h][5] if step else row_late[h][4]
            south_next[...] = late * has_south
        theirs_v = scaled * (line[3, at_edge, :] + c * own_corner * far[3:4, :])
        row_sums.append(far[4:5, :] + far[5:6, :] * theirs_v)
    row_sum_north, row_sum_south = row_sums[0], row_sums[-1]

    c = jnp.zeros((rows, cols), f32)
    for y in range(rows):
        c = jnp.where(row == y, coup[y], c)
    own_corner = lane_of(mine[7], CORNER_LANE)
    other_corner = lane_of(theirs[7], CORNER_LANE)
    scaled = c / (1.0 - c * c * own_corner * other_corner)
    co, cm = c * other_corner, c * own_corner
    carried = [scaled * (theirs[f] + co * mine[f]) for f in range(4)]
    misc = theirs[7]
    carried_side = scaled * (misc + co * mine[7])
    theirs_side = scaled * (mine[7] + cm * misc)

    spk = spike_packed[...]
    for side, const in enumerate((west_const, east_const)):
        wet = jnp.where(lane < half, const[2], pltpu.roll(const[2], half, 1))
        for p in range(2):
            joined = jnp.where(
                lane < half,
                lane_of(carried_side, side * 8 + 2 * p),
                lane_of(carried_side, side * 8 + 2 * p + 1),
            )
            sides[2 * side + p] = wet * (side_proj[2 * side + p] + spk * joined)

    sum_u = theirs[4] + theirs[6] * (scaled * (mine[2] + cm * theirs[2]))
    sum_v = theirs[5] + theirs[6] * (scaled * (mine[3] + cm * theirs[3]))
    side_u = [lane_of(misc, q * 8 + 4) + lane_of(misc, q * 8 + 5) * lane_of(theirs_side, q * 8 + 2) for q in (0, 1)]

    def shifted(value, west_in, east_in, south_in, north_in):
        return (
            jnp.where(lane == 0, west_in, pltpu.roll(value, 1, 1)),
            jnp.where(lane == cols - 1, east_in, pltpu.roll(value, cols - 1, 1)),
            jnp.where(row == 0, south_in, pltpu.roll(value, 1, 0)),
            jnp.where(row == rows - 1, north_in, pltpu.roll(value, rows - 1, 0)),
        )

    west_u = jnp.where(lane == 0, side_u[0], pltpu.roll(sum_u, 1, 1))
    east_u = jnp.where(lane == cols - 1, side_u[1], pltpu.roll(sum_u, cols - 1, 1))
    south_v = jnp.where(row == 0, row_sum_south * has_south, pltpu.roll(sum_v, 1, 0))
    north_v = jnp.where(row == rows - 1, row_sum_north * has_north, pltpu.roll(sum_v, rows - 1, 0))
    upper = jnp.where(depth == 0, 1.0, 0.0)
    deeper = (-0.5 * pressure_scale) * (west_u - east_u + south_v - north_v) * upper

    north_index = (lat * rows + row).astype(f32)
    coriolis = 0.2 + 0.6 * (north_index + 0.5) / (rows * parts).astype(f32)

    west_sides = (sides[0], sides[1])
    east_sides = (sides[2], sides[3])
    sea_east_side = east_const[2]
    next_west_side = west_const[2] if step else west_const[3]
    next_shift = half if step else 0

    def some(b, carry):
        below, *accs = carry
        for i in range(BLOCK):
            k = levels - 1 - (b * BLOCK + i)
            wet = level(sea, k, rows).astype(f32)
            speed_e, speed_n = level(east, k, rows), level(north, k, rows)
            zonal_b, merid_b = branches(level(flags.at[step], k, rows))
            east_self = wet * (speed_e * (1.0 - zonal_b) + diffusion)
            east_next = wet * (speed_e * zonal_b - diffusion)
            north_self = wet * (speed_n * (1.0 - merid_b) + diffusion)
            north_next = wet * (speed_n * merid_b - diffusion)
            one = pl.ds(k, 1)
            sea_east = jnp.where(
                lane == cols - 1, pltpu.roll(sea_east_side, cols - 1 - k, 1), pltpu.roll(wet, cols - 1, 1)
            )
            next_west = jnp.where(
                lane == 0, pltpu.roll(next_west_side, (cols - next_shift) - k, 1), pltpu.roll(east_next, 1, 1)
            )
            sea_north = jnp.where(row == rows - 1, north_sea[one, :], pltpu.roll(wet, rows - 1, 0))
            next_south = jnp.where(row == 0, south_next[one, :], pltpu.roll(north_next, 1, 0))
            east_own = advect_scale * east_self * sea_east
            west_own = advect_scale * next_west * wet
            north_own = advect_scale * north_self * sea_north
            south_own = advect_scale * next_south * wet
            spk_k = level(spike, k, rows)
            solved, around = [], []
            for f in range(4):
                w = wet * (level(proj.at[f], k, rows) + spk_k * carried[f])
                shift = (f % 2) * half
                solved.append(w)
                around.append(
                    shifted(
                        w,
                        pltpu.roll(west_sides[f // 2], (cols - shift) - k, 1),
                        pltpu.roll(east_sides[f // 2], (cols - 1 - shift) - k, 1),
                        south_w[f, one, :],
                        north_w[f, one, :],
                    )
                )
            pressure = (-0.5 * pressure_scale) * (
                around[2][0] - around[2][1] + around[3][2] - around[3][3]
            )
            below = below + pressure
            buoyancy = gravity * below
            new = []
            for f in range(2):
                w, (ww, we, ws, wn) = solved[f], around[f]
                q = w + (
                    (east_own * (we - w) + west_own * (w - ww)) + (north_own * (wn - w) + south_own * (w - ws))
                )
                new.append(q + buoyancy if f == 0 else q - haline * buoyancy)
            for f in (2, 3):
                w, (ww, we, ws, wn) = solved[f], around[f]
                turn = -solved[3] if f == 2 else solved[2]
                new.append(w + coriolis * turn + viscosity * ((we + ww) + (wn + ws) - 4.0 * w))
            here = pl.ds(pl.multiple_of(k * rows, rows), rows)
            for f in range(4):
                outs[f][here, :] = new[f]
            if not final:
                for f in range(4):
                    place = k + (f % 2) * half
                    there = lane == place
                    accs[f // 2] = jnp.where(there, pltpu.roll(new[f], (place + 1) % cols, 1), accs[f // 2])
                    accs[2 + f // 2] = jnp.where(there, pltpu.roll(new[f], place % cols, 1), accs[2 + f // 2])
        return (below, *accs)

    zero = jnp.zeros((rows, cols), f32)
    extra = () if final else (zero,) * 4
    _, *accs = lax.fori_loop(0, levels // BLOCK, some, (deeper, *extra))
    if not final:
        for p in range(2):
            to_east[p] = accs[p]
            to_west[p] = accs[2 + p]
        for which, at in enumerate(row_choices(pair, rows, lat)):
            for f in range(4):
                lat_msgs[which][f] = take_row(outs[f], at, levels, rows)
            lat_msgs[which][4] = late_out[...]


def call(kernel, outs, args, smem=(0,), scratch=(), name=None):
    specs = [
        pl.BlockSpec(memory_space=pltpu.SMEM if i in smem else pltpu.VMEM) for i in range(len(args))
    ]
    return pl.pallas_call(
        kernel,
        out_shape=[jax.ShapeDtypeStruct(shape, kind) for shape, kind in outs],
        in_specs=specs,
        out_specs=[pl.BlockSpec(memory_space=pltpu.VMEM)] * len(outs),
        scratch_shapes=list(scratch),
        name=name,
    )(*args)


def on_device(
    adj_temp,
    adj_salt,
    adj_zonal,
    adj_merid,
    east_speed,
    north_speed,
    branch_flags,
    sea_mask,
    block_inverse,
    coupling,
):
    levels, rows, cols = adj_temp.shape
    half = cols // 2
    lons, lats, depths = (lax.axis_size(a) for a in ("lon", "lat", "depth"))
    pair = lats == 2
    dims = (levels, rows, cols, half, pair)
    count = 1 if pair else 2
    n = levels * rows
    lat, depth = lax.axis_index("lat"), lax.axis_index("depth")
    ids = jnp.stack([lat, depth, (levels - 1) * (1 - depth), jnp.int32(lats)]).astype(jnp.int32)
    flat = lambda x: x.reshape(x.shape[:-3] + (n, cols))
    sea, east, north, flags = flat(sea_mask), flat(east_speed), flat(north_speed), flat(branch_flags)
    state = [flat(x) for x in (adj_temp, adj_salt, adj_zonal, adj_merid)]
    plane = (rows, cols)
    grid = (levels, cols)

    ring = [(i, (i + 1) % lons) for i in range(lons)]
    back = [(b, a) for a, b in ring]
    up = [(i, i + 1) for i in range(lats - 1)]
    down = [(b, a) for a, b in up]

    def to_lat(msgs, flip):
        routes = [up + down] if pair else [down, up]
        if not flip:
            return [lax.ppermute(m, "lat", r) for m, r in zip(msgs, routes)]
        both = [
            [(a * depths + d, b * depths + (depths - 1 - d)) for a, b in r for d in range(depths)] for r in routes
        ]
        return [lax.ppermute(m, ("lat", "depth"), r) for m, r in zip(msgs, both)]

    def to_depth(msg):
        return lax.ppermute(msg, "depth", [(d, depths - 1 - d) for d in range(depths)])

    to_east, to_west, late, *lat_msgs = call(
        functools.partial(pack_kernel, dims),
        [((4,) + plane, f32), ((3,) + plane, f32), (grid, f32)] + [((7,) + grid, f32)] * count,
        (ids, *state, sea, east, north, flags, block_inverse),
        name="pack",
    )
    row_const = to_lat(lat_msgs, False)
    west_const = lax.ppermute(to_east, "lon", ring)
    east_const = lax.ppermute(to_west, "lon", back)
    row_new, west, east_in = row_const, west_const, east_const

    for step in reversed(range(STEPS)):
        first = step == STEPS - 1
        outs = [((4, n, cols), f32), ((7,) + plane, f32)] + [(plane, f32)] * count
        if first:
            outs += [((n, cols), f32)] + [((n, n), bf16)] * 2 + [((rows * cols, cols), bf16)] * 2 + [(plane, f32)]
            args = (ids, *state, sea, block_inverse, coupling)
            smem = (0, 7)
            scratch = (pltpu.VMEM((n, levels), f32), pltpu.VMEM((rows, cols, cols), f32))
        else:
            args = (ids, *state, sea, coupling, spike, w_high, w_low)
            smem = (0, 6)
            scratch = ()
        proj, planes, *more = call(
            functools.partial(project_kernel, dims, first), outs, args, smem, scratch, name="project"
        )
        far_msgs = more[:count]
        if first:
            spike, w_high, w_low, p_high, p_low, spike_packed = more[count:]
        row_far = to_lat(far_msgs, True)
        mine, side_proj = call(
            functools.partial(side_kernel, dims),
            [((8,) + plane, f32), ((4,) + plane, f32)],
            (ids, west, east_in, west_const, east_const, planes, spike, spike_packed, p_high, p_low),
            name="sides",
        )
        theirs = to_depth(mine)
        final = step == 0
        state_shape = [((n, cols), f32)] * 4
        if final:
            outs, extra = state_shape, ()
        else:
            outs = state_shape + [((2,) + plane, f32)] * 2 + [((5,) + grid, f32)] * count
            extra = (late,)
        result = call(
            functools.partial(stencil_kernel, dims, step, final),
            outs,
            (
                ids, coupling, proj, spike, spike_packed, mine, theirs, side_proj, west_const, east_const,
                sea, east, north, flags, *row_new, *row_const, *row_new, *row_far, *extra,
            ),
            (0, 1),
            (
                pltpu.VMEM((4,) + grid, f32),
                pltpu.VMEM((4,) + grid, f32),
                pltpu.VMEM(grid, f32),
                pltpu.VMEM(grid, f32),
                pltpu.VMEM((5,) + grid, f32),
                pltpu.VMEM((4,) + plane, f32),
            ),
            name="stencil",
        )
        state = result[:4]
        if not final:
            row_new = to_lat(result[6:], False)
            west = lax.ppermute(result[4], "lon", ring)
            east_in = lax.ppermute(result[5], "lon", back)
    return tuple(x.reshape(levels, rows, cols) for x in state)


def solution(mesh):
    in_specs = (
        P("depth", "lat", "lon"),
        P("depth", "lat", "lon"),
        P("depth", "lat", "lon"),
        P("depth", "lat", "lon"),
        P("depth", "lat", "lon"),
        P("depth", "lat", "lon"),
        P(None, "depth", "lat", "lon"),
        P("depth", "lat", "lon"),
        P("lat", "depth", None),
        P("lat"),
    )
    out_specs = (
        P("depth", "lat", "lon"),
        P("depth", "lat", "lon"),
        P("depth", "lat", "lon"),
        P("depth", "lat", "lon"),
    )
    return jax.shard_map(
        on_device, mesh=mesh, in_specs=in_specs, out_specs=out_specs, check_vma=False
    )
```

time: 85.4 us -> 53.2 us (0.62)
  Pallas kernels: 0 us -> 26 us
  local copies, waits for them, and re-layouts: 27.9 us -> 2.49 us
  other arithmetic: 12.2 us -> 0.66 us
  blocking collectives: 8.69 us -> 0 us
  starting transfers between devices: 22.9 us -> 15.4 us
  matrix products: 3.3 us -> 0 us
    pallas_call x0 -> x7, Pallas kernels: none -> 26 us  [call(): pl.pallas_call(kernel, out_shape=[jax.ShapeDtypeStruct(shape, kind) for s...]
    all_gather x2 -> x0, blocking collectives: 8.69 us -> none  [entering(): gathered = lax.all_gather(part, axis)]
    slice x12 -> x0, local copies, waits for them, and re-layouts: 7.54 us -> none  [the longest x6 4.68 us: with_halo(): lax.slice_in_dim(block, 0, width, axis=dim)]
    ppermute x11 -> x10, starting transfers between devices: 22.9 us -> 15.4 us  [the longest x2 4.12 us: to_lat(): return [lax.ppermute(m, 'lat', r) for m, r in zip(msgs, routes)]]
    unnamed x68 -> x24, local copies, waits for them, and re-layouts: 9.62 us -> 2.49 us
    ppermute x4 -> x0, local copies, waits for them, and re-layouts: 4.97 us -> none  [the longest x2 3.39 us: with_halo(): lax.ppermute(lax.slice_in_dim(block, 0, width, axis=dim), axis, backward)]
    add x7 -> x0, other arithmetic: 3.84 us -> none  [the longest x2 3.05 us: on_device(): tracers = weighted[:2] + east_part + north_part]
    dot_general x4 -> x0, matrix products: 3.3 us -> none  [the longest x2 1.66 us: project(): jnp.einsum('yjk,fjyx->fkyx', inverse, stack, precision=lax.Precision.HIGH...]
  transfers between devices with their start and end apart: 11 -> 10, of which waited for: 4 -> 2; matrix products, arithmetic and copies ran while one was open for 20% -> 0% of each run, Pallas kernels for 0% -> 22%
where the time goes in v1:
time: 53.2 us; the launch traced here: 52.9 us
  Pallas kernels  26 us (49%)
  starting transfers between devices  15.4 us (29%)
  waiting for transfers between devices  7.56 us (14%)
  local copies, waits for them, and re-layouts  2.49 us (5%)
  between operations  0.74 us (1%)
  other arithmetic  0.66 us (1%)
    pallas_call x7, Pallas kernels, call(): pl.pallas_call(kernel, out_shape=[jax.ShapeDtypeStruct(shape, kind) for s...  26 us
    ppermute x2, waiting for transfers between devices, to_lat(): return [lax.ppermute(m, ('lat', 'depth'), r) for m, r in zip(msgs, both)]  7.54 us
    ppermute x2, starting transfers between devices, to_lat(): return [lax.ppermute(m, 'lat', r) for m, r in zip(msgs, routes)]  4.12 us
    ppermute x2, starting transfers between devices, to_lat(): return [lax.ppermute(m, ('lat', 'depth'), r) for m, r in zip(msgs, both)]  3.27 us
    ppermute x1, starting transfers between devices, on_device(): east_const = lax.ppermute(to_west, 'lon', back)  2.64 us
    ppermute x1, starting transfers between devices, on_device(): east_in = lax.ppermute(result[5], 'lon', back)  2.63 us
    ppermute x2, starting transfers between devices, to_depth(): lax.ppermute(msg, 'depth', [(d, depths - 1 - d) for d in range(depths)])  2.63 us
    unnamed x24, local copies, waits for them, and re-layouts  2.49 us
  transfers between devices with their start and end apart: 10, of which 2 were waited for; matrix products, arithmetic and copies ran while one was open for 0% of the time, Pallas kernels for 22%

profile of v1, /device:TPU:0, one launch (start us, length us, event | category | flops | bytes accessed | tf_op | source)
XLA Modules:
  0.0 52.9 jit_solution(5411215556614187771)
XLA Ops:
  0.6 0.7 %pad_add_fusion.ids = s32[4]{0:T(128)} fusion(s32[1]{0:T(128)} %constant.11.clone.1, s32[1]{0:T(128)} %bitcast.2, s32[1]{0:T(128)} %bitcast.1, s32[1]{0:T(128)} %bitcast), kind=kLoop, calls=%fused_computation | loop fusion | flops 12 | bytes 32 | tf_op jit(solution)/shard_map/stack | solution.py:441
  1.3 3.4 %pack.1 = (f32[4,8,128]{2,1,0:T(8,128)}, f32[3,8,128]{2,1,0:T(8,128)}, f32[48,128]{1,0:T(8,128)}, f32[7,48,128]{2,1,0:T(8,128)}) custom-call(s32[4]{0:T(128)} %pad_add_fusion.ids, f32[384,128]{1,0:T(8,128)} %bitcast.29, f32[384,128]{1,0:T(8,128)} %bitcast.31, f32[384,128]{1,0:T(8,128)} %bitcast.33, f32[384,128]{1,0:T(8,128)} %bitcast.35, ...), custom_call_target="tpu_custom_call" | custom-call | tf_op jit(solution)/shard_map/pack/pallas_call | solution.py:411
  4.7 4.1 %collective-permute-start.3 = (f32[7,48,128]{2,1,0:T(8,128)}, f32[7,48,128]{2,1,0:T(8,128)S(1)}, u32[]{:S(2)}, u32[]{:S(2)}) collective-permute-start(f32[7,48,128]{2,1,0:T(8,128)} %get-tuple-element.45), channel_id=1, source_target_pairs={{0,2},{2,0},{1,3},{3,1},{4,6},{6,4},{5,7},{7,5},{8,10},{10,8},{9,1... | collective-permute-start | bytes 516104 | tf_op jit(solution)/shard_map/ppermute | solution.py:456
  8.7 0.0 collective-permute-start
  8.7 2.6 %collective-permute-start.1 = (f32[3,8,128]{2,1,0:T(8,128)}, f32[3,8,128]{2,1,0:T(8,128)S(1)}, u32[]{:S(2)}, u32[]{:S(2)}) collective-permute-start(f32[3,8,128]{2,1,0:T(8,128)} %get-tuple-element.39), channel_id=1, source_target_pairs={{4,0},{8,4},{12,8},{16,12},{20,16},{24,20},{28,24},{0,28},{5,1},{9... | collective-permute-start | bytes 36872 | tf_op jit(solution)/shard_map/ppermute | solution.py:473
  11.4 4.0 %project.2 = (f32[4,384,128]{2,1,0:T(8,128)}, f32[7,8,128]{2,1,0:T(8,128)}, f32[8,128]{1,0:T(8,128)}, f32[384,128]{1,0:T(8,128)}, bf16[384,384]{1,0:T(8,128)(2,1...) custom-call(s32[4]{0:T(128)} %pad_add_fusion.ids, ...), custom_call_target="tpu_custom_call" | custom-call | tf_op jit(solution)/shard_map/project/pallas_call | solution.py:411
  15.4 0.0 collective-permute-done.1.east.east_sea.east_const
  15.4 0.0 copy-start.3
  15.4 0.0 collective-permute-done.west.west_sea.west_const
  15.4 0.0 copy-start.2
  15.4 0.6 %copy-done.3 = f32[3,8,128]{2,1,0:T(8,128)} copy-done((f32[3,8,128]{2,1,0:T(8,128)}, f32[3,8,128]{2,1,0:T(8,128)S(1)}, u32[]{:S(2)}) %copy-start.3) | copy-done | bytes 12312
  16.0 0.0 copy-done.2
  16.0 0.0 copy-start.11
  16.0 2.1 %sides.2 = (f32[8,8,128]{2,1,0:T(8,128)}, f32[4,8,128]{2,1,0:T(8,128)}) custom-call(s32[4]{0:T(128)} %pad_add_fusion.ids, f32[4,8,128]{2,1,0:T(8,128)} %copy-done.2, f32[3,8,128]{2,1,0:T(8,128)} %copy-done.3, f32[4,8,128]{2,1,0:T(8,128)} %copy-done.2, f32[3,8,128]{2,1,0:T(8,128)} %copy-done.3, f32[7,8,128]{2,1,0:T(8,128)} %get-tuple-element.40.planes, ...), custom_call_target="tpu_custom_call" | custom-call | tf_op jit(solution)/shard_map/sides/pallas_call | solution.py:411
  18.2 1.6 %collective-permute-start.2 = (f32[8,8,128]{2,1,0:T(8,128)}, f32[8,8,128]{2,1,0:T(8,128)S(1)}, u32[]{:S(2)}, u32[]{:S(2)}) collective-permute-start(f32[8,8,128]{2,1,0:T(8,128)} %get-tuple-element.43.mine), channel_id=1, source_target_pairs={{0,1},{1,0},{2,3},{3,2},{4,5},{5,4},{6,7},{7,6},{8,9},{9,8},{10,11... | collective-permute-start | bytes 98312 | tf_op jit(solution)/shard_map/ppermute | solution.py:463
  19.7 0.0 copy-done.11
  19.7 0.0 collective-permute-start.4
  19.7 5.4 %collective-permute-done.4.rest_3_ = f32[8,128]{1,0:T(8,128)S(1)} collective-permute-done((f32[8,128]{1,0:T(8,128)S(1)}, f32[8,128]{1,0:T(8,128)S(1)}, u32[]{:S(2)}, u32[]{:S(2)}) %collective-permute-start.4) | collective-permute-done | bytes 4128 | tf_op jit(solution)/shard_map/ppermute | solution.py:460
  25.1 0.0 copy-start.9
  25.1 0.0 collective-permute-done.2.theirs
  25.1 0.0 copy-start.5
  25.2 0.0 collective-permute-done.3.rest_0_.rest_1_.rest_2_
  25.2 0.0 copy-start
  25.2 0.6 %copy-done.9 = f32[8,128]{1,0:T(8,128)} copy-done((f32[8,128]{1,0:T(8,128)}, f32[8,128]{1,0:T(8,128)S(1)}, u32[]{:S(2)}) %copy-start.9) | copy-done | bytes 4120
  25.7 0.0 copy-done.5
  25.8 0.1 copy-done
  25.8 6.4 %stencil.2 = (f32[384,128]{1,0:T(8,128)}, f32[384,128]{1,0:T(8,128)}, f32[384,128]{1,0:T(8,128)}, f32[384,128]{1,0:T(8,128)}, f32[2,8,128]{2,1,0:T(8,128)}, /*index=5*/f32[2,8,128]{2,1,0:T(8,128)}, f32[5,48,128]{2,1,0:T(8,128)}) custom-call(s32[4]{0:T(128)} %pad_add_fusion.ids, f32[8]{0:T(128)} %coup.3, f32[4,384,128]{2,1,0:T(8,128)} %get-tuple-element.35.proj, ...), custom_call_target="tpu_custom_call" | custom-call | tf_op jit(solution)/shard_map/stencil/pallas_call | solution.py:411
  32.2 0.1 collective-permute-start.8
  32.2 0.1 collective-permute-start.5
  32.3 2.6 %collective-permute-start.6 = (f32[2,8,128]{2,1,0:T(8,128)}, f32[2,8,128]{2,1,0:T(8,128)S(1)}, u32[]{:S(2)}, u32[]{:S(2)}) collective-permute-start(f32[2,8,128]{2,1,0:T(8,128)} %get-tuple-element.56), channel_id=1, source_target_pairs={{4,0},{8,4},{12,8},{16,12},{20,16},{24,20},{28,24},{0,28},{5,1},{9... | collective-permute-start | bytes 24584 | tf_op jit(solution)/shard_map/ppermute | solution.py:531
  34.9 3.5 %project.3 = (f32[4,384,128]{2,1,0:T(8,128)}, f32[7,8,128]{2,1,0:T(8,128)}, f32[8,128]{1,0:T(8,128)}) custom-call(s32[4]{0:T(128)} %pad_add_fusion.ids, f32[384,128]{1,0:T(8,128)} %get-tuple-element.48.t, f32[384,128]{1,0:T(8,128)} %get-tuple-element.49.s, f32[384,128]{1,0:T(8,128)} %get-tuple-element.50.u, f32[384,128]{1,0:T(8,128)} %get-tuple-element.51.v, ...), custom_call_target="tpu_custom_call" | custom-call | tf_op jit(solution)/shard_map/project/pallas_call | solution.py:411
  38.5 0.0 collective-permute-done.5.west
  38.5 0.0 copy-start.6
  38.5 0.0 collective-permute-done.6.east
  38.5 0.0 copy-start.7
  38.5 0.6 %copy-done.6 = f32[2,8,128]{2,1,0:T(8,128)} copy-done((f32[2,8,128]{2,1,0:T(8,128)}, f32[2,8,128]{2,1,0:T(8,128)S(1)}, u32[]{:S(2)}) %copy-start.6) | copy-done | bytes 8216
  39.1 0.0 copy-done.7
  39.1 0.0 copy-start.10
  39.1 2.1 %sides.3 = (f32[8,8,128]{2,1,0:T(8,128)}, f32[4,8,128]{2,1,0:T(8,128)}) custom-call(s32[4]{0:T(128)} %pad_add_fusion.ids, f32[2,8,128]{2,1,0:T(8,128)} %copy-done.6, f32[2,8,128]{2,1,0:T(8,128)} %copy-done.7, f32[4,8,128]{2,1,0:T(8,128)} %copy-done.2, f32[3,8,128]{2,1,0:T(8,128)} %copy-done.3, f32[7,8,128]{2,1,0:T(8,128)} %get-tuple-element.57.planes, ...), custom_call_target="tpu_custom_call" | custom-call | tf_op jit(solution)/shard_map/sides/pallas_call | solution.py:411
  41.3 1.1 %collective-permute-start.7 = (f32[8,8,128]{2,1,0:T(8,128)}, f32[8,8,128]{2,1,0:T(8,128)S(1)}, u32[]{:S(2)}, u32[]{:S(2)}) collective-permute-start(f32[8,8,128]{2,1,0:T(8,128)} %get-tuple-element.58.mine), channel_id=1, source_target_pairs={{0,1},{1,0},{2,3},{3,2},{4,5},{5,4},{6,7},{7,6},{8,9},{9,8},{10,11... | collective-permute-start | bytes 98312 | tf_op jit(solution)/shard_map/ppermute | solution.py:463
  42.3 0.0 copy-done.10
  42.3 3.3 %collective-permute-start.9 = (f32[8,128]{1,0:T(8,128)S(1)}, f32[8,128]{1,0:T(8,128)S(1)}, u32[]{:S(2)}, u32[]{:S(2)}) collective-permute-start(f32[8,128]{1,0:T(8,128)S(1)} %copy-done.10), channel_id=1, source_target_pairs={{0,3},{1,2},{2,1},{3,0},{4,7},{5,6},{6,5},{7,4},{8,11},{9,10},{10,... | collective-permute-start | bytes 12296 | tf_op jit(solution)/shard_map/ppermute | solution.py:460
  45.6 2.1 %collective-permute-done.9.rest_3_ = f32[8,128]{1,0:T(8,128)S(1)} collective-permute-done((f32[8,128]{1,0:T(8,128)S(1)}, f32[8,128]{1,0:T(8,128)S(1)}, u32[]{:S(2)}, u32[]{:S(2)}) %collective-permute-start.9) | collective-permute-done | bytes 4128 | tf_op jit(solution)/shard_map/ppermute | solution.py:460
  47.7 0.0 copy-start.8
  47.7 0.0 collective-permute-done.7.theirs
  47.7 0.0 copy-start.4
  47.7 0.0 collective-permute-done.8.rest_0_.rest_2_
  47.7 0.0 copy-start.1
  47.7 0.6 %copy-done.8 = f32[8,128]{1,0:T(8,128)} copy-done((f32[8,128]{1,0:T(8,128)}, f32[8,128]{1,0:T(8,128)S(1)}, u32[]{:S(2)}) %copy-start.8) | copy-done | bytes 4120
  48.3 0.0 copy-done.4
  48.3 0.0 copy-done.1
  48.4 4.5 %stencil.3 = (f32[384,128]{1,0:T(8,128)}, f32[384,128]{1,0:T(8,128)}, f32[384,128]{1,0:T(8,128)}, f32[384,128]{1,0:T(8,128)}) custom-call(s32[4]{0:T(128)} %pad_add_fusion.ids, f32[8]{0:T(128)} %coup.3, f32[4,384,128]{2,1,0:T(8,128)} %get-tuple-element.54.proj, f32[384,128]{1,0:T(8,128)} %get-tuple-element.36.spike.rest_1_, ...), custom_call_target="tpu_custom_call" | custom-call | tf_op jit(solution)/shard_map/stencil/pallas_call | solution.py:411
Async XLA Ops:
  4.7 20.5 %collective-permute-start.3 = (f32[7,48,128]{2,1,0:T(8,128)}, f32[7,48,128]{2,1,0:T(8,128)S(1)}, u32[]{:S(2)}, u32[]{:S(2)}) collective-permute-start(f32[7,48,128]{2,1,0:T(8,128)} %get-tuple-element.45), channel_id=1, source_target_pairs={{0,2},{2,0},{1,3},{3,1},{4,6},{6,4},{5,7},{7,5},{8,10},{10,8},{9,1... | collective-permute-start | bytes 516104 | tf_op jit(solution)/shard_map/ppermute | solution.py:456
  8.7 6.7 %collective-permute-start = (f32[4,8,128]{2,1,0:T(8,128)}, f32[4,8,128]{2,1,0:T(8,128)S(1)}, u32[]{:S(2)}, u32[]{:S(2)}) collective-permute-start(f32[4,8,128]{2,1,0:T(8,128)} %get-tuple-element.38), channel_id=1, source_target_pairs={{0,4},{4,8},{8,12},{12,16},{16,20},{20,24},{24,28},{28,0},{1,5},{5... | collective-permute-start | bytes 49160 | tf_op jit(solution)/shard_map/ppermute | solution.py:472
  8.7 6.7 %collective-permute-start.1 = (f32[3,8,128]{2,1,0:T(8,128)}, f32[3,8,128]{2,1,0:T(8,128)S(1)}, u32[]{:S(2)}, u32[]{:S(2)}) collective-permute-start(f32[3,8,128]{2,1,0:T(8,128)} %get-tuple-element.39), channel_id=1, source_target_pairs={{4,0},{8,4},{12,8},{16,12},{20,16},{24,20},{28,24},{0,28},{5,1},{9... | collective-permute-start | bytes 36872 | tf_op jit(solution)/shard_map/ppermute | solution.py:473
  15.4 0.6 %copy-start.3 = (f32[3,8,128]{2,1,0:T(8,128)}, f32[3,8,128]{2,1,0:T(8,128)S(1)}, u32[]{:S(2)}) copy-start(f32[3,8,128]{2,1,0:T(8,128)S(1)} %collective-permute-done.1.east.east_sea.east_const) | copy-start | bytes 36868
  15.4 0.6 %copy-start.2 = (f32[4,8,128]{2,1,0:T(8,128)}, f32[4,8,128]{2,1,0:T(8,128)S(1)}, u32[]{:S(2)}) copy-start(f32[4,8,128]{2,1,0:T(8,128)S(1)} %collective-permute-done.west.west_sea.west_const) | copy-start | bytes 49156
  16.0 3.7 %copy-start.11 = (f32[8,128]{1,0:T(8,128)S(1)}, f32[8,128]{1,0:T(8,128)}, u32[]{:S(2)}) copy-start(f32[8,128]{1,0:T(8,128)} %get-tuple-element.46) | copy-start | bytes 12292
  18.2 7.0 %collective-permute-start.2 = (f32[8,8,128]{2,1,0:T(8,128)}, f32[8,8,128]{2,1,0:T(8,128)S(1)}, u32[]{:S(2)}, u32[]{:S(2)}) collective-permute-start(f32[8,8,128]{2,1,0:T(8,128)} %get-tuple-element.43.mine), channel_id=1, source_target_pairs={{0,1},{1,0},{2,3},{3,2},{4,5},{5,4},{6,7},{7,6},{8,9},{9,8},{10,11... | collective-permute-start | bytes 98312 | tf_op jit(solution)/shard_map/ppermute | solution.py:463
  19.7 5.4 %collective-permute-start.4 = (f32[8,128]{1,0:T(8,128)S(1)}, f32[8,128]{1,0:T(8,128)S(1)}, u32[]{:S(2)}, u32[]{:S(2)}) collective-permute-start(f32[8,128]{1,0:T(8,128)S(1)} %copy-done.11), channel_id=1, source_target_pairs={{0,3},{1,2},{2,1},{3,0},{4,7},{5,6},{6,5},{7,4},{8,11},{9,10},{10,... | collective-permute-start | bytes 12296 | tf_op jit(solution)/shard_map/ppermute | solution.py:460
  25.1 0.6 %copy-start.9 = (f32[8,128]{1,0:T(8,128)}, f32[8,128]{1,0:T(8,128)S(1)}, u32[]{:S(2)}) copy-start(f32[8,128]{1,0:T(8,128)S(1)} %collective-permute-done.4.rest_3_) | copy-start | bytes 12292
  25.1 0.6 %copy-start.5 = (f32[8,8,128]{2,1,0:T(8,128)}, f32[8,8,128]{2,1,0:T(8,128)S(1)}, u32[]{:S(2)}) copy-start(f32[8,8,128]{2,1,0:T(8,128)S(1)} %collective-permute-done.2.theirs) | copy-start | bytes 98308
  25.2 0.7 %copy-start = (f32[7,48,128]{2,1,0:T(8,128)}, f32[7,48,128]{2,1,0:T(8,128)S(1)}, u32[]{:S(2)}) copy-start(f32[7,48,128]{2,1,0:T(8,128)S(1)} %collective-permute-done.3.rest_0_.rest_1_.rest_2_) | copy-start | bytes 516100
  32.2 15.5 %collective-permute-start.8 = (f32[5,48,128]{2,1,0:T(8,128)}, f32[5,48,128]{2,1,0:T(8,128)S(1)}, u32[]{:S(2)}, u32[]{:S(2)}) collective-permute-start(f32[5,48,128]{2,1,0:T(8,128)} %get-tuple-element.60), channel_id=1, source_target_pairs={{0,2},{2,0},{1,3},{3,1},{4,6},{6,4},{5,7},{7,5},{8,10},{10,8},{9,1... | collective-permute-start | bytes 368648 | tf_op jit(solution)/shard_map/ppermute | solution.py:456
  32.2 6.2 %collective-permute-start.5 = (f32[2,8,128]{2,1,0:T(8,128)}, f32[2,8,128]{2,1,0:T(8,128)S(1)}, u32[]{:S(2)}, u32[]{:S(2)}) collective-permute-start(f32[2,8,128]{2,1,0:T(8,128)} %get-tuple-element.55), channel_id=1, source_target_pairs={{0,4},{4,8},{8,12},{12,16},{16,20},{20,24},{24,28},{28,0},{1,5},{5... | collective-permute-start | bytes 24584 | tf_op jit(solution)/shard_map/ppermute | solution.py:530
  32.3 6.2 %collective-permute-start.6 = (f32[2,8,128]{2,1,0:T(8,128)}, f32[2,8,128]{2,1,0:T(8,128)S(1)}, u32[]{:S(2)}, u32[]{:S(2)}) collective-permute-start(f32[2,8,128]{2,1,0:T(8,128)} %get-tuple-element.56), channel_id=1, source_target_pairs={{4,0},{8,4},{12,8},{16,12},{20,16},{24,20},{28,24},{0,28},{5,1},{9... | collective-permute-start | bytes 24584 | tf_op jit(solution)/shard_map/ppermute | solution.py:531
  38.5 0.6 %copy-start.6 = (f32[2,8,128]{2,1,0:T(8,128)}, f32[2,8,128]{2,1,0:T(8,128)S(1)}, u32[]{:S(2)}) copy-start(f32[2,8,128]{2,1,0:T(8,128)S(1)} %collective-permute-done.5.west) | copy-start | bytes 24580
  38.5 0.6 %copy-start.7 = (f32[2,8,128]{2,1,0:T(8,128)}, f32[2,8,128]{2,1,0:T(8,128)S(1)}, u32[]{:S(2)}) copy-start(f32[2,8,128]{2,1,0:T(8,128)S(1)} %collective-permute-done.6.east) | copy-start | bytes 24580
  39.1 3.2 %copy-start.10 = (f32[8,128]{1,0:T(8,128)S(1)}, f32[8,128]{1,0:T(8,128)}, u32[]{:S(2)}) copy-start(f32[8,128]{1,0:T(8,128)} %get-tuple-element.61) | copy-start | bytes 12292
  41.3 6.5 %collective-permute-start.7 = (f32[8,8,128]{2,1,0:T(8,128)}, f32[8,8,128]{2,1,0:T(8,128)S(1)}, u32[]{:S(2)}, u32[]{:S(2)}) collective-permute-start(f32[8,8,128]{2,1,0:T(8,128)} %get-tuple-element.58.mine), channel_id=1, source_target_pairs={{0,1},{1,0},{2,3},{3,2},{4,5},{5,4},{6,7},{7,6},{8,9},{9,8},{10,11... | collective-permute-start | bytes 98312 | tf_op jit(solution)/shard_map/ppermute | solution.py:463
  42.3 5.4 %collective-permute-start.9 = (f32[8,128]{1,0:T(8,128)S(1)}, f32[8,128]{1,0:T(8,128)S(1)}, u32[]{:S(2)}, u32[]{:S(2)}) collective-permute-start(f32[8,128]{1,0:T(8,128)S(1)} %copy-done.10), channel_id=1, source_target_pairs={{0,3},{1,2},{2,1},{3,0},{4,7},{5,6},{6,5},{7,4},{8,11},{9,10},{10,... | collective-permute-start | bytes 12296 | tf_op jit(solution)/shard_map/ppermute | solution.py:460
  47.7 0.6 %copy-start.8 = (f32[8,128]{1,0:T(8,128)}, f32[8,128]{1,0:T(8,128)S(1)}, u32[]{:S(2)}) copy-start(f32[8,128]{1,0:T(8,128)S(1)} %collective-permute-done.9.rest_3_) | copy-start | bytes 12292
  47.7 0.6 %copy-start.4 = (f32[8,8,128]{2,1,0:T(8,128)}, f32[8,8,128]{2,1,0:T(8,128)S(1)}, u32[]{:S(2)}) copy-start(f32[8,8,128]{2,1,0:T(8,128)S(1)} %collective-permute-done.7.theirs) | copy-start | bytes 98308
  47.7 0.6 %copy-start.1 = (f32[5,48,128]{2,1,0:T(8,128)}, f32[5,48,128]{2,1,0:T(8,128)S(1)}, u32[]{:S(2)}) copy-start(f32[5,48,128]{2,1,0:T(8,128)S(1)} %collective-permute-done.8.rest_0_.rest_2_) | copy-start | bytes 368644

commit v2 on v1

--- a/solution.py
+++ b/solution.py
@@ -17,6 +17,7 @@
 haline = 0.8
 
 BLOCK = 8
+VMEM_BYTES = 12 * 1024 * 1024
 f32 = jnp.float32
 bf16 = jnp.bfloat16
 CORNER_LANE = 16
@@ -414,6 +415,7 @@
         in_specs=specs,
         out_specs=[pl.BlockSpec(memory_space=pltpu.VMEM)] * len(outs),
         scratch_shapes=list(scratch),
+        compiler_params=pltpu.CompilerParams(vmem_limit_bytes=VMEM_BYTES),
         name=name,
     )(*args)
 

time: 53.2 us -> 47.4 us (0.89)
  Pallas kernels: 26 us -> 14.9 us
  local copies, waits for them, and re-layouts: 2.49 us -> 8.43 us
  other arithmetic: 0.66 us -> 0.08 us
    pallas_call x7, Pallas kernels: 26 us -> 14.9 us  [call(): pl.pallas_call(kernel, out_shape=[jax.ShapeDtypeStruct(shape, kind) for s...]
    unnamed x24 -> x28, local copies, waits for them, and re-layouts: 2.49 us -> 8.43 us
    another operation x1, other arithmetic: 0.66 us -> 0.08 us  [on_device(): jnp.stack([lat, depth, (levels - 1) * (1 - depth), jnp.int32(lats)])]
  transfers between devices with their start and end apart: 10 -> 10, of which waited for: 2 -> 2; matrix products, arithmetic and copies ran while one was open for 0% -> 0% of each run, Pallas kernels for 22% -> 12%
where the time goes in v2:
time: 47.4 us; the launch traced here: 47.1 us
  starting transfers between devices  15.6 us (33%)
  Pallas kernels  14.9 us (31%)
  local copies, waits for them, and re-layouts  8.43 us (18%)
  waiting for transfers between devices  7.35 us (16%)
  between operations  0.79 us (2%)
    pallas_call x7, Pallas kernels, call(): pl.pallas_call(kernel, out_shape=[jax.ShapeDtypeStruct(shape, kind) for s...  14.9 us
    unnamed x28, local copies, waits for them, and re-layouts  8.43 us
    ppermute x2, waiting for transfers between devices, to_lat(): return [lax.ppermute(m, ('lat', 'depth'), r) for m, r in zip(msgs, both)]  7.33 us
    ppermute x2, starting transfers between devices, to_lat(): return [lax.ppermute(m, 'lat', r) for m, r in zip(msgs, routes)]  4.2 us
    ppermute x2, starting transfers between devices, to_lat(): return [lax.ppermute(m, ('lat', 'depth'), r) for m, r in zip(msgs, both)]  3.48 us
    ppermute x1, starting transfers between devices, on_device(): east_const = lax.ppermute(to_west, 'lon', back)  2.64 us
    ppermute x1, starting transfers between devices, on_device(): east_in = lax.ppermute(result[5], 'lon', back)  2.63 us
    ppermute x2, starting transfers between devices, to_depth(): lax.ppermute(msg, 'depth', [(d, depths - 1 - d) for d in range(depths)])  2.55 us
  transfers between devices with their start and end apart: 10, of which 2 were waited for; matrix products, arithmetic and copies ran while one was open for 0% of the time, Pallas kernels for 12%

profile of v2, /device:TPU:0, one launch (start us, length us, event | category | flops | bytes accessed | tf_op | source)
XLA Modules:
  0.0 47.1 jit_solution(1315546297304046317)
XLA Ops:
  0.6 0.1 pad_add_fusion.ids
  0.7 0.0 copy-start
  0.7 0.9 %copy-done = s32[48,8,128]{2,1,0:T(8,128)S(1)} copy-done((s32[48,8,128]{2,1,0:T(8,128)S(1)}, s32[48,8,128]{2,1,0:T(8,128)}, u32[]{:S(2)}) %copy-start) | copy-done | bytes 196632
  1.6 0.0 copy-start.2
  1.6 1.0 %copy-done.2 = s32[2,48,8,128]{3,2,1,0:T(8,128)S(1)} copy-done((s32[2,48,8,128]{3,2,1,0:T(8,128)S(1)}, s32[2,48,8,128]{3,2,1,0:T(8,128)}, u32[]{:S(2)}) %copy-start.2) | copy-done | bytes 393240
  2.6 0.0 copy-start.4
  2.6 0.9 %copy-done.4 = f32[48,8,128]{2,1,0:T(8,128)S(1)} copy-done((f32[48,8,128]{2,1,0:T(8,128)S(1)}, f32[48,8,128]{2,1,0:T(8,128)}, u32[]{:S(2)}) %copy-start.4) | copy-done | bytes 196632
  3.6 0.0 copy-start.6
  3.6 0.9 %copy-done.6 = f32[48,8,128]{2,1,0:T(8,128)S(1)} copy-done((f32[48,8,128]{2,1,0:T(8,128)S(1)}, f32[48,8,128]{2,1,0:T(8,128)}, u32[]{:S(2)}) %copy-start.6) | copy-done | bytes 196632
  4.5 0.0 copy-start.8
  4.5 0.9 %copy-done.8 = f32[48,8,128]{2,1,0:T(8,128)S(1)} copy-done((f32[48,8,128]{2,1,0:T(8,128)S(1)}, f32[48,8,128]{2,1,0:T(8,128)}, u32[]{:S(2)}) %copy-start.8) | copy-done | bytes 196632
  5.4 0.0 copy-start.9
  5.4 0.9 %copy-done.9 = f32[48,8,128]{2,1,0:T(8,128)S(1)} copy-done((f32[48,8,128]{2,1,0:T(8,128)S(1)}, f32[48,8,128]{2,1,0:T(8,128)}, u32[]{:S(2)}) %copy-start.9) | copy-done | bytes 196632
  6.3 0.0 copy-start.10
  6.4 0.9 %copy-done.10 = f32[48,8,128]{2,1,0:T(8,128)S(1)} copy-done((f32[48,8,128]{2,1,0:T(8,128)S(1)}, f32[48,8,128]{2,1,0:T(8,128)}, u32[]{:S(2)}) %copy-start.10) | copy-done | bytes 196632
  7.3 0.0 copy-start.11
  7.3 0.9 %copy-done.11 = f32[48,8,128]{2,1,0:T(8,128)S(1)} copy-done((f32[48,8,128]{2,1,0:T(8,128)S(1)}, f32[48,8,128]{2,1,0:T(8,128)}, u32[]{:S(2)}) %copy-start.11) | copy-done | bytes 196632
  8.2 0.0 copy-start.12
  8.2 0.9 %copy-done.12 = f32[8,48,48]{2,1,0:T(8,128)S(1)} copy-done((f32[8,48,48]{2,1,0:T(8,128)S(1)}, f32[8,48,48]{2,1,0:T(8,128)}, u32[]{:S(2)}) %copy-start.12) | copy-done | bytes 73752
  9.1 1.7 %pack.1 = (f32[4,8,128]{2,1,0:T(8,128)S(1)}, f32[3,8,128]{2,1,0:T(8,128)S(1)}, f32[48,128]{1,0:T(8,128)S(1)}, f32[7,48,128]{2,1,0:T(8,128)S(1)}) custom-call(s32[4]{0:T(128)S(1)} %pad_add_fusion.ids, f32[384,128]{1,0:T(8,128)S(1)} %bitcast.29, f32[384,128]{1,0:T(8,128)S(1)} %bitcast.31, f32[384,128]{1,0:T(8,128)S(1)} %bitcast.33, f32[384,128]{1,0:T(8,128)S(1)} %bitcast.35, ...), custom_call_target="tpu_custom_call" | custom-call | tf_op jit(solution)/shard_map/pack/pallas_call | solution.py:412
  10.8 4.1 %collective-permute-start.3 = (f32[7,48,128]{2,1,0:T(8,128)S(1)}, f32[7,48,128]{2,1,0:T(8,128)S(1)}, u32[]{:S(2)}, u32[]{:S(2)}) collective-permute-start(f32[7,48,128]{2,1,0:T(8,128)S(1)} %get-tuple-element.45), channel_id=1, source_target_pairs={{0,2},{2,0},{1,3},{3,1},{4,6},{6,4},{5,7},{7,5},{8,10},{10,8},{9,1... | collective-permute-start | bytes 516104 | tf_op jit(solution)/shard_map/ppermute | solution.py:458
  14.9 0.0 copy-start.13
  14.9 0.0 collective-permute-start
  14.9 2.6 %collective-permute-start.1 = (f32[3,8,128]{2,1,0:T(8,128)S(1)}, f32[3,8,128]{2,1,0:T(8,128)S(1)}, u32[]{:S(2)}, u32[]{:S(2)}) collective-permute-start(f32[3,8,128]{2,1,0:T(8,128)S(1)} %get-tuple-element.39), channel_id=1, source_target_pairs={{4,0},{8,4},{12,8},{16,12},{20,16},{24,20},{28,24},{0,28},{5,1},{9... | collective-permute-start | bytes 36872 | tf_op jit(solution)/shard_map/ppermute | solution.py:475
  17.6 0.0 copy-done.13
  17.6 0.0 copy-start.7
  17.6 2.2 %project.2 = (f32[4,384,128]{2,1,0:T(8,128)S(1)}, f32[7,8,128]{2,1,0:T(8,128)S(1)}, f32[8,128]{1,0:T(8,128)S(1)}, f32[384,128]{1,0:T(8,128)S(1)}, bf16[384,384]{...) custom-call(s32[4]{0:T(128)S(1)} %pad_add_fusion.ids, ...), custom_call_target="tpu_custom_call" | custom-call | tf_op jit(solution)/shard_map/project/pallas_call | solution.py:412
  19.8 0.0 collective-permute-done.1.east.east_sea.east_const
  19.8 0.0 collective-permute-done.west.west_sea.west_const
  19.8 0.0 copy-start.1
  19.8 0.0 copy-start.3
  19.8 0.0 copy-start.5
  19.8 0.9 %sides.2 = (f32[8,8,128]{2,1,0:T(8,128)S(1)}, f32[4,8,128]{2,1,0:T(8,128)S(1)}) custom-call(s32[4]{0:T(128)S(1)} %pad_add_fusion.ids, f32[4,8,128]{2,1,0:T(8,128)S(1)} %collective-permute-done.west.west_sea.west_const, f32[3,8,128]{2,1,0:T(8,128)S(1)} %collective-permute-done.1.east.east_sea.east_const, ...), custom_call_target="tpu_custom_call" | custom-call | tf_op jit(solution)/shard_map/sides/pallas_call | solution.py:412
  20.7 1.6 %collective-permute-start.2 = (f32[8,8,128]{2,1,0:T(8,128)S(1)}, f32[8,8,128]{2,1,0:T(8,128)S(1)}, u32[]{:S(2)}, u32[]{:S(2)}) collective-permute-start(f32[8,8,128]{2,1,0:T(8,128)S(1)} %get-tuple-element.43.mine), channel_id=1, source_target_pairs={{0,1},{1,0},{2,3},{3,2},{4,5},{5,4},{6,7},{7,6},{8,9},{9,8},{10,11... | collective-permute-start | bytes 98312 | tf_op jit(solution)/shard_map/ppermute | solution.py:465
  22.3 0.0 collective-permute-start.4
  22.3 5.4 %collective-permute-done.4.rest_3_ = f32[8,128]{1,0:T(8,128)S(1)} collective-permute-done((f32[8,128]{1,0:T(8,128)S(1)}, f32[8,128]{1,0:T(8,128)S(1)}, u32[]{:S(2)}, u32[]{:S(2)}) %collective-permute-start.4) | collective-permute-done | bytes 4128 | tf_op jit(solution)/shard_map/ppermute | solution.py:462
  27.7 0.0 collective-permute-done.2.theirs
  27.8 0.0 collective-permute-done.3.rest_0_.rest_1_.rest_2_
  27.8 0.0 copy-done.7
  27.8 0.0 copy-done.1
  27.8 0.0 copy-done.3
  27.8 0.0 copy-done.5
  27.8 4.3 %stencil.2 = (f32[384,128]{1,0:T(8,128)S(1)}, f32[384,128]{1,0:T(8,128)S(1)}, f32[384,128]{1,0:T(8,128)S(1)}, f32[384,128]{1,0:T(8,128)S(1)}, f32[2,8,128]{2,1,0...) custom-call(s32[4]{0:T(128)S(1)} %pad_add_fusion.ids, f32[8]{0:T(128)S(1)} %copy-done.13, ...), custom_call_target="tpu_custom_call" | custom-call | tf_op jit(solution)/shard_map/stencil/pallas_call | solution.py:412
  32.1 0.1 collective-permute-start.8
  32.2 0.1 collective-permute-start.5
  32.3 2.6 %collective-permute-start.6 = (f32[2,8,128]{2,1,0:T(8,128)S(1)}, f32[2,8,128]{2,1,0:T(8,128)S(1)}, u32[]{:S(2)}, u32[]{:S(2)}) collective-permute-start(f32[2,8,128]{2,1,0:T(8,128)S(1)} %get-tuple-element.56), channel_id=1, source_target_pairs={{4,0},{8,4},{12,8},{16,12},{20,16},{24,20},{28,24},{0,28},{5,1},{9... | collective-permute-start | bytes 24584 | tf_op jit(solution)/shard_map/ppermute | solution.py:533
  34.9 1.7 %project.3 = (f32[4,384,128]{2,1,0:T(8,128)S(1)}, f32[7,8,128]{2,1,0:T(8,128)S(1)}, f32[8,128]{1,0:T(8,128)S(1)}) custom-call(s32[4]{0:T(128)S(1)} %pad_add_fusion.ids, f32[384,128]{1,0:T(8,128)S(1)} %get-tuple-element.48.t, f32[384,128]{1,0:T(8,128)S(1)} %get-tuple-element.49.s, f32[384,128]{1,0:T(8,128)S(1)} %get-tuple-element.50.u, ...), custom_call_target="tpu_custom_call" | custom-call | tf_op jit(solution)/shard_map/project/pallas_call | solution.py:412
  36.6 0.0 collective-permute-done.5.west
  36.6 0.0 collective-permute-done.6.east
  36.6 0.9 %sides.3 = (f32[8,8,128]{2,1,0:T(8,128)S(1)}, f32[4,8,128]{2,1,0:T(8,128)S(1)}) custom-call(s32[4]{0:T(128)S(1)} %pad_add_fusion.ids, f32[2,8,128]{2,1,0:T(8,128)S(1)} %collective-permute-done.5.west, f32[2,8,128]{2,1,0:T(8,128)S(1)} %collective-permute-done.6.east, f32[4,8,128]{2,1,0:T(8,128)S(1)} %collective-permute-done.west.west_sea.west_const, ...), custom_call_target="tpu_custom_call" | custom-call | tf_op jit(solution)/shard_map/sides/pallas_call | solution.py:412
  37.4 0.9 %collective-permute-start.7 = (f32[8,8,128]{2,1,0:T(8,128)S(1)}, f32[8,8,128]{2,1,0:T(8,128)S(1)}, u32[]{:S(2)}, u32[]{:S(2)}) collective-permute-start(f32[8,8,128]{2,1,0:T(8,128)S(1)} %get-tuple-element.58.mine), channel_id=1, source_target_pairs={{0,1},{1,0},{2,3},{3,2},{4,5},{5,4},{6,7},{7,6},{8,9},{9,8},{10,11... | collective-permute-start | bytes 98312 | tf_op jit(solution)/shard_map/ppermute | solution.py:465
  38.4 3.5 %collective-permute-start.9 = (f32[8,128]{1,0:T(8,128)S(1)}, f32[8,128]{1,0:T(8,128)S(1)}, u32[]{:S(2)}, u32[]{:S(2)}) collective-permute-start(f32[8,128]{1,0:T(8,128)S(1)} %get-tuple-element.61), channel_id=1, source_target_pairs={{0,3},{1,2},{2,1},{3,0},{4,7},{5,6},{6,5},{7,4},{8,11},{9,10},{10,... | collective-permute-start | bytes 12296 | tf_op jit(solution)/shard_map/ppermute | solution.py:462
  41.8 1.9 %collective-permute-done.9.rest_3_ = f32[8,128]{1,0:T(8,128)S(1)} collective-permute-done((f32[8,128]{1,0:T(8,128)S(1)}, f32[8,128]{1,0:T(8,128)S(1)}, u32[]{:S(2)}, u32[]{:S(2)}) %collective-permute-start.9) | collective-permute-done | bytes 4128 | tf_op jit(solution)/shard_map/ppermute | solution.py:462
  43.8 0.0 collective-permute-done.7.theirs
  43.8 0.0 collective-permute-done.8.rest_0_.rest_2_
  43.8 3.3 %stencil.3 = (f32[384,128]{1,0:T(8,128)}, f32[384,128]{1,0:T(8,128)}, f32[384,128]{1,0:T(8,128)}, f32[384,128]{1,0:T(8,128)}) custom-call(s32[4]{0:T(128)S(1)} %pad_add_fusion.ids, f32[8]{0:T(128)S(1)} %copy-done.13, f32[4,384,128]{2,1,0:T(8,128)S(1)} %get-tuple-element.54.proj, f32[384,128]{1,0:T(8,128)S(1)} %get-tuple-element.36.spike.rest_1_, ...), custom_call_target="tpu_custom_call" | custom-call | tf_op jit(solution)/shard_map/stencil/pallas_call | solution.py:412
Async XLA Ops:
  0.7 0.9 %copy-start = (s32[48,8,128]{2,1,0:T(8,128)S(1)}, s32[48,8,128]{2,1,0:T(8,128)}, u32[]{:S(2)}) copy-start(s32[48,8,128]{2,1,0:T(8,128)} %param.17) | copy-start | bytes 589828
  1.6 1.0 %copy-start.2 = (s32[2,48,8,128]{3,2,1,0:T(8,128)S(1)}, s32[2,48,8,128]{3,2,1,0:T(8,128)}, u32[]{:S(2)}) copy-start(s32[2,48,8,128]{3,2,1,0:T(8,128)} %param.16) | copy-start | bytes 1179652
  2.6 0.9 %copy-start.4 = (f32[48,8,128]{2,1,0:T(8,128)S(1)}, f32[48,8,128]{2,1,0:T(8,128)}, u32[]{:S(2)}) copy-start(f32[48,8,128]{2,1,0:T(8,128)} %param.14) | copy-start | bytes 589828
  3.6 0.9 %copy-start.6 = (f32[48,8,128]{2,1,0:T(8,128)S(1)}, f32[48,8,128]{2,1,0:T(8,128)}, u32[]{:S(2)}) copy-start(f32[48,8,128]{2,1,0:T(8,128)} %param.15) | copy-start | bytes 589828
  4.5 0.9 %copy-start.8 = (f32[48,8,128]{2,1,0:T(8,128)S(1)}, f32[48,8,128]{2,1,0:T(8,128)}, u32[]{:S(2)}) copy-start(f32[48,8,128]{2,1,0:T(8,128)} %param.10) | copy-start | bytes 589828
  5.4 0.9 %copy-start.9 = (f32[48,8,128]{2,1,0:T(8,128)S(1)}, f32[48,8,128]{2,1,0:T(8,128)}, u32[]{:S(2)}) copy-start(f32[48,8,128]{2,1,0:T(8,128)} %param.11) | copy-start | bytes 589828
  6.3 0.9 %copy-start.10 = (f32[48,8,128]{2,1,0:T(8,128)S(1)}, f32[48,8,128]{2,1,0:T(8,128)}, u32[]{:S(2)}) copy-start(f32[48,8,128]{2,1,0:T(8,128)} %param.12) | copy-start | bytes 589828
  7.3 0.9 %copy-start.11 = (f32[48,8,128]{2,1,0:T(8,128)S(1)}, f32[48,8,128]{2,1,0:T(8,128)}, u32[]{:S(2)}) copy-start(f32[48,8,128]{2,1,0:T(8,128)} %param.13) | copy-start | bytes 589828
  8.2 0.9 %copy-start.12 = (f32[8,48,48]{2,1,0:T(8,128)S(1)}, f32[8,48,48]{2,1,0:T(8,128)}, u32[]{:S(2)}) copy-start(f32[8,48,48]{2,1,0:T(8,128)} %inverse.1) | copy-start | bytes 221188
  10.8 16.9 %collective-permute-start.3 = (f32[7,48,128]{2,1,0:T(8,128)S(1)}, f32[7,48,128]{2,1,0:T(8,128)S(1)}, u32[]{:S(2)}, u32[]{:S(2)}) collective-permute-start(f32[7,48,128]{2,1,0:T(8,128)S(1)} %get-tuple-element.45), channel_id=1, source_target_pairs={{0,2},{2,0},{1,3},{3,1},{4,6},{6,4},{5,7},{7,5},{8,10},{10,8},{9,1... | collective-permute-start | bytes 516104 | tf_op jit(solution)/shard_map/ppermute | solution.py:458
  14.9 2.6 %copy-start.13 = (f32[8]{0:T(128)S(1)}, f32[8]{0:T(128)}, u32[]{:S(2)}) copy-start(f32[8]{0:T(128)} %coup.3) | copy-start | bytes 100
  14.9 4.9 %collective-permute-start = (f32[4,8,128]{2,1,0:T(8,128)S(1)}, f32[4,8,128]{2,1,0:T(8,128)S(1)}, u32[]{:S(2)}, u32[]{:S(2)}) collective-permute-start(f32[4,8,128]{2,1,0:T(8,128)S(1)} %get-tuple-element.38), channel_id=1, source_target_pairs={{0,4},{4,8},{8,12},{12,16},{16,20},{20,24},{24,28},{28,0},{1,5},{5... | collective-permute-start | bytes 49160 | tf_op jit(solution)/shard_map/ppermute | solution.py:474
  14.9 4.8 %collective-permute-start.1 = (f32[3,8,128]{2,1,0:T(8,128)S(1)}, f32[3,8,128]{2,1,0:T(8,128)S(1)}, u32[]{:S(2)}, u32[]{:S(2)}) collective-permute-start(f32[3,8,128]{2,1,0:T(8,128)S(1)} %get-tuple-element.39), channel_id=1, source_target_pairs={{4,0},{8,4},{12,8},{16,12},{20,16},{24,20},{28,24},{0,28},{5,1},{9... | collective-permute-start | bytes 36872 | tf_op jit(solution)/shard_map/ppermute | solution.py:475
  17.6 10.2 %copy-start.7 = (f32[48,8,128]{2,1,0:T(8,128)S(1)}, f32[48,8,128]{2,1,0:T(8,128)}, u32[]{:S(2)}) copy-start(f32[48,8,128]{2,1,0:T(8,128)} %param.15) | copy-start | bytes 589828
  19.8 8.0 %copy-start.1 = (s32[48,8,128]{2,1,0:T(8,128)S(1)}, s32[48,8,128]{2,1,0:T(8,128)}, u32[]{:S(2)}) copy-start(s32[48,8,128]{2,1,0:T(8,128)} %param.17) | copy-start | bytes 589828
  19.8 8.0 %copy-start.3 = (s32[2,48,8,128]{3,2,1,0:T(8,128)S(1)}, s32[2,48,8,128]{3,2,1,0:T(8,128)}, u32[]{:S(2)}) copy-start(s32[2,48,8,128]{3,2,1,0:T(8,128)} %param.16) | copy-start | bytes 1179652
  19.8 8.0 %copy-start.5 = (f32[48,8,128]{2,1,0:T(8,128)S(1)}, f32[48,8,128]{2,1,0:T(8,128)}, u32[]{:S(2)}) copy-start(f32[48,8,128]{2,1,0:T(8,128)} %param.14) | copy-start | bytes 589828
  20.7 7.0 %collective-permute-start.2 = (f32[8,8,128]{2,1,0:T(8,128)S(1)}, f32[8,8,128]{2,1,0:T(8,128)S(1)}, u32[]{:S(2)}, u32[]{:S(2)}) collective-permute-start(f32[8,8,128]{2,1,0:T(8,128)S(1)} %get-tuple-element.43.mine), channel_id=1, source_target_pairs={{0,1},{1,0},{2,3},{3,2},{4,5},{5,4},{6,7},{7,6},{8,9},{9,8},{10,11... | collective-permute-start | bytes 98312 | tf_op jit(solution)/shard_map/ppermute | solution.py:465
  22.3 5.4 %collective-permute-start.4 = (f32[8,128]{1,0:T(8,128)S(1)}, f32[8,128]{1,0:T(8,128)S(1)}, u32[]{:S(2)}, u32[]{:S(2)}) collective-permute-start(f32[8,128]{1,0:T(8,128)S(1)} %get-tuple-element.46), channel_id=1, source_target_pairs={{0,3},{1,2},{2,1},{3,0},{4,7},{5,6},{6,5},{7,4},{8,11},{9,10},{10,... | collective-permute-start | bytes 12296 | tf_op jit(solution)/shard_map/ppermute | solution.py:462
  32.1 11.7 %collective-permute-start.8 = (f32[5,48,128]{2,1,0:T(8,128)S(1)}, f32[5,48,128]{2,1,0:T(8,128)S(1)}, u32[]{:S(2)}, u32[]{:S(2)}) collective-permute-start(f32[5,48,128]{2,1,0:T(8,128)S(1)} %get-tuple-element.60), channel_id=1, source_target_pairs={{0,2},{2,0},{1,3},{3,1},{4,6},{6,4},{5,7},{7,5},{8,10},{10,8},{9,1... | collective-permute-start | bytes 368648 | tf_op jit(solution)/shard_map/ppermute | solution.py:458
  32.2 4.4 %collective-permute-start.5 = (f32[2,8,128]{2,1,0:T(8,128)S(1)}, f32[2,8,128]{2,1,0:T(8,128)S(1)}, u32[]{:S(2)}, u32[]{:S(2)}) collective-permute-start(f32[2,8,128]{2,1,0:T(8,128)S(1)} %get-tuple-element.55), channel_id=1, source_target_pairs={{0,4},{4,8},{8,12},{12,16},{16,20},{20,24},{24,28},{28,0},{1,5},{5... | collective-permute-start | bytes 24584 | tf_op jit(solution)/shard_map/ppermute | solution.py:532
  32.3 4.3 %collective-permute-start.6 = (f32[2,8,128]{2,1,0:T(8,128)S(1)}, f32[2,8,128]{2,1,0:T(8,128)S(1)}, u32[]{:S(2)}, u32[]{:S(2)}) collective-permute-start(f32[2,8,128]{2,1,0:T(8,128)S(1)} %get-tuple-element.56), channel_id=1, source_target_pairs={{4,0},{8,4},{12,8},{16,12},{20,16},{24,20},{28,24},{0,28},{5,1},{9... | collective-permute-start | bytes 24584 | tf_op jit(solution)/shard_map/ppermute | solution.py:533
  37.4 6.3 %collective-permute-start.7 = (f32[8,8,128]{2,1,0:T(8,128)S(1)}, f32[8,8,128]{2,1,0:T(8,128)S(1)}, u32[]{:S(2)}, u32[]{:S(2)}) collective-permute-start(f32[8,8,128]{2,1,0:T(8,128)S(1)} %get-tuple-element.58.mine), channel_id=1, source_target_pairs={{0,1},{1,0},{2,3},{3,2},{4,5},{5,4},{6,7},{7,6},{8,9},{9,8},{10,11... | collective-permute-start | bytes 98312 | tf_op jit(solution)/shard_map/ppermute | solution.py:465
  38.4 5.4 %collective-permute-start.9 = (f32[8,128]{1,0:T(8,128)S(1)}, f32[8,128]{1,0:T(8,128)S(1)}, u32[]{:S(2)}, u32[]{:S(2)}) collective-permute-start(f32[8,128]{1,0:T(8,128)S(1)} %get-tuple-element.61), channel_id=1, source_target_pairs={{0,3},{1,2},{2,1},{3,0},{4,7},{5,6},{6,5},{7,4},{8,11},{9,10},{10,... | collective-permute-start | bytes 12296 | tf_op jit(solution)/shard_map/ppermute | solution.py:462

commit v3 on v2

--- a/solution.py
+++ b/solution.py
@@ -16,7 +16,7 @@
 viscosity = 0.1
 haline = 0.8
 
-BLOCK = 8
+BLOCK = 48
 VMEM_BYTES = 12 * 1024 * 1024
 f32 = jnp.float32
 bf16 = jnp.bfloat16
@@ -50,8 +50,29 @@
     return jnp.broadcast_to(value[:, lane : lane + 1], value.shape)
 
 
+def level_at(k, rows):
+    return pl.ds(k * rows if isinstance(k, int) else pl.multiple_of(k * rows, rows), rows)
+
+
 def level(ref, k, rows):
-    return ref[pl.ds(pl.multiple_of(k * rows, rows), rows), :]
+    return ref[level_at(k, rows), :]
+
+
+def turn(value, shift):
+    return pltpu.roll(value, shift % value.shape[1], 1)
+
+
+def each_level(levels, body, carry):
+    block = min(BLOCK, levels)
+
+    def some(b, carry):
+        for i in range(block):
+            carry = body(b * block + i, carry)
+        return carry
+
+    if block == levels:
+        return some(0, carry)
+    return lax.fori_loop(0, levels // block, some, carry)
 
 
 def take_row(ref, row, levels, rows):
@@ -66,42 +87,43 @@
     return [jnp.where(lat == 0, rows - 1, 0)] if pair else [0, rows - 1]
 
 
-def pack_kernel(dims, ids, t, s, u, v, sea, east, north, flags, inverse, to_east, to_west, nn_late, *lat_msgs):
+def pack_kernel(dims, ids, *refs):
     levels, rows, cols, half, pair = dims
+    sources, (to_east, to_west, nn_late), rest = refs[:9], refs[9:12], refs[12:]
+    count = 1 if pair else 2
+    lat_msgs, copies, sems = rest[:count], rest[count : count + 9], rest[-1]
+    moves = [pltpu.make_async_copy(a, b, sems.at[i]) for i, (a, b) in enumerate(zip(sources, copies))]
+    for move in moves:
+        move.start()
+    t, s, u, v, sea, east, north, flags, inverse = copies
     lane = iota((rows, cols), 1)
     fields = (t, s, u, v)
-
-    def some(b, carry):
-        accs = list(carry)
-        for i in range(BLOCK):
-            k = b * BLOCK + i
-            here = [level(x, k, rows) for x in fields]
-            wet = level(sea, k, rows).astype(f32)
-            speed = level(east, k, rows)
-            nexts = []
-            for step in (1, 0):
-                zonal, _ = branches(level(flags.at[step], k, rows))
-                nexts.append(wet * (speed * zonal - diffusion))
-            low, high = lane == k, lane == k + half
-            last = here + [wet] + nexts
-            for j, value in enumerate(last):
-                place = k + (j % 2) * half
-                accs[j // 2] = jnp.where(
-                    high if j % 2 else low, pltpu.roll(value, (place + 1) % cols, 1), accs[j // 2]
-                )
-            for j, value in enumerate(here + [wet]):
-                place = k + (j % 2) * half
-                accs[4 + j // 2] = jnp.where(
-                    high if j % 2 else low, pltpu.roll(value, place % cols, 1), accs[4 + j // 2]
-                )
+    for move in moves:
+        move.wait()
+
+    def one(k, accs):
+        accs = list(accs)
+        here = [level(x, k, rows) for x in (*fields, sea, east, flags.at[1], flags.at[0])]
+        at = lane == k, lane == k + half
+        for j, value in enumerate(here):
+            accs[j // 2 if j < 4 else j - 2] = jnp.where(
+                at[j % 2 if j < 4 else 0],
+                turn(value, k + (j % 2 if j < 4 else 0) * half + 1),
+                accs[j // 2 if j < 4 else j - 2],
+            )
+        for j, value in enumerate(here[:5]):
+            accs[6 + j // 2] = jnp.where(at[j % 2], turn(value, k + (j % 2) * half), accs[6 + j // 2])
         return tuple(accs)
 
-    zero = jnp.zeros((rows, cols), f32)
-    accs = lax.fori_loop(0, levels // BLOCK, some, (zero,) * 7)
-    for j in range(4):
-        to_east[j] = accs[j]
-    for j in range(3):
-        to_west[j] = accs[4 + j]
+    zero, none = jnp.zeros((rows, cols), f32), jnp.zeros((rows, cols), jnp.int32)
+    accs = each_level(levels, one, (zero, zero, none, zero, none, none, zero, zero, none))
+    wet, speed = accs[2].astype(f32), accs[3]
+    nexts = [wet * (speed * branches(flag)[0] - diffusion) for flag in accs[4:6]]
+    to_east[0], to_east[1] = accs[0], accs[1]
+    to_east[2] = jnp.where(lane < half, wet, turn(nexts[0], half))
+    to_east[3] = nexts[1]
+    to_west[0], to_west[1] = accs[6], accs[7]
+    to_west[2] = accs[8].astype(f32)
     for which, row in enumerate(row_choices(pair, rows, ids[0])):
         msg = lat_msgs[which]
         for j, x in enumerate(fields):
@@ -124,11 +146,40 @@
         msg[6, :, pl.ds(0, levels)] = block
 
 
+def coef_kernel(dims, sea, east, north, flags, west_const, east_const, out):
+    levels, rows, cols, half, pair = dims
+    lane, row = iota((rows, cols), 1), iota((rows, cols), 0)
+    sea_side = east_const[2]
+    sides = (west_const[3], west_const[2])
+
+    def one(k, carry):
+        wet = level(sea, k, rows).astype(f32)
+        part = advect_scale * wet
+        speed_e, speed_n = level(east, k, rows), level(north, k, rows)
+        sea_east = jnp.where(lane == cols - 1, turn(sea_side, cols - 1 - k), turn(wet, cols - 1))
+        sea_north = jnp.where(row == rows - 1, 1.0, pltpu.roll(wet, rows - 1, 0))
+        here = level_at(k, rows)
+        for step in (1, 0):
+            zonal, merid = branches(level(flags.at[step], k, rows))
+            speed_z, speed_m = speed_e * zonal, speed_n * merid
+            out[step, 0, here, :] = part * (speed_e - speed_z + diffusion) * sea_east
+            next_west = jnp.where(
+                lane == 0, turn(sides[step], 2 * cols - step * half - k), turn(wet * (speed_z - diffusion), 1)
+            )
+            out[step, 1, here, :] = part * next_west
+            out[step, 2, here, :] = part * (speed_n - speed_m + diffusion) * sea_north
+            next_south = jnp.where(row == 0, 1.0, pltpu.roll(wet * (speed_m - diffusion), 1, 0))
+            out[step, 3, here, :] = part * next_south
+        return carry
+
+    each_level(levels, one, ())
+
+
 def project_kernel(dims, setup, ids, t, s, u, v, sea, *rest):
     levels, rows, cols, half, pair = dims
     if setup:
         inverse, coup, proj, planes, *rest = rest
-        lat_out, (spike, w_high, w_low, p_high, p_low, spike_packed, cells, wide) = rest[:-8], rest[-8:]
+        lat_out, (spike, w_high, w_low, p_high, p_low, spike_packed, corner, b_plane, cells, wide) = rest[:-10], rest[-10:]
         n = levels * rows
         for y in range(rows):
             cells[pl.ds(y, levels, stride=rows), :] = inverse[y]
@@ -151,34 +202,46 @@
             spike_packed[pl.ds(y, 1), pl.ds(0, levels)] = line
             spike_packed[pl.ds(y, 1), pl.ds(half, levels)] = line
     else:
-        coup, spike, w_high, w_low, proj, planes, *lat_out = rest
+        coup, corner, b_plane, w_high, w_low, proj, planes, *lat_out = rest
     w = (w_high[...], w_low[...])
-    for f, x in enumerate((t, s, u, v)):
-        proj[f] = dot3(w, split(x[...]))
+    for f, (x, y) in enumerate(((t, s), (u, v))):
+        both = dot3(w, split(jnp.concatenate([x[...], y[...]], axis=1)))
+        proj[2 * f] = both[:, :cols]
+        proj[2 * f + 1] = both[:, cols:]
+    edge = pl.ds(pl.multiple_of(ids[2] * rows, rows), rows)
+    zero = jnp.zeros((rows, cols), f32)
     if setup:
         n = levels * rows
         pick = (iota((n, cols), 0) // rows == ids[2]).astype(bf16)
         spike[...] = dot(w[0], pick) + dot(w[1], pick)
-    edge = pl.ds(pl.multiple_of(ids[2] * rows, rows), rows)
+        corner[...] = spike[edge, :]
     for f in range(4):
         planes[f] = proj[f, edge, :]
-    sums = [jnp.zeros((rows, cols), f32)] * 3
-    for k in range(levels):
-        here = pl.ds(k * rows, rows)
+
+    def one(k, sums):
+        here = level_at(k, rows)
         wet = sea[here, :].astype(f32)
-        sums = [
-            sums[0] + wet * proj[2, here, :],
-            sums[1] + wet * proj[3, here, :],
-            sums[2] + wet * spike[here, :],
-        ]
+        values = [wet * proj[f, here, :] for f in range(4)]
+        for f in range(4):
+            proj[f, here, :] = values[f]
+        sums = [sums[0] + values[2], sums[1] + values[3], *sums[2:]]
+        if setup:
+            value = wet * spike[here, :]
+            spike[here, :] = value
+            sums[2] = sums[2] + value
+        return tuple(sums)
+
+    sums = each_level(levels, one, (zero,) * (3 if setup else 2))
+    if setup:
+        b_plane[...] = sums[2]
+    sums = [sums[0], sums[1], b_plane[...]]
     for j in range(3):
         planes[4 + j] = sums[j]
-    corner = spike[edge, :]
     lane_row = iota((rows, cols), 0)
     coupled = jnp.zeros((rows, cols), f32)
     for y in range(rows):
         coupled = jnp.where(lane_row == y, coup[y], coupled)
-    lines = [proj[f, edge, :] for f in range(4)] + [sums[1], sums[2], corner, coupled]
+    lines = [planes[f] for f in range(4)] + [sums[1], sums[2], corner[...], coupled]
     for which, row in enumerate(row_choices(pair, rows, ids[0])):
         for j, value in enumerate(lines):
             if pair:
@@ -188,7 +251,7 @@
             lat_out[which][pl.ds(j, 1), :] = line
 
 
-def side_kernel(dims, ids, west, east, west_sea, east_sea, planes, spike, spike_packed, p_high, p_low, msg, proj):
+def side_kernel(dims, ids, west, east, west_sea, east_sea, planes, corner, spike_packed, p_high, p_low, msg, proj):
     levels, rows, cols, half, pair = dims
     lane = iota((rows, cols), 1)
     row = iota((rows, cols), 0)
@@ -217,12 +280,11 @@
                 misc = jnp.where(lane == side * 8 + 4, column, misc)
         column = jnp.sum(wet * spk, axis=1, keepdims=True)
         misc = jnp.where(lane == side * 8 + 5, column, misc)
-    corner = level(spike, edge, rows)
-    msg[7] = jnp.where(lane == CORNER_LANE, corner, misc)
+    msg[7] = jnp.where(lane == CORNER_LANE, corner[...], misc)
 
 
 def stencil_kernel(dims, step, final, ids, coup, proj, spike, spike_packed, mine, theirs, side_proj,
-                   west_const, east_const, sea, east, north, flags, *rest):
+                   west_const, east_const, coef, *rest):
     levels, rows, cols, half, pair = dims
     count = 1 if pair else 2
     row_new, row_const, row_late, row_far = (rest[i * count : (i + 1) * count] for i in range(4))
@@ -315,86 +377,65 @@
     south_v = jnp.where(row == 0, row_sum_south * has_south, pltpu.roll(sum_v, 1, 0))
     north_v = jnp.where(row == rows - 1, row_sum_north * has_north, pltpu.roll(sum_v, rows - 1, 0))
     upper = jnp.where(depth == 0, 1.0, 0.0)
-    deeper = (-0.5 * pressure_scale) * (west_u - east_u + south_v - north_v) * upper
+    deeper = (west_u - east_u + south_v - north_v) * upper
 
     north_index = (lat * rows + row).astype(f32)
     coriolis = 0.2 + 0.6 * (north_index + 0.5) / (rows * parts).astype(f32)
 
     west_sides = (sides[0], sides[1])
     east_sides = (sides[2], sides[3])
-    sea_east_side = east_const[2]
-    next_west_side = west_const[2] if step else west_const[3]
-    next_shift = half if step else 0
-
-    def some(b, carry):
+    push = -0.5 * pressure_scale * gravity
+    top, bottom = row == rows - 1, row == 0
+
+    def one(j, carry):
         below, *accs = carry
-        for i in range(BLOCK):
-            k = levels - 1 - (b * BLOCK + i)
-            wet = level(sea, k, rows).astype(f32)
-            speed_e, speed_n = level(east, k, rows), level(north, k, rows)
-            zonal_b, merid_b = branches(level(flags.at[step], k, rows))
-            east_self = wet * (speed_e * (1.0 - zonal_b) + diffusion)
-            east_next = wet * (speed_e * zonal_b - diffusion)
-            north_self = wet * (speed_n * (1.0 - merid_b) + diffusion)
-            north_next = wet * (speed_n * merid_b - diffusion)
-            one = pl.ds(k, 1)
-            sea_east = jnp.where(
-                lane == cols - 1, pltpu.roll(sea_east_side, cols - 1 - k, 1), pltpu.roll(wet, cols - 1, 1)
+        k = levels - 1 - j
+        here = level_at(k, rows)
+        one = pl.ds(k, 1)
+        east_own, west_own = coef[step, 0, here, :], coef[step, 1, here, :]
+        north_own = coef[step, 2, here, :] * jnp.where(top, north_sea[one, :], 1.0)
+        south_own = coef[step, 3, here, :] * jnp.where(bottom, south_next[one, :], 1.0)
+        spk_k = spike[here, :]
+        solved, around = [], []
+        for f in range(4):
+            w = proj[f, here, :] + spk_k * carried[f]
+            shift = (f % 2) * half
+            solved.append(w)
+            around.append(
+                shifted(
+                    w,
+                    turn(west_sides[f // 2], 2 * cols - shift - k),
+                    turn(east_sides[f // 2], 2 * cols - 1 - shift - k),
+                    south_w[f, one, :],
+                    north_w[f, one, :],
+                )
             )
-            next_west = jnp.where(
-                lane == 0, pltpu.roll(next_west_side, (cols - next_shift) - k, 1), pltpu.roll(east_next, 1, 1)
-            )
-            sea_north = jnp.where(row == rows - 1, north_sea[one, :], pltpu.roll(wet, rows - 1, 0))
-            next_south = jnp.where(row == 0, south_next[one, :], pltpu.roll(north_next, 1, 0))
-            east_own = advect_scale * east_self * sea_east
-            west_own = advect_scale * next_west * wet
-            north_own = advect_scale * north_self * sea_north
-            south_own = advect_scale * next_south * wet
-            spk_k = level(spike, k, rows)
-            solved, around = [], []
+        below = below + ((around[2][0] - around[2][1]) + (around[3][2] - around[3][3]))
+        buoyancy = push * below
+        new = []
+        for f in range(2):
+            w, (ww, we, ws, wn) = solved[f], around[f]
+            q = w + ((east_own * (we - w) + west_own * (w - ww)) + (north_own * (wn - w) + south_own * (w - ws)))
+            new.append(q + buoyancy if f == 0 else q - haline * buoyancy)
+        for f in (2, 3):
+            w, (ww, we, ws, wn) = solved[f], around[f]
+            spin = coriolis * solved[5 - f]
+            centre = (1.0 - 4.0 * viscosity) * w
+            centre = centre - spin if f == 2 else centre + spin
+            new.append(centre + viscosity * ((we + ww) + (wn + ws)))
+        for f in range(4):
+            outs[f][here, :] = new[f]
+        if not final:
             for f in range(4):
-                w = wet * (level(proj.at[f], k, rows) + spk_k * carried[f])
-                shift = (f % 2) * half
-                solved.append(w)
-                around.append(
-                    shifted(
-                        w,
-                        pltpu.roll(west_sides[f // 2], (cols - shift) - k, 1),
-                        pltpu.roll(east_sides[f // 2], (cols - 1 - shift) - k, 1),
-                        south_w[f, one, :],
-                        north_w[f, one, :],
-                    )
-                )
-            pressure = (-0.5 * pressure_scale) * (
-                around[2][0] - around[2][1] + around[3][2] - around[3][3]
-            )
-            below = below + pressure
-            buoyancy = gravity * below
-            new = []
-            for f in range(2):
-                w, (ww, we, ws, wn) = solved[f], around[f]
-                q = w + (
-                    (east_own * (we - w) + west_own * (w - ww)) + (north_own * (wn - w) + south_own * (w - ws))
-                )
-                new.append(q + buoyancy if f == 0 else q - haline * buoyancy)
-            for f in (2, 3):
-                w, (ww, we, ws, wn) = solved[f], around[f]
-                turn = -solved[3] if f == 2 else solved[2]
-                new.append(w + coriolis * turn + viscosity * ((we + ww) + (wn + ws) - 4.0 * w))
-            here = pl.ds(pl.multiple_of(k * rows, rows), rows)
-            for f in range(4):
-                outs[f][here, :] = new[f]
-            if not final:
-                for f in range(4):
-                    place = k + (f % 2) * half
-                    there = lane == place
-                    accs[f // 2] = jnp.where(there, pltpu.roll(new[f], (place + 1) % cols, 1), accs[f // 2])
-                    accs[2 + f // 2] = jnp.where(there, pltpu.roll(new[f], place % cols, 1), accs[2 + f // 2])
+                place = k + (f % 2) * half
+                there = lane == place
+                accs[f // 2] = jnp.where(there, turn(new[f], place + 1), accs[f // 2])
+                accs[2 + f // 2] = jnp.where(there, turn(new[f], place), accs[2 + f // 2])
         return (below, *accs)
 
     zero = jnp.zeros((rows, cols), f32)
     extra = () if final else (zero,) * 4
-    _, *accs = lax.fori_loop(0, levels // BLOCK, some, (deeper, *extra))
+    _, *accs = each_level(levels, one, (deeper, *extra))
     if not final:
         for p in range(2):
             to_east[p] = accs[p]
@@ -405,10 +446,9 @@
             lat_msgs[which][4] = late_out[...]
 
 
-def call(kernel, outs, args, smem=(0,), scratch=(), name=None):
-    specs = [
-        pl.BlockSpec(memory_space=pltpu.SMEM if i in smem else pltpu.VMEM) for i in range(len(args))
-    ]
+def call(kernel, outs, args, smem=(0,), scratch=(), name=None, hbm=()):
+    places = [pltpu.SMEM if i in smem else pltpu.HBM if i in hbm else pltpu.VMEM for i in range(len(args))]
+    specs = [pl.BlockSpec(memory_space=place) for place in places]
     return pl.pallas_call(
         kernel,
         out_shape=[jax.ShapeDtypeStruct(shape, kind) for shape, kind in outs],
@@ -464,12 +504,19 @@
     def to_depth(msg):
         return lax.ppermute(msg, "depth", [(d, depths - 1 - d) for d in range(depths)])
 
-    to_east, to_west, late, *lat_msgs = call(
+    sources = (*state, sea, east, north, flags, block_inverse)
+    to_east, to_west, late, *rest = call(
         functools.partial(pack_kernel, dims),
-        [((4,) + plane, f32), ((3,) + plane, f32), (grid, f32)] + [((7,) + grid, f32)] * count,
-        (ids, *state, sea, east, north, flags, block_inverse),
+        [((4,) + plane, f32), ((3,) + plane, f32), (grid, f32)]
+        + [((7,) + grid, f32)] * count
+        + [(x.shape, x.dtype) for x in sources],
+        (ids, *sources),
+        scratch=(pltpu.SemaphoreType.DMA((9,)),),
         name="pack",
+        hbm=range(1, 10),
     )
+    lat_msgs, rest = rest[:count], rest[count:]
+    state, (sea, east, north, flags, block_inverse) = rest[:4], rest[4:]
     row_const = to_lat(lat_msgs, False)
     west_const = lax.ppermute(to_east, "lon", ring)
     east_const = lax.ppermute(to_west, "lon", back)
@@ -479,12 +526,12 @@
         first = step == STEPS - 1
         outs = [((4, n, cols), f32), ((7,) + plane, f32)] + [(plane, f32)] * count
         if first:
-            outs += [((n, cols), f32)] + [((n, n), bf16)] * 2 + [((rows * cols, cols), bf16)] * 2 + [(plane, f32)]
+            outs += [((n, cols), f32)] + [((n, n), bf16)] * 2 + [((rows * cols, cols), bf16)] * 2 + [(plane, f32)] * 3
             args = (ids, *state, sea, block_inverse, coupling)
             smem = (0, 7)
             scratch = (pltpu.VMEM((n, levels), f32), pltpu.VMEM((rows, cols, cols), f32))
         else:
-            args = (ids, *state, sea, coupling, spike, w_high, w_low)
+            args = (ids, *state, sea, coupling, corner, b_plane, w_high, w_low)
             smem = (0, 6)
             scratch = ()
         proj, planes, *more = call(
@@ -492,15 +539,23 @@
         )
         far_msgs = more[:count]
         if first:
-            spike, w_high, w_low, p_high, p_low, spike_packed = more[count:]
+            spike, w_high, w_low, p_high, p_low, spike_packed, corner, b_plane = more[count:]
         row_far = to_lat(far_msgs, True)
         mine, side_proj = call(
             functools.partial(side_kernel, dims),
             [((8,) + plane, f32), ((4,) + plane, f32)],
-            (ids, west, east_in, west_const, east_const, planes, spike, spike_packed, p_high, p_low),
+            (ids, west, east_in, west_const, east_const, planes, corner, spike_packed, p_high, p_low),
             name="sides",
         )
         theirs = to_depth(mine)
+        if first:
+            (coef,) = call(
+                functools.partial(coef_kernel, dims),
+                [((STEPS, 4, n, cols), f32)],
+                (sea, east, north, flags, west_const, east_const),
+                (),
+                name="coef",
+            )
         final = step == 0
         state_shape = [((n, cols), f32)] * 4
         if final:
@@ -513,7 +568,7 @@
             outs,
             (
                 ids, coupling, proj, spike, spike_packed, mine, theirs, side_proj, west_const, east_const,
-                sea, east, north, flags, *row_new, *row_const, *row_new, *row_far, *extra,
+                coef, *row_new, *row_const, *row_new, *row_far, *extra,
             ),
             (0, 1),
             (

time: 47.4 us -> 48 us (1.013)
  Pallas kernels: 14.9 us -> 16 us
  waiting for transfers between devices: 7.35 us -> 6.86 us
    pallas_call x7 -> x8, Pallas kernels: 14.9 us -> 16 us  [call(): pl.pallas_call(kernel, out_shape=[jax.ShapeDtypeStruct(shape, kind) for s...]
    ppermute x2, waiting for transfers between devices: 7.33 us -> 6.83 us  [to_lat(): return [lax.ppermute(m, ('lat', 'depth'), r) for m, r in zip(msgs, both)]]
    unnamed x28 -> x20, local copies, waits for them, and re-layouts: 8.43 us -> 8.41 us
  transfers between devices with their start and end apart: 10 -> 10, of which waited for: 2 -> 2; matrix products, arithmetic and copies ran while one was open for 0% -> 0% of each run, Pallas kernels for 12% -> 11%
where the time goes in v3:
time: 48 us; the launch traced here: 47.7 us
  Pallas kernels  16 us (33%)
  starting transfers between devices  15.6 us (32%)
  local copies, waits for them, and re-layouts  8.41 us (18%)
  waiting for transfers between devices  6.86 us (14%)
  between operations  0.75 us (2%)
    pallas_call x8, Pallas kernels, call(): pl.pallas_call(kernel, out_shape=[jax.ShapeDtypeStruct(shape, kind) for s...  16 us
    unnamed x20, local copies, waits for them, and re-layouts  8.41 us
    ppermute x2, waiting for transfers between devices, to_lat(): return [lax.ppermute(m, ('lat', 'depth'), r) for m, r in zip(msgs, both)]  6.83 us
    ppermute x2, starting transfers between devices, to_lat(): return [lax.ppermute(m, 'lat', r) for m, r in zip(msgs, routes)]  4.2 us
    ppermute x2, starting transfers between devices, to_lat(): return [lax.ppermute(m, ('lat', 'depth'), r) for m, r in zip(msgs, both)]  3.47 us
    ppermute x1, starting transfers between devices, on_device(): east_const = lax.ppermute(to_west, 'lon', back)  2.64 us
    ppermute x1, starting transfers between devices, on_device(): east_in = lax.ppermute(result[5], 'lon', back)  2.63 us
    ppermute x2, starting transfers between devices, to_depth(): lax.ppermute(msg, 'depth', [(d, depths - 1 - d) for d in range(depths)])  2.56 us
  transfers between devices with their start and end apart: 10, of which 2 were waited for; matrix products, arithmetic and copies ran while one was open for 0% of the time, Pallas kernels for 11%

profile of v3, /device:TPU:0, one launch (start us, length us, event | category | flops | bytes accessed | tf_op | source)
XLA Modules:
  0.0 47.7 jit_solution(11350658292376434341)
XLA Ops:
  0.6 0.0 copy-start.9
  0.6 0.1 pad_add_fusion.ids
  0.7 0.0 copy-start
  0.7 1.0 %copy-done = s32[2,48,8,128]{3,2,1,0:T(8,128)S(1)} copy-done((s32[2,48,8,128]{3,2,1,0:T(8,128)S(1)}, s32[2,48,8,128]{3,2,1,0:T(8,128)}, u32[]{:S(2)}) %copy-start) | copy-done | bytes 393240
  1.7 0.0 copy-start.1
  1.7 0.9 %copy-done.1 = f32[48,8,128]{2,1,0:T(8,128)S(1)} copy-done((f32[48,8,128]{2,1,0:T(8,128)S(1)}, f32[48,8,128]{2,1,0:T(8,128)}, u32[]{:S(2)}) %copy-start.1) | copy-done | bytes 196632
  2.6 0.0 copy-start.2
  2.7 0.9 %copy-done.2 = f32[48,8,128]{2,1,0:T(8,128)S(1)} copy-done((f32[48,8,128]{2,1,0:T(8,128)S(1)}, f32[48,8,128]{2,1,0:T(8,128)}, u32[]{:S(2)}) %copy-start.2) | copy-done | bytes 196632
  3.6 0.0 copy-start.3
  3.6 0.9 %copy-done.3 = f32[48,8,128]{2,1,0:T(8,128)S(1)} copy-done((f32[48,8,128]{2,1,0:T(8,128)S(1)}, f32[48,8,128]{2,1,0:T(8,128)}, u32[]{:S(2)}) %copy-start.3) | copy-done | bytes 196632
  4.5 0.0 copy-start.4
  4.5 0.9 %copy-done.4 = f32[48,8,128]{2,1,0:T(8,128)S(1)} copy-done((f32[48,8,128]{2,1,0:T(8,128)S(1)}, f32[48,8,128]{2,1,0:T(8,128)}, u32[]{:S(2)}) %copy-start.4) | copy-done | bytes 196632
  5.4 0.0 copy-start.5
  5.4 0.9 %copy-done.5 = s32[48,8,128]{2,1,0:T(8,128)S(1)} copy-done((s32[48,8,128]{2,1,0:T(8,128)S(1)}, s32[48,8,128]{2,1,0:T(8,128)}, u32[]{:S(2)}) %copy-start.5) | copy-done | bytes 196632
  6.4 0.0 copy-start.6
  6.4 0.9 %copy-done.6 = f32[48,8,128]{2,1,0:T(8,128)S(1)} copy-done((f32[48,8,128]{2,1,0:T(8,128)S(1)}, f32[48,8,128]{2,1,0:T(8,128)}, u32[]{:S(2)}) %copy-start.6) | copy-done | bytes 196632
  7.3 0.0 copy-start.7
  7.3 0.9 %copy-done.7 = f32[48,8,128]{2,1,0:T(8,128)S(1)} copy-done((f32[48,8,128]{2,1,0:T(8,128)S(1)}, f32[48,8,128]{2,1,0:T(8,128)}, u32[]{:S(2)}) %copy-start.7) | copy-done | bytes 196632
  8.2 0.0 copy-start.8
  8.2 0.9 %copy-done.8 = f32[8,48,48]{2,1,0:T(8,128)S(1)} copy-done((f32[8,48,48]{2,1,0:T(8,128)S(1)}, f32[8,48,48]{2,1,0:T(8,128)}, u32[]{:S(2)}) %copy-start.8) | copy-done | bytes 73752
  9.1 3.9 %pack.1 = (f32[4,8,128]{2,1,0:T(8,128)S(1)}, f32[3,8,128]{2,1,0:T(8,128)S(1)}, f32[48,128]{1,0:T(8,128)S(1)}, f32[7,48,128]{2,1,0:T(8,128)S(1)}, f32[384,128]{1,...) custom-call(s32[4]{0:T(128)S(1)} %pad_add_fusion.ids, ...), custom_call_target="tpu_custom_call" | custom-call | tf_op jit(solution)/shard_map/pack/pallas_call | solution.py:452
  13.1 4.1 %collective-permute-start.3 = (f32[7,48,128]{2,1,0:T(8,128)S(1)}, f32[7,48,128]{2,1,0:T(8,128)S(1)}, u32[]{:S(2)}, u32[]{:S(2)}) collective-permute-start(f32[7,48,128]{2,1,0:T(8,128)S(1)} %get-tuple-element.66), channel_id=1, source_target_pairs={{0,2},{2,0},{1,3},{3,1},{4,6},{6,4},{5,7},{7,5},{8,10},{10,8},{9,1... | collective-permute-start | bytes 516104 | tf_op jit(solution)/shard_map/ppermute | solution.py:498
  17.2 0.0 collective-permute-start
  17.2 2.6 %collective-permute-start.1 = (f32[3,8,128]{2,1,0:T(8,128)S(1)}, f32[3,8,128]{2,1,0:T(8,128)S(1)}, u32[]{:S(2)}, u32[]{:S(2)}) collective-permute-start(f32[3,8,128]{2,1,0:T(8,128)S(1)} %get-tuple-element.56), channel_id=1, source_target_pairs={{4,0},{8,4},{12,8},{16,12},{20,16},{24,20},{28,24},{0,28},{5,1},{9... | collective-permute-start | bytes 36872 | tf_op jit(solution)/shard_map/ppermute | solution.py:522
  19.8 0.0 copy-done.9
  19.8 1.9 %project.2 = (f32[4,384,128]{2,1,0:T(8,128)S(1)}, f32[7,8,128]{2,1,0:T(8,128)S(1)}, f32[8,128]{1,0:T(8,128)S(1)}, f32[384,128]{1,0:T(8,128)S(1)}, bf16[384,384]{...) custom-call(s32[4]{0:T(128)S(1)} %pad_add_fusion.ids, ...), custom_call_target="tpu_custom_call" | custom-call | tf_op jit(solution)/shard_map/project/pallas_call | solution.py:452
  21.7 0.0 collective-permute-done.1.east.east_sea.east_const
  21.7 0.0 collective-permute-done.west.west_sea.west_const
  21.7 0.9 %sides.2 = (f32[8,8,128]{2,1,0:T(8,128)S(1)}, f32[4,8,128]{2,1,0:T(8,128)S(1)}) custom-call(s32[4]{0:T(128)S(1)} %pad_add_fusion.ids, f32[4,8,128]{2,1,0:T(8,128)S(1)} %collective-permute-done.west.west_sea.west_const, f32[3,8,128]{2,1,0:T(8,128)S(1)} %collective-permute-done.1.east.east_sea.east_const, ...), custom_call_target="tpu_custom_call" | custom-call | tf_op jit(solution)/shard_map/sides/pallas_call | solution.py:452
  22.6 1.6 %collective-permute-start.2 = (f32[8,8,128]{2,1,0:T(8,128)S(1)}, f32[8,8,128]{2,1,0:T(8,128)S(1)}, u32[]{:S(2)}, u32[]{:S(2)}) collective-permute-start(f32[8,8,128]{2,1,0:T(8,128)S(1)} %get-tuple-element.61.mine), channel_id=1, source_target_pairs={{0,1},{1,0},{2,3},{3,2},{4,5},{5,4},{6,7},{7,6},{8,9},{9,8},{10,11... | collective-permute-start | bytes 98312 | tf_op jit(solution)/shard_map/ppermute | solution.py:505
  24.2 0.0 collective-permute-start.4
  24.2 0.5 %coef.1 = f32[2,4,384,128]{3,2,1,0:T(8,128)S(1)} custom-call(s32[384,128]{1,0:T(8,128)S(1)} %get-tuple-element.50.sea, f32[384,128]{1,0:T(8,128)S(1)} %get-tuple-element.63.east, f32[384,128]{1,0:T(8,128)S(1)} %get-tuple-element.64.north, s32[2,384,128]{2,1,0:T(8,128)S(1)} %get-tuple-element.65.flags, ...), custom_call_target="tpu_custom_call" | custom-call | tf_op jit(solution)/shard_map/coef/pallas_call | solution.py:452
  24.7 4.9 %collective-permute-done.4.rest_3_ = f32[8,128]{1,0:T(8,128)S(1)} collective-permute-done((f32[8,128]{1,0:T(8,128)S(1)}, f32[8,128]{1,0:T(8,128)S(1)}, u32[]{:S(2)}, u32[]{:S(2)}) %collective-permute-start.4) | collective-permute-done | bytes 4128 | tf_op jit(solution)/shard_map/ppermute | solution.py:502
  29.6 0.0 collective-permute-done.2.theirs
  29.6 0.0 collective-permute-done.3.rest_0_.rest_1_.rest_2_
  29.6 4.1 %stencil.2 = (f32[384,128]{1,0:T(8,128)S(1)}, f32[384,128]{1,0:T(8,128)S(1)}, f32[384,128]{1,0:T(8,128)S(1)}, f32[384,128]{1,0:T(8,128)S(1)}, f32[2,8,128]{2,1,0...) custom-call(s32[4]{0:T(128)S(1)} %pad_add_fusion.ids, f32[8]{0:T(128)S(1)} %copy-done.9, ...), custom_call_target="tpu_custom_call" | custom-call | tf_op jit(solution)/shard_map/stencil/pallas_call | solution.py:452
  33.8 0.1 collective-permute-start.8
  33.9 0.1 collective-permute-start.5
  33.9 2.6 %collective-permute-start.6 = (f32[2,8,128]{2,1,0:T(8,128)S(1)}, f32[2,8,128]{2,1,0:T(8,128)S(1)}, u32[]{:S(2)}, u32[]{:S(2)}) collective-permute-start(f32[2,8,128]{2,1,0:T(8,128)S(1)} %get-tuple-element.78), channel_id=1, source_target_pairs={{4,0},{8,4},{12,8},{16,12},{20,16},{24,20},{28,24},{0,28},{5,1},{9... | collective-permute-start | bytes 24584 | tf_op jit(solution)/shard_map/ppermute | solution.py:588
  36.5 1.4 %project.3 = (f32[4,384,128]{2,1,0:T(8,128)S(1)}, f32[7,8,128]{2,1,0:T(8,128)S(1)}, f32[8,128]{1,0:T(8,128)S(1)}) custom-call(s32[4]{0:T(128)S(1)} %pad_add_fusion.ids, f32[384,128]{1,0:T(8,128)S(1)} %get-tuple-element.69.t, f32[384,128]{1,0:T(8,128)S(1)} %get-tuple-element.70.s, f32[384,128]{1,0:T(8,128)S(1)} %get-tuple-element.71.u, ...), custom_call_target="tpu_custom_call" | custom-call | tf_op jit(solution)/shard_map/project/pallas_call | solution.py:452
  38.0 0.0 collective-permute-done.5.west
  38.0 0.0 collective-permute-done.6.east
  38.0 0.9 %sides.3 = (f32[8,8,128]{2,1,0:T(8,128)S(1)}, f32[4,8,128]{2,1,0:T(8,128)S(1)}) custom-call(s32[4]{0:T(128)S(1)} %pad_add_fusion.ids, f32[2,8,128]{2,1,0:T(8,128)S(1)} %collective-permute-done.5.west, f32[2,8,128]{2,1,0:T(8,128)S(1)} %collective-permute-done.6.east, f32[4,8,128]{2,1,0:T(8,128)S(1)} %collective-permute-done.west.west_sea.west_const, ...), custom_call_target="tpu_custom_call" | custom-call | tf_op jit(solution)/shard_map/sides/pallas_call | solution.py:452
  38.8 0.9 %collective-permute-start.7 = (f32[8,8,128]{2,1,0:T(8,128)S(1)}, f32[8,8,128]{2,1,0:T(8,128)S(1)}, u32[]{:S(2)}, u32[]{:S(2)}) collective-permute-start(f32[8,8,128]{2,1,0:T(8,128)S(1)} %get-tuple-element.80.mine), channel_id=1, source_target_pairs={{0,1},{1,0},{2,3},{3,2},{4,5},{5,4},{6,7},{7,6},{8,9},{9,8},{10,11... | collective-permute-start | bytes 98312 | tf_op jit(solution)/shard_map/ppermute | solution.py:505
  39.8 3.5 %collective-permute-start.9 = (f32[8,128]{1,0:T(8,128)S(1)}, f32[8,128]{1,0:T(8,128)S(1)}, u32[]{:S(2)}, u32[]{:S(2)}) collective-permute-start(f32[8,128]{1,0:T(8,128)S(1)} %get-tuple-element.83), channel_id=1, source_target_pairs={{0,3},{1,2},{2,1},{3,0},{4,7},{5,6},{6,5},{7,4},{8,11},{9,10},{10,... | collective-permute-start | bytes 12296 | tf_op jit(solution)/shard_map/ppermute | solution.py:502
  43.2 1.9 %collective-permute-done.9.rest_3_ = f32[8,128]{1,0:T(8,128)S(1)} collective-permute-done((f32[8,128]{1,0:T(8,128)S(1)}, f32[8,128]{1,0:T(8,128)S(1)}, u32[]{:S(2)}, u32[]{:S(2)}) %collective-permute-start.9) | collective-permute-done | bytes 4128 | tf_op jit(solution)/shard_map/ppermute | solution.py:502
  45.2 0.0 collective-permute-done.7.theirs
  45.2 0.0 collective-permute-done.8.rest_0_.rest_2_
  45.2 2.5 %stencil.3 = (f32[384,128]{1,0:T(8,128)}, f32[384,128]{1,0:T(8,128)}, f32[384,128]{1,0:T(8,128)}, f32[384,128]{1,0:T(8,128)}) custom-call(s32[4]{0:T(128)S(1)} %pad_add_fusion.ids, f32[8]{0:T(128)S(1)} %copy-done.9, f32[4,384,128]{2,1,0:T(8,128)S(1)} %get-tuple-element.76.proj, f32[384,128]{1,0:T(8,128)S(1)} %get-tuple-element.53.spike, ...), custom_call_target="tpu_custom_call" | custom-call | tf_op jit(solution)/shard_map/stencil/pallas_call | solution.py:452
Async XLA Ops:
  0.6 19.2 %copy-start.9 = (f32[8]{0:T(128)S(1)}, f32[8]{0:T(128)}, u32[]{:S(2)}) copy-start(f32[8]{0:T(128)} %coup.3) | copy-start | bytes 100
  0.7 1.0 %copy-start = (s32[2,48,8,128]{3,2,1,0:T(8,128)S(1)}, s32[2,48,8,128]{3,2,1,0:T(8,128)}, u32[]{:S(2)}) copy-start(s32[2,48,8,128]{3,2,1,0:T(8,128)} %param.16) | copy-start | bytes 1179652
  1.7 0.9 %copy-start.1 = (f32[48,8,128]{2,1,0:T(8,128)S(1)}, f32[48,8,128]{2,1,0:T(8,128)}, u32[]{:S(2)}) copy-start(f32[48,8,128]{2,1,0:T(8,128)} %param.10) | copy-start | bytes 589828
  2.6 0.9 %copy-start.2 = (f32[48,8,128]{2,1,0:T(8,128)S(1)}, f32[48,8,128]{2,1,0:T(8,128)}, u32[]{:S(2)}) copy-start(f32[48,8,128]{2,1,0:T(8,128)} %param.11) | copy-start | bytes 589828
  3.6 0.9 %copy-start.3 = (f32[48,8,128]{2,1,0:T(8,128)S(1)}, f32[48,8,128]{2,1,0:T(8,128)}, u32[]{:S(2)}) copy-start(f32[48,8,128]{2,1,0:T(8,128)} %param.12) | copy-start | bytes 589828
  4.5 0.9 %copy-start.4 = (f32[48,8,128]{2,1,0:T(8,128)S(1)}, f32[48,8,128]{2,1,0:T(8,128)}, u32[]{:S(2)}) copy-start(f32[48,8,128]{2,1,0:T(8,128)} %param.13) | copy-start | bytes 589828
  5.4 0.9 %copy-start.5 = (s32[48,8,128]{2,1,0:T(8,128)S(1)}, s32[48,8,128]{2,1,0:T(8,128)}, u32[]{:S(2)}) copy-start(s32[48,8,128]{2,1,0:T(8,128)} %param.17) | copy-start | bytes 589828
  6.4 0.9 %copy-start.6 = (f32[48,8,128]{2,1,0:T(8,128)S(1)}, f32[48,8,128]{2,1,0:T(8,128)}, u32[]{:S(2)}) copy-start(f32[48,8,128]{2,1,0:T(8,128)} %param.14) | copy-start | bytes 589828
  7.3 0.9 %copy-start.7 = (f32[48,8,128]{2,1,0:T(8,128)S(1)}, f32[48,8,128]{2,1,0:T(8,128)}, u32[]{:S(2)}) copy-start(f32[48,8,128]{2,1,0:T(8,128)} %param.15) | copy-start | bytes 589828
  8.2 0.9 %copy-start.8 = (f32[8,48,48]{2,1,0:T(8,128)S(1)}, f32[8,48,48]{2,1,0:T(8,128)}, u32[]{:S(2)}) copy-start(f32[8,48,48]{2,1,0:T(8,128)} %refs_8_.1) | copy-start | bytes 221188
  13.1 16.6 %collective-permute-start.3 = (f32[7,48,128]{2,1,0:T(8,128)S(1)}, f32[7,48,128]{2,1,0:T(8,128)S(1)}, u32[]{:S(2)}, u32[]{:S(2)}) collective-permute-start(f32[7,48,128]{2,1,0:T(8,128)S(1)} %get-tuple-element.66), channel_id=1, source_target_pairs={{0,2},{2,0},{1,3},{3,1},{4,6},{6,4},{5,7},{7,5},{8,10},{10,8},{9,1... | collective-permute-start | bytes 516104 | tf_op jit(solution)/shard_map/ppermute | solution.py:498
  17.2 4.5 %collective-permute-start = (f32[4,8,128]{2,1,0:T(8,128)S(1)}, f32[4,8,128]{2,1,0:T(8,128)S(1)}, u32[]{:S(2)}, u32[]{:S(2)}) collective-permute-start(f32[4,8,128]{2,1,0:T(8,128)S(1)} %get-tuple-element.55), channel_id=1, source_target_pairs={{0,4},{4,8},{8,12},{12,16},{16,20},{20,24},{24,28},{28,0},{1,5},{5... | collective-permute-start | bytes 49160 | tf_op jit(solution)/shard_map/ppermute | solution.py:521
  17.2 4.5 %collective-permute-start.1 = (f32[3,8,128]{2,1,0:T(8,128)S(1)}, f32[3,8,128]{2,1,0:T(8,128)S(1)}, u32[]{:S(2)}, u32[]{:S(2)}) collective-permute-start(f32[3,8,128]{2,1,0:T(8,128)S(1)} %get-tuple-element.56), channel_id=1, source_target_pairs={{4,0},{8,4},{12,8},{16,12},{20,16},{24,20},{28,24},{0,28},{5,1},{9... | collective-permute-start | bytes 36872 | tf_op jit(solution)/shard_map/ppermute | solution.py:522
  22.6 7.0 %collective-permute-start.2 = (f32[8,8,128]{2,1,0:T(8,128)S(1)}, f32[8,8,128]{2,1,0:T(8,128)S(1)}, u32[]{:S(2)}, u32[]{:S(2)}) collective-permute-start(f32[8,8,128]{2,1,0:T(8,128)S(1)} %get-tuple-element.61.mine), channel_id=1, source_target_pairs={{0,1},{1,0},{2,3},{3,2},{4,5},{5,4},{6,7},{7,6},{8,9},{9,8},{10,11... | collective-permute-start | bytes 98312 | tf_op jit(solution)/shard_map/ppermute | solution.py:505
  24.2 5.4 %collective-permute-start.4 = (f32[8,128]{1,0:T(8,128)S(1)}, f32[8,128]{1,0:T(8,128)S(1)}, u32[]{:S(2)}, u32[]{:S(2)}) collective-permute-start(f32[8,128]{1,0:T(8,128)S(1)} %get-tuple-element.67), channel_id=1, source_target_pairs={{0,3},{1,2},{2,1},{3,0},{4,7},{5,6},{6,5},{7,4},{8,11},{9,10},{10,... | collective-permute-start | bytes 12296 | tf_op jit(solution)/shard_map/ppermute | solution.py:502
  33.8 11.4 %collective-permute-start.8 = (f32[5,48,128]{2,1,0:T(8,128)S(1)}, f32[5,48,128]{2,1,0:T(8,128)S(1)}, u32[]{:S(2)}, u32[]{:S(2)}) collective-permute-start(f32[5,48,128]{2,1,0:T(8,128)S(1)} %get-tuple-element.82), channel_id=1, source_target_pairs={{0,2},{2,0},{1,3},{3,1},{4,6},{6,4},{5,7},{7,5},{8,10},{10,8},{9,1... | collective-permute-start | bytes 368648 | tf_op jit(solution)/shard_map/ppermute | solution.py:498
  33.9 4.1 %collective-permute-start.5 = (f32[2,8,128]{2,1,0:T(8,128)S(1)}, f32[2,8,128]{2,1,0:T(8,128)S(1)}, u32[]{:S(2)}, u32[]{:S(2)}) collective-permute-start(f32[2,8,128]{2,1,0:T(8,128)S(1)} %get-tuple-element.77), channel_id=1, source_target_pairs={{0,4},{4,8},{8,12},{12,16},{16,20},{20,24},{24,28},{28,0},{1,5},{5... | collective-permute-start | bytes 24584 | tf_op jit(solution)/shard_map/ppermute | solution.py:587
  33.9 4.1 %collective-permute-start.6 = (f32[2,8,128]{2,1,0:T(8,128)S(1)}, f32[2,8,128]{2,1,0:T(8,128)S(1)}, u32[]{:S(2)}, u32[]{:S(2)}) collective-permute-start(f32[2,8,128]{2,1,0:T(8,128)S(1)} %get-tuple-element.78), channel_id=1, source_target_pairs={{4,0},{8,4},{12,8},{16,12},{20,16},{24,20},{28,24},{0,28},{5,1},{9... | collective-permute-start | bytes 24584 | tf_op jit(solution)/shard_map/ppermute | solution.py:588
  38.8 6.3 %collective-permute-start.7 = (f32[8,8,128]{2,1,0:T(8,128)S(1)}, f32[8,8,128]{2,1,0:T(8,128)S(1)}, u32[]{:S(2)}, u32[]{:S(2)}) collective-permute-start(f32[8,8,128]{2,1,0:T(8,128)S(1)} %get-tuple-element.80.mine), channel_id=1, source_target_pairs={{0,1},{1,0},{2,3},{3,2},{4,5},{5,4},{6,7},{7,6},{8,9},{9,8},{10,11... | collective-permute-start | bytes 98312 | tf_op jit(solution)/shard_map/ppermute | solution.py:505
  39.8 5.4 %collective-permute-start.9 = (f32[8,128]{1,0:T(8,128)S(1)}, f32[8,128]{1,0:T(8,128)S(1)}, u32[]{:S(2)}, u32[]{:S(2)}) collective-permute-start(f32[8,128]{1,0:T(8,128)S(1)} %get-tuple-element.83), channel_id=1, source_target_pairs={{0,3},{1,2},{2,1},{3,0},{4,7},{5,6},{6,5},{7,4},{8,11},{9,10},{10,... | collective-permute-start | bytes 12296 | tf_op jit(solution)/shard_map/ppermute | solution.py:502

commit v4 on v3

--- a/solution.py
+++ b/solution.py
@@ -505,6 +505,7 @@
         return lax.ppermute(msg, "depth", [(d, depths - 1 - d) for d in range(depths)])
 
     sources = (*state, sea, east, north, flags, block_inverse)
+    sources = tuple(pltpu.with_memory_space_constraint(x, pltpu.HBM) for x in sources)
     to_east, to_west, late, *rest = call(
         functools.partial(pack_kernel, dims),
         [((4,) + plane, f32), ((3,) + plane, f32), (grid, f32)]

time: 48 us -> 38.4 us (0.80)
  local copies, waits for them, and re-layouts: 8.41 us -> 0.01 us
  Pallas kernels: 16 us -> 15 us
    unnamed x20 -> x2, local copies, waits for them, and re-layouts: 8.41 us -> 0.01 us
    pallas_call x8, Pallas kernels: 16 us -> 15 us  [call(): pl.pallas_call(kernel, out_shape=[jax.ShapeDtypeStruct(shape, kind) for s...]
  transfers between devices with their start and end apart: 10 -> 10, of which waited for: 2 -> 2; matrix products, arithmetic and copies ran while one was open for 0% -> 0% of each run, Pallas kernels for 11% -> 14%
where the time goes in v4:
time: 38.4 us; the launch traced here: 38.3 us
  starting transfers between devices  15.6 us (41%)
  Pallas kernels  15 us (39%)
  waiting for transfers between devices  6.86 us (18%)
  between operations  0.74 us (2%)
    pallas_call x8, Pallas kernels, call(): pl.pallas_call(kernel, out_shape=[jax.ShapeDtypeStruct(shape, kind) for s...  15 us
    ppermute x2, waiting for transfers between devices, to_lat(): return [lax.ppermute(m, ('lat', 'depth'), r) for m, r in zip(msgs, both)]  6.84 us
    ppermute x2, starting transfers between devices, to_lat(): return [lax.ppermute(m, 'lat', r) for m, r in zip(msgs, routes)]  4.2 us
    ppermute x2, starting transfers between devices, to_lat(): return [lax.ppermute(m, ('lat', 'depth'), r) for m, r in zip(msgs, both)]  3.47 us
    ppermute x1, starting transfers between devices, on_device(): east_const = lax.ppermute(to_west, 'lon', back)  2.64 us
    ppermute x1, starting transfers between devices, on_device(): east_in = lax.ppermute(result[5], 'lon', back)  2.63 us
    ppermute x2, starting transfers between devices, to_depth(): lax.ppermute(msg, 'depth', [(d, depths - 1 - d) for d in range(depths)])  2.56 us
  transfers between devices with their start and end apart: 10, of which 2 were waited for; matrix products, arithmetic and copies ran while one was open for 0% of the time, Pallas kernels for 14%

profile of v4, /device:TPU:0, one launch (start us, length us, event | category | flops | bytes accessed | tf_op | source)
XLA Modules:
  0.0 38.3 jit_solution(10236738689111441421)
XLA Ops:
  0.6 0.0 copy-start
  0.6 0.1 pad_add_fusion.ids
  0.7 3.0 %pack.1 = (f32[4,8,128]{2,1,0:T(8,128)S(1)}, f32[3,8,128]{2,1,0:T(8,128)S(1)}, f32[48,128]{1,0:T(8,128)S(1)}, f32[7,48,128]{2,1,0:T(8,128)S(1)}, f32[384,128]{1,...) custom-call(s32[4]{0:T(128)S(1)} %pad_add_fusion.ids, ...), custom_call_target="tpu_custom_call" | custom-call | tf_op jit(solution)/shard_map/pack/pallas_call | solution.py:452
  3.7 4.1 %collective-permute-start.3 = (f32[7,48,128]{2,1,0:T(8,128)S(1)}, f32[7,48,128]{2,1,0:T(8,128)S(1)}, u32[]{:S(2)}, u32[]{:S(2)}) collective-permute-start(f32[7,48,128]{2,1,0:T(8,128)S(1)} %get-tuple-element.66), channel_id=1, source_target_pairs={{0,2},{2,0},{1,3},{3,1},{4,6},{6,4},{5,7},{7,5},{8,10},{10,8},{9,1... | collective-permute-start | bytes 516104 | tf_op jit(solution)/shard_map/ppermute | solution.py:498
  7.8 0.0 collective-permute-start
  7.8 2.6 %collective-permute-start.1 = (f32[3,8,128]{2,1,0:T(8,128)S(1)}, f32[3,8,128]{2,1,0:T(8,128)S(1)}, u32[]{:S(2)}, u32[]{:S(2)}) collective-permute-start(f32[3,8,128]{2,1,0:T(8,128)S(1)} %get-tuple-element.56), channel_id=1, source_target_pairs={{4,0},{8,4},{12,8},{16,12},{20,16},{24,20},{28,24},{0,28},{5,1},{9... | collective-permute-start | bytes 36872 | tf_op jit(solution)/shard_map/ppermute | solution.py:523
  10.5 0.0 copy-done
  10.5 1.8 %project.2 = (f32[4,384,128]{2,1,0:T(8,128)S(1)}, f32[7,8,128]{2,1,0:T(8,128)S(1)}, f32[8,128]{1,0:T(8,128)S(1)}, f32[384,128]{1,0:T(8,128)S(1)}, bf16[384,384]{...) custom-call(s32[4]{0:T(128)S(1)} %pad_add_fusion.ids, ...), custom_call_target="tpu_custom_call" | custom-call | tf_op jit(solution)/shard_map/project/pallas_call | solution.py:452
  12.3 0.0 collective-permute-done.1.east.east_sea.east_const
  12.3 0.0 collective-permute-done.west.west_sea.west_const
  12.4 0.9 %sides.2 = (f32[8,8,128]{2,1,0:T(8,128)S(1)}, f32[4,8,128]{2,1,0:T(8,128)S(1)}) custom-call(s32[4]{0:T(128)S(1)} %pad_add_fusion.ids, f32[4,8,128]{2,1,0:T(8,128)S(1)} %collective-permute-done.west.west_sea.west_const, f32[3,8,128]{2,1,0:T(8,128)S(1)} %collective-permute-done.1.east.east_sea.east_const, ...), custom_call_target="tpu_custom_call" | custom-call | tf_op jit(solution)/shard_map/sides/pallas_call | solution.py:452
  13.2 1.6 %collective-permute-start.2 = (f32[8,8,128]{2,1,0:T(8,128)S(1)}, f32[8,8,128]{2,1,0:T(8,128)S(1)}, u32[]{:S(2)}, u32[]{:S(2)}) collective-permute-start(f32[8,8,128]{2,1,0:T(8,128)S(1)} %get-tuple-element.61.mine), channel_id=1, source_target_pairs={{0,1},{1,0},{2,3},{3,2},{4,5},{5,4},{6,7},{7,6},{8,9},{9,8},{10,11... | collective-permute-start | bytes 98312 | tf_op jit(solution)/shard_map/ppermute | solution.py:505
  14.9 0.0 collective-permute-start.4
  14.9 0.5 %coef.1 = f32[2,4,384,128]{3,2,1,0:T(8,128)S(1)} custom-call(s32[384,128]{1,0:T(8,128)S(1)} %get-tuple-element.50.sea, f32[384,128]{1,0:T(8,128)S(1)} %get-tuple-element.63.east, f32[384,128]{1,0:T(8,128)S(1)} %get-tuple-element.64.north, s32[2,384,128]{2,1,0:T(8,128)S(1)} %get-tuple-element.65.flags, ...), custom_call_target="tpu_custom_call" | custom-call | tf_op jit(solution)/shard_map/coef/pallas_call | solution.py:452
  15.4 4.9 %collective-permute-done.4.rest_3_ = f32[8,128]{1,0:T(8,128)S(1)} collective-permute-done((f32[8,128]{1,0:T(8,128)S(1)}, f32[8,128]{1,0:T(8,128)S(1)}, u32[]{:S(2)}, u32[]{:S(2)}) %collective-permute-start.4) | collective-permute-done | bytes 4128 | tf_op jit(solution)/shard_map/ppermute | solution.py:502
  20.3 0.0 collective-permute-done.2.theirs
  20.3 0.0 collective-permute-done.3.rest_0_.rest_1_.rest_2_
  20.3 4.1 %stencil.2 = (f32[384,128]{1,0:T(8,128)S(1)}, f32[384,128]{1,0:T(8,128)S(1)}, f32[384,128]{1,0:T(8,128)S(1)}, f32[384,128]{1,0:T(8,128)S(1)}, f32[2,8,128]{2,1,0...) custom-call(s32[4]{0:T(128)S(1)} %pad_add_fusion.ids, f32[8]{0:T(128)S(1)} %copy-done, ...), custom_call_target="tpu_custom_call" | custom-call | tf_op jit(solution)/shard_map/stencil/pallas_call | solution.py:452
  24.4 0.1 collective-permute-start.8
  24.5 0.1 collective-permute-start.5
  24.5 2.6 %collective-permute-start.6 = (f32[2,8,128]{2,1,0:T(8,128)S(1)}, f32[2,8,128]{2,1,0:T(8,128)S(1)}, u32[]{:S(2)}, u32[]{:S(2)}) collective-permute-start(f32[2,8,128]{2,1,0:T(8,128)S(1)} %get-tuple-element.78), channel_id=1, source_target_pairs={{4,0},{8,4},{12,8},{16,12},{20,16},{24,20},{28,24},{0,28},{5,1},{9... | collective-permute-start | bytes 24584 | tf_op jit(solution)/shard_map/ppermute | solution.py:589
  27.2 1.4 %project.3 = (f32[4,384,128]{2,1,0:T(8,128)S(1)}, f32[7,8,128]{2,1,0:T(8,128)S(1)}, f32[8,128]{1,0:T(8,128)S(1)}) custom-call(s32[4]{0:T(128)S(1)} %pad_add_fusion.ids, f32[384,128]{1,0:T(8,128)S(1)} %get-tuple-element.69.t, f32[384,128]{1,0:T(8,128)S(1)} %get-tuple-element.70.s, f32[384,128]{1,0:T(8,128)S(1)} %get-tuple-element.71.u, ...), custom_call_target="tpu_custom_call" | custom-call | tf_op jit(solution)/shard_map/project/pallas_call | solution.py:452
  28.6 0.0 collective-permute-done.5.west
  28.6 0.0 collective-permute-done.6.east
  28.6 0.9 %sides.3 = (f32[8,8,128]{2,1,0:T(8,128)S(1)}, f32[4,8,128]{2,1,0:T(8,128)S(1)}) custom-call(s32[4]{0:T(128)S(1)} %pad_add_fusion.ids, f32[2,8,128]{2,1,0:T(8,128)S(1)} %collective-permute-done.5.west, f32[2,8,128]{2,1,0:T(8,128)S(1)} %collective-permute-done.6.east, f32[4,8,128]{2,1,0:T(8,128)S(1)} %collective-permute-done.west.west_sea.west_const, ...), custom_call_target="tpu_custom_call" | custom-call | tf_op jit(solution)/shard_map/sides/pallas_call | solution.py:452
  29.5 0.9 %collective-permute-start.7 = (f32[8,8,128]{2,1,0:T(8,128)S(1)}, f32[8,8,128]{2,1,0:T(8,128)S(1)}, u32[]{:S(2)}, u32[]{:S(2)}) collective-permute-start(f32[8,8,128]{2,1,0:T(8,128)S(1)} %get-tuple-element.80.mine), channel_id=1, source_target_pairs={{0,1},{1,0},{2,3},{3,2},{4,5},{5,4},{6,7},{7,6},{8,9},{9,8},{10,11... | collective-permute-start | bytes 98312 | tf_op jit(solution)/shard_map/ppermute | solution.py:505
  30.4 3.5 %collective-permute-start.9 = (f32[8,128]{1,0:T(8,128)S(1)}, f32[8,128]{1,0:T(8,128)S(1)}, u32[]{:S(2)}, u32[]{:S(2)}) collective-permute-start(f32[8,128]{1,0:T(8,128)S(1)} %get-tuple-element.83), channel_id=1, source_target_pairs={{0,3},{1,2},{2,1},{3,0},{4,7},{5,6},{6,5},{7,4},{8,11},{9,10},{10,... | collective-permute-start | bytes 12296 | tf_op jit(solution)/shard_map/ppermute | solution.py:502
  33.8 1.9 %collective-permute-done.9.rest_3_ = f32[8,128]{1,0:T(8,128)S(1)} collective-permute-done((f32[8,128]{1,0:T(8,128)S(1)}, f32[8,128]{1,0:T(8,128)S(1)}, u32[]{:S(2)}, u32[]{:S(2)}) %collective-permute-start.9) | collective-permute-done | bytes 4128 | tf_op jit(solution)/shard_map/ppermute | solution.py:502
  35.8 0.0 collective-permute-done.7.theirs
  35.8 0.0 collective-permute-done.8.rest_0_.rest_2_
  35.8 2.5 %stencil.3 = (f32[384,128]{1,0:T(8,128)}, f32[384,128]{1,0:T(8,128)}, f32[384,128]{1,0:T(8,128)}, f32[384,128]{1,0:T(8,128)}) custom-call(s32[4]{0:T(128)S(1)} %pad_add_fusion.ids, f32[8]{0:T(128)S(1)} %copy-done, f32[4,384,128]{2,1,0:T(8,128)S(1)} %get-tuple-element.76.proj, f32[384,128]{1,0:T(8,128)S(1)} %get-tuple-element.53.spike, ...), custom_call_target="tpu_custom_call" | custom-call | tf_op jit(solution)/shard_map/stencil/pallas_call | solution.py:452
Async XLA Ops:
  0.6 9.8 %copy-start = (f32[8]{0:T(128)S(1)}, f32[8]{0:T(128)}, u32[]{:S(2)}) copy-start(f32[8]{0:T(128)} %coup.3) | copy-start | bytes 100
  3.7 16.6 %collective-permute-start.3 = (f32[7,48,128]{2,1,0:T(8,128)S(1)}, f32[7,48,128]{2,1,0:T(8,128)S(1)}, u32[]{:S(2)}, u32[]{:S(2)}) collective-permute-start(f32[7,48,128]{2,1,0:T(8,128)S(1)} %get-tuple-element.66), channel_id=1, source_target_pairs={{0,2},{2,0},{1,3},{3,1},{4,6},{6,4},{5,7},{7,5},{8,10},{10,8},{9,1... | collective-permute-start | bytes 516104 | tf_op jit(solution)/shard_map/ppermute | solution.py:498
  7.8 4.5 %collective-permute-start = (f32[4,8,128]{2,1,0:T(8,128)S(1)}, f32[4,8,128]{2,1,0:T(8,128)S(1)}, u32[]{:S(2)}, u32[]{:S(2)}) collective-permute-start(f32[4,8,128]{2,1,0:T(8,128)S(1)} %get-tuple-element.55), channel_id=1, source_target_pairs={{0,4},{4,8},{8,12},{12,16},{16,20},{20,24},{24,28},{28,0},{1,5},{5... | collective-permute-start | bytes 49160 | tf_op jit(solution)/shard_map/ppermute | solution.py:522
  7.8 4.5 %collective-permute-start.1 = (f32[3,8,128]{2,1,0:T(8,128)S(1)}, f32[3,8,128]{2,1,0:T(8,128)S(1)}, u32[]{:S(2)}, u32[]{:S(2)}) collective-permute-start(f32[3,8,128]{2,1,0:T(8,128)S(1)} %get-tuple-element.56), channel_id=1, source_target_pairs={{4,0},{8,4},{12,8},{16,12},{20,16},{24,20},{28,24},{0,28},{5,1},{9... | collective-permute-start | bytes 36872 | tf_op jit(solution)/shard_map/ppermute | solution.py:523
  13.2 7.0 %collective-permute-start.2 = (f32[8,8,128]{2,1,0:T(8,128)S(1)}, f32[8,8,128]{2,1,0:T(8,128)S(1)}, u32[]{:S(2)}, u32[]{:S(2)}) collective-permute-start(f32[8,8,128]{2,1,0:T(8,128)S(1)} %get-tuple-element.61.mine), channel_id=1, source_target_pairs={{0,1},{1,0},{2,3},{3,2},{4,5},{5,4},{6,7},{7,6},{8,9},{9,8},{10,11... | collective-permute-start | bytes 98312 | tf_op jit(solution)/shard_map/ppermute | solution.py:505
  14.9 5.4 %collective-permute-start.4 = (f32[8,128]{1,0:T(8,128)S(1)}, f32[8,128]{1,0:T(8,128)S(1)}, u32[]{:S(2)}, u32[]{:S(2)}) collective-permute-start(f32[8,128]{1,0:T(8,128)S(1)} %get-tuple-element.67), channel_id=1, source_target_pairs={{0,3},{1,2},{2,1},{3,0},{4,7},{5,6},{6,5},{7,4},{8,11},{9,10},{10,... | collective-permute-start | bytes 12296 | tf_op jit(solution)/shard_map/ppermute | solution.py:502
  24.4 11.4 %collective-permute-start.8 = (f32[5,48,128]{2,1,0:T(8,128)S(1)}, f32[5,48,128]{2,1,0:T(8,128)S(1)}, u32[]{:S(2)}, u32[]{:S(2)}) collective-permute-start(f32[5,48,128]{2,1,0:T(8,128)S(1)} %get-tuple-element.82), channel_id=1, source_target_pairs={{0,2},{2,0},{1,3},{3,1},{4,6},{6,4},{5,7},{7,5},{8,10},{10,8},{9,1... | collective-permute-start | bytes 368648 | tf_op jit(solution)/shard_map/ppermute | solution.py:498
  24.5 4.1 %collective-permute-start.5 = (f32[2,8,128]{2,1,0:T(8,128)S(1)}, f32[2,8,128]{2,1,0:T(8,128)S(1)}, u32[]{:S(2)}, u32[]{:S(2)}) collective-permute-start(f32[2,8,128]{2,1,0:T(8,128)S(1)} %get-tuple-element.77), channel_id=1, source_target_pairs={{0,4},{4,8},{8,12},{12,16},{16,20},{20,24},{24,28},{28,0},{1,5},{5... | collective-permute-start | bytes 24584 | tf_op jit(solution)/shard_map/ppermute | solution.py:588
  24.5 4.1 %collective-permute-start.6 = (f32[2,8,128]{2,1,0:T(8,128)S(1)}, f32[2,8,128]{2,1,0:T(8,128)S(1)}, u32[]{:S(2)}, u32[]{:S(2)}) collective-permute-start(f32[2,8,128]{2,1,0:T(8,128)S(1)} %get-tuple-element.78), channel_id=1, source_target_pairs={{4,0},{8,4},{12,8},{16,12},{20,16},{24,20},{28,24},{0,28},{5,1},{9... | collective-permute-start | bytes 24584 | tf_op jit(solution)/shard_map/ppermute | solution.py:589
  29.5 6.3 %collective-permute-start.7 = (f32[8,8,128]{2,1,0:T(8,128)S(1)}, f32[8,8,128]{2,1,0:T(8,128)S(1)}, u32[]{:S(2)}, u32[]{:S(2)}) collective-permute-start(f32[8,8,128]{2,1,0:T(8,128)S(1)} %get-tuple-element.80.mine), channel_id=1, source_target_pairs={{0,1},{1,0},{2,3},{3,2},{4,5},{5,4},{6,7},{7,6},{8,9},{9,8},{10,11... | collective-permute-start | bytes 98312 | tf_op jit(solution)/shard_map/ppermute | solution.py:505
  30.4 5.4 %collective-permute-start.9 = (f32[8,128]{1,0:T(8,128)S(1)}, f32[8,128]{1,0:T(8,128)S(1)}, u32[]{:S(2)}, u32[]{:S(2)}) collective-permute-start(f32[8,128]{1,0:T(8,128)S(1)} %get-tuple-element.83), channel_id=1, source_target_pairs={{0,3},{1,2},{2,1},{3,0},{4,7},{5,6},{6,5},{7,4},{8,11},{9,10},{10,... | collective-permute-start | bytes 12296 | tf_op jit(solution)/shard_map/ppermute | solution.py:502

commit v5 on v4

--- a/solution.py
+++ b/solution.py
@@ -17,7 +17,7 @@
 haline = 0.8
 
 BLOCK = 48
-VMEM_BYTES = 12 * 1024 * 1024
+VMEM_BYTES = 16 * 1024 * 1024
 f32 = jnp.float32
 bf16 = jnp.bfloat16
 CORNER_LANE = 16
@@ -100,30 +100,17 @@
     fields = (t, s, u, v)
     for move in moves:
         move.wait()
-
-    def one(k, accs):
-        accs = list(accs)
-        here = [level(x, k, rows) for x in (*fields, sea, east, flags.at[1], flags.at[0])]
-        at = lane == k, lane == k + half
-        for j, value in enumerate(here):
-            accs[j // 2 if j < 4 else j - 2] = jnp.where(
-                at[j % 2 if j < 4 else 0],
-                turn(value, k + (j % 2 if j < 4 else 0) * half + 1),
-                accs[j // 2 if j < 4 else j - 2],
-            )
-        for j, value in enumerate(here[:5]):
-            accs[6 + j // 2] = jnp.where(at[j % 2], turn(value, k + (j % 2) * half), accs[6 + j // 2])
-        return tuple(accs)
-
-    zero, none = jnp.zeros((rows, cols), f32), jnp.zeros((rows, cols), jnp.int32)
-    accs = each_level(levels, one, (zero, zero, none, zero, none, none, zero, zero, none))
-    wet, speed = accs[2].astype(f32), accs[3]
-    nexts = [wet * (speed * branches(flag)[0] - diffusion) for flag in accs[4:6]]
-    to_east[0], to_east[1] = accs[0], accs[1]
+    pairs = ((t, s, 2), (u, v, 2), (sea, east, 2), (flags.at[1], flags.at[0], 1))
+    packed = [edge_columns(levels, rows, x, y, pieces) for x, y, pieces in pairs]
+    for j in range(2):
+        to_east[j], to_west[j] = packed[j]
+    wet_speed, flag = packed[2][0], packed[3][0]
+    wet, speed = wet_speed, turn(wet_speed, half)
+    zonal = branches(jnp.round(flag).astype(jnp.int32))[0]
+    nexts = [wet * (speed * z - diffusion) for z in (zonal, turn(zonal, half))]
     to_east[2] = jnp.where(lane < half, wet, turn(nexts[0], half))
     to_east[3] = nexts[1]
-    to_west[0], to_west[1] = accs[6], accs[7]
-    to_west[2] = accs[8].astype(f32)
+    to_west[2] = packed[2][1]
     for which, row in enumerate(row_choices(pair, rows, ids[0])):
         msg = lat_msgs[which]
         for j, x in enumerate(fields):
@@ -146,11 +133,49 @@
         msg[6, :, pl.ds(0, levels)] = block
 
 
-def coef_kernel(dims, sea, east, north, flags, west_const, east_const, out):
+def edge_columns(levels, rows, x, y, pieces):
+    cols = x.shape[1]
+    half = cols // 2
+    source, target = iota((2 * cols, 2 * cols), 0), iota((2 * cols, 2 * cols), 1)
+    column = jnp.where(target < cols, cols - 1, 0) + jnp.where(target % cols < half, 0, cols)
+    spread = (source == column).astype(bf16)
+    both = jnp.concatenate([x[...].astype(f32), y[...].astype(f32)], axis=1)
+    high, low = split(both)
+    wide = dot(high, spread)
+    if pieces == 2:
+        wide = wide + dot(low, spread)
+    place = iota((rows, 2 * cols), 1) % half
+    out = jnp.zeros((rows, 2 * cols), f32)
+    for k in range(levels):
+        out = jnp.where(place == k, wide[k * rows : (k + 1) * rows], out)
+    return out[:, :cols], out[:, cols:]
+
+
+def insert(lane, value, west_in, east_in):
+    cols = value.shape[1]
+    return (
+        jnp.where(lane == 0, west_in, turn(value, 1)),
+        jnp.where(lane == cols - 1, east_in, turn(value, cols - 1)),
+    )
+
+
+def inner(row, value):
+    rows = value.shape[0]
+    return (
+        jnp.where(row == 0, 0.0, pltpu.roll(value, 1, 0)),
+        jnp.where(row == rows - 1, 0.0, pltpu.roll(value, rows - 1, 0)),
+    )
+
+
+def coef_kernel(dims, sea, east, north, flags, west_const, east_const, spike, spike_packed, out, factor, beside):
     levels, rows, cols, half, pair = dims
     lane, row = iota((rows, cols), 1), iota((rows, cols), 0)
     sea_side = east_const[2]
     sides = (west_const[3], west_const[2])
+
+    spk = spike_packed[...]
+    spike_west = jnp.where(lane < half, west_const[2], 0.0) * spk
+    spike_east = jnp.where(lane < half, east_const[2], 0.0) * spk
 
     def one(k, carry):
         wet = level(sea, k, rows).astype(f32)
@@ -159,20 +184,112 @@
         sea_east = jnp.where(lane == cols - 1, turn(sea_side, cols - 1 - k), turn(wet, cols - 1))
         sea_north = jnp.where(row == rows - 1, 1.0, pltpu.roll(wet, rows - 1, 0))
         here = level_at(k, rows)
+        mid = level(spike, k, rows)
+        west, east_ = insert(lane, mid, turn(spike_west, cols - k), turn(spike_east, cols - 1 - k))
+        south, north_ = inner(row, mid)
+        for j, value in enumerate((east_, west, north_, south)):
+            beside[j, here, :] = value
         for step in (1, 0):
             zonal, merid = branches(level(flags.at[step], k, rows))
             speed_z, speed_m = speed_e * zonal, speed_n * merid
-            out[step, 0, here, :] = part * (speed_e - speed_z + diffusion) * sea_east
+            east_own = part * (speed_e - speed_z + diffusion) * sea_east
             next_west = jnp.where(
                 lane == 0, turn(sides[step], 2 * cols - step * half - k), turn(wet * (speed_z - diffusion), 1)
             )
-            out[step, 1, here, :] = part * next_west
-            out[step, 2, here, :] = part * (speed_n - speed_m + diffusion) * sea_north
+            west_own = part * next_west
+            north_own = part * (speed_n - speed_m + diffusion) * sea_north
             next_south = jnp.where(row == 0, 1.0, pltpu.roll(wet * (speed_m - diffusion), 1, 0))
-            out[step, 3, here, :] = part * next_south
+            south_own = part * next_south
+            for j, value in enumerate((east_own, west_own, north_own, south_own)):
+                out[step, j, here, :] = value
+            inside_n = jnp.where(row == rows - 1, 0.0, north_own)
+            inside_s = jnp.where(row == 0, 0.0, south_own)
+            factor[step, 0, here, :] = mid * (1.0 + ((west_own - east_own) + (inside_s - inside_n)))
+            factor[step, 1, here, :] = east_own * east_
+            factor[step, 2, here, :] = -west_own * west
+            factor[step, 3, here, :] = inside_n * north_
+            factor[step, 4, here, :] = -inside_s * south
         return carry
 
     each_level(levels, one, ())
+
+
+def coriolis_of(dims, ids):
+    levels, rows, cols, half, pair = dims
+    index = (ids[0] * rows + iota((rows, cols), 0)).astype(f32)
+    return 0.2 + 0.6 * (index + 0.5) / (rows * ids[3]).astype(f32)
+
+
+def base_kernel(dims, step, ids, proj, side_proj, west_const, east_const, coef, out):
+    levels, rows, cols, half, pair = dims
+    lane, row = iota((rows, cols), 1), iota((rows, cols), 0)
+    parts = []
+    for p in range(2):
+        line = []
+        for side, const in enumerate((west_const, east_const)):
+            wet = jnp.where(lane < half, const[2], turn(const[2], half))
+            line.append(wet * side_proj[2 * side + p])
+        parts.append(jnp.concatenate(line, axis=1))
+    source, target = iota((2 * cols, 2 * cols), 0), iota((2 * cols, 2 * cols), 1)
+    pick = target % cols
+    wanted = pick // 2 + jnp.where(target < cols, 0, half) + jnp.where(pick % 2 == 1, 0, cols)
+    spread = (source == wanted).astype(bf16)
+    high, low = split(jnp.concatenate(parts, axis=0))
+    mixed = dot(high, spread) + dot(low, spread)
+    halo = [mixed[p * rows : (p + 1) * rows, i * cols : (i + 1) * cols] for p in range(2) for i in range(2)]
+    coriolis = coriolis_of(dims, ids)
+    push = -0.5 * pressure_scale * gravity
+    top, bottom = row == rows - 1, row == 0
+
+    def one(j, below):
+        k = levels - 1 - j
+        here = level_at(k, rows)
+        east_own, west_own = coef[step, 0, here, :], coef[step, 1, here, :]
+        north_own = jnp.where(top, 0.0, coef[step, 2, here, :])
+        south_own = jnp.where(bottom, 0.0, coef[step, 3, here, :])
+        mids, around = [], []
+        for f in range(4):
+            w = proj[f, here, :]
+            mids.append(w)
+            side = turn(halo[f], 2 * cols - 2 * k - 1)
+            around.append((*insert(lane, w, side, side), *inner(row, w)))
+        below = below + ((around[2][0] - around[2][1]) + (around[3][2] - around[3][3]))
+        buoyancy = push * below
+        for f in range(2):
+            w, (ww, we, ws, wn) = mids[f], around[f]
+            q = w + ((east_own * (we - w) + west_own * (w - ww)) + (north_own * (wn - w) + south_own * (w - ws)))
+            out[f, here, :] = q + buoyancy if f == 0 else q - haline * buoyancy
+        for f in (2, 3):
+            w, (ww, we, ws, wn) = mids[f], around[f]
+            spin = coriolis * mids[5 - f]
+            centre = (1.0 - 4.0 * viscosity) * w
+            centre = centre - spin if f == 2 else centre + spin
+            out[f, here, :] = centre + viscosity * ((we + ww) + (wn + ws))
+        return below
+
+    each_level(levels, one, jnp.zeros((rows, cols), f32))
+
+
+def rows_kernel(dims, ids, *refs):
+    levels, rows, cols, half, pair = dims
+    count = 1 if pair else 2
+    new, const, outs, lines, (scratch,) = (refs[i * count : (i + 1) * count] for i in range(5))
+    eye = (iota((levels, levels), 0) == iota((levels, levels), 1)).astype(bf16)
+    pick = (iota((levels, cols), 0) == ids[2]).astype(bf16)
+    at_edge = pl.ds(ids[2], 1)
+    for h in range(count):
+        block = split(const[h][6][:, :levels])
+        turned = tuple(dot(eye, piece, ((1,), (1,))).astype(bf16) for piece in block)
+        scratch[4] = dot(turned[0], pick) + dot(turned[1], pick)
+        for p in range(2):
+            both = dot3(turned, split(jnp.concatenate([new[h][2 * p], new[h][2 * p + 1]], axis=1)))
+            scratch[2 * p] = both[:, :cols]
+            scratch[2 * p + 1] = both[:, cols:]
+        lines[h][...] = jnp.zeros_like(lines[h])
+        wet = const[h][4]
+        for j in range(5):
+            lines[h][pl.ds(j, 1), :] = scratch[j, at_edge, :]
+            outs[h][j] = wet * scratch[j]
 
 
 def project_kernel(dims, setup, ids, t, s, u, v, sea, *rest):
@@ -283,59 +400,20 @@
     msg[7] = jnp.where(lane == CORNER_LANE, corner[...], misc)
 
 
-def stencil_kernel(dims, step, final, ids, coup, proj, spike, spike_packed, mine, theirs, side_proj,
-                   west_const, east_const, coef, *rest):
+def apply_kernel(dims, step, final, ids, coup, proj, spike, mine, theirs, base, coef, factor, beside, *rest):
     levels, rows, cols, half, pair = dims
     count = 1 if pair else 2
-    row_new, row_const, row_late, row_far = (rest[i * count : (i + 1) * count] for i in range(4))
-    rest = rest[4 * count :]
+    row_proj, row_line, row_const, row_late, row_far = (rest[i * count : (i + 1) * count] for i in range(5))
+    rest = rest[5 * count :]
     if final:
-        outs, rest = rest[:4], rest[4:]
+        outs = rest
     else:
-        late_out, rest = rest[0], rest[1:]
-        outs, (to_east, to_west), rest = rest[:4], rest[4:6], rest[6:]
-        lat_msgs, rest = rest[:count], rest[count:]
-    north_w, south_w, north_sea, south_next, line, sides = rest
-    lat, depth, edge, parts = ids[0], ids[1], ids[2], ids[3]
+        late_out, outs, (to_east, to_west), lat_msgs = rest[0], rest[1:5], rest[5:7], rest[7:]
+    lat, depth, parts = ids[0], ids[1], ids[3]
     lane = iota((rows, cols), 1)
     row = iota((rows, cols), 0)
     has_north = jnp.where(lat < parts - 1, 1.0, 0.0)
     has_south = jnp.where(lat > 0, 1.0, 0.0)
-
-    row_sums = []
-    for h in range(count):
-        block = split(row_const[h][6][:, :levels])
-        eye = (iota((levels, levels), 0) == iota((levels, levels), 1)).astype(bf16)
-        turned = tuple(dot(eye, piece, ((1,), (1,))).astype(bf16) for piece in block)
-        pick = (iota((levels, cols), 0) == edge).astype(bf16)
-        thin = dot(turned[0], pick) + dot(turned[1], pick)
-        line[4] = thin
-        for f in range(4):
-            line[f] = dot3(turned, split(row_new[h][f]))
-        at_edge = pl.ds(edge, 1)
-        far = row_far[h]
-        c = far[7:8, :]
-        other_corner = far[6:7, :]
-        own_corner = line[4, at_edge, :]
-        scaled = c / (1.0 - c * c * own_corner * other_corner)
-        wet = row_const[h][4]
-        if pair:
-            masks = ((north_w, has_north), (south_w, has_south))
-        else:
-            masks = ((north_w, has_north),) if h == 0 else ((south_w, has_south),)
-        for f in range(4):
-            carried = scaled * (far[f : f + 1, :] + c * other_corner * line[f, at_edge, :])
-            value = wet * (line[f] + thin * carried)
-            for target, mask in masks:
-                target[f] = value * mask
-        if pair or h == 0:
-            north_sea[...] = wet * has_north
-        if pair or h == 1:
-            late = row_const[h][5] if step else row_late[h][4]
-            south_next[...] = late * has_south
-        theirs_v = scaled * (line[3, at_edge, :] + c * own_corner * far[3:4, :])
-        row_sums.append(far[4:5, :] + far[5:6, :] * theirs_v)
-    row_sum_north, row_sum_south = row_sums[0], row_sums[-1]
 
     c = jnp.zeros((rows, cols), f32)
     for y in range(rows):
@@ -349,101 +427,108 @@
     carried_side = scaled * (misc + co * mine[7])
     theirs_side = scaled * (mine[7] + cm * misc)
 
-    spk = spike_packed[...]
-    for side, const in enumerate((west_const, east_const)):
-        wet = jnp.where(lane < half, const[2], pltpu.roll(const[2], half, 1))
-        for p in range(2):
-            joined = jnp.where(
-                lane < half,
-                lane_of(carried_side, side * 8 + 2 * p),
-                lane_of(carried_side, side * 8 + 2 * p + 1),
-            )
-            sides[2 * side + p] = wet * (side_proj[2 * side + p] + spk * joined)
+    row_solved, row_sums = [], []
+    for h in range(count):
+        far, line = row_far[h], row_line[h]
+        c_row, other, own = far[7:8, :], far[6:7, :], line[4:5, :]
+        scaled_row = c_row / (1.0 - c_row * c_row * own * other)
+        joined = [scaled_row * (far[f : f + 1, :] + c_row * other * line[f : f + 1, :]) for f in range(4)]
+        row_solved.append([row_proj[h][f] + row_proj[h][4] * joined[f] for f in range(4)])
+        theirs_v = scaled_row * (line[3:4, :] + c_row * own * far[3:4, :])
+        row_sums.append(far[4:5, :] + far[5:6, :] * theirs_v)
 
     sum_u = theirs[4] + theirs[6] * (scaled * (mine[2] + cm * theirs[2]))
     sum_v = theirs[5] + theirs[6] * (scaled * (mine[3] + cm * theirs[3]))
     side_u = [lane_of(misc, q * 8 + 4) + lane_of(misc, q * 8 + 5) * lane_of(theirs_side, q * 8 + 2) for q in (0, 1)]
-
-    def shifted(value, west_in, east_in, south_in, north_in):
-        return (
-            jnp.where(lane == 0, west_in, pltpu.roll(value, 1, 1)),
-            jnp.where(lane == cols - 1, east_in, pltpu.roll(value, cols - 1, 1)),
-            jnp.where(row == 0, south_in, pltpu.roll(value, 1, 0)),
-            jnp.where(row == rows - 1, north_in, pltpu.roll(value, rows - 1, 0)),
-        )
-
-    west_u = jnp.where(lane == 0, side_u[0], pltpu.roll(sum_u, 1, 1))
-    east_u = jnp.where(lane == cols - 1, side_u[1], pltpu.roll(sum_u, cols - 1, 1))
-    south_v = jnp.where(row == 0, row_sum_south * has_south, pltpu.roll(sum_v, 1, 0))
-    north_v = jnp.where(row == rows - 1, row_sum_north * has_north, pltpu.roll(sum_v, rows - 1, 0))
+    west_u, east_u = insert(lane, sum_u, *side_u)
+    south_v = jnp.where(row == 0, row_sums[-1] * has_south, pltpu.roll(sum_v, 1, 0))
+    north_v = jnp.where(row == rows - 1, row_sums[0] * has_north, pltpu.roll(sum_v, rows - 1, 0))
     upper = jnp.where(depth == 0, 1.0, 0.0)
     deeper = (west_u - east_u + south_v - north_v) * upper
 
-    north_index = (lat * rows + row).astype(f32)
-    coriolis = 0.2 + 0.6 * (north_index + 0.5) / (rows * parts).astype(f32)
-
-    west_sides = (sides[0], sides[1])
-    east_sides = (sides[2], sides[3])
+    coriolis = coriolis_of(dims, ids)
     push = -0.5 * pressure_scale * gravity
-    top, bottom = row == rows - 1, row == 0
-
-    def one(j, carry):
-        below, *accs = carry
+    around = []
+    for f in range(4):
+        west, east = insert(lane, carried[f], lane_of(carried_side, f), lane_of(carried_side, 8 + f))
+        south, north = inner(row, carried[f])
+        around.append((east, west, north, south))
+    plain = 1.0 - 4.0 * viscosity
+    mids = (plain * carried[2] - coriolis * carried[3], plain * carried[3] + coriolis * carried[2])
+
+    def one(j, below):
         k = levels - 1 - j
         here = level_at(k, rows)
-        one = pl.ds(k, 1)
-        east_own, west_own = coef[step, 0, here, :], coef[step, 1, here, :]
-        north_own = coef[step, 2, here, :] * jnp.where(top, north_sea[one, :], 1.0)
-        south_own = coef[step, 3, here, :] * jnp.where(bottom, south_next[one, :], 1.0)
-        spk_k = spike[here, :]
-        solved, around = [], []
+        sides = [beside[j, here, :] for j in range(4)]
+        moved = [[side * plane for side, plane in zip(sides, around[f])] for f in (2, 3)]
+        below = below + ((moved[0][1] - moved[0][0]) + (moved[1][3] - moved[1][2]))
+        buoyancy = push * below
+        factors = [factor[step, j, here, :] for j in range(5)]
+        for f in range(2):
+            q = base[f, here, :] + factors[0] * carried[f]
+            q = q + (
+                (factors[1] * around[f][0] + factors[2] * around[f][1])
+                + (factors[3] * around[f][2] + factors[4] * around[f][3])
+            )
+            outs[f][here, :] = q + buoyancy if f == 0 else q - haline * buoyancy
+        spk = spike[here, :]
+        for i in range(2):
+            total = (moved[i][0] + moved[i][1]) + (moved[i][2] + moved[i][3])
+            outs[2 + i][here, :] = base[2 + i, here, :] + (spk * mids[i] + viscosity * total)
+        return below
+
+    each_level(levels, one, deeper)
+
+    later = (iota((levels, levels), 1) >= iota((levels, levels), 0)).astype(bf16)
+    for h in range(count):
+        if pair:
+            at, sign = jnp.where(lat == 0, rows - 1, 0), jnp.where(lat == 0, -1.0, 1.0)
+        else:
+            at, sign = ((rows - 1, -1.0), (0, 1.0))[h]
+        take = lambda ref: take_row(ref, at, levels, rows)
+        beyond = row_solved[h]
+        if pair:
+            own = jnp.where(lat == 0, coef[step, 2, pl.ds(rows - 1, levels, stride=rows), :],
+                            coef[step, 3, pl.ds(0, levels, stride=rows), :])
+        else:
+            own = coef[step, 2 + h, pl.ds(at, levels, stride=rows), :]
+        late = row_const[h][5] if step else row_late[h][4]
+        here_north = row_const[h][4]
+        if pair:
+            other = jnp.where(lat == 0, here_north, -late)
+        else:
+            other = here_north if h == 0 else -late
+        gate = own * other
+        above = push * sign * beyond[3]
+        high, low = split(above)
+        rise = dot(later, high) + dot(later, low)
+        spk = take(spike)
+        pick = lambda plane: (
+            jnp.where(lat == 0, plane[rows - 1 : rows], plane[0:1]) if pair else plane[at : at + 1]
+        )
+        extra = []
+        for f in range(2):
+            mid = take(proj.at[f]) + spk * pick(carried[f])
+            flow = gate * (beyond[f] - mid)
+            extra.append(flow + rise if f == 0 else flow - haline * rise)
+        for f in (2, 3):
+            extra.append(viscosity * beyond[f])
         for f in range(4):
-            w = proj[f, here, :] + spk_k * carried[f]
-            shift = (f % 2) * half
-            solved.append(w)
-            around.append(
-                shifted(
-                    w,
-                    turn(west_sides[f // 2], 2 * cols - shift - k),
-                    turn(east_sides[f // 2], 2 * cols - 1 - shift - k),
-                    south_w[f, one, :],
-                    north_w[f, one, :],
-                )
-            )
-        below = below + ((around[2][0] - around[2][1]) + (around[3][2] - around[3][3]))
-        buoyancy = push * below
-        new = []
-        for f in range(2):
-            w, (ww, we, ws, wn) = solved[f], around[f]
-            q = w + ((east_own * (we - w) + west_own * (w - ww)) + (north_own * (wn - w) + south_own * (w - ws)))
-            new.append(q + buoyancy if f == 0 else q - haline * buoyancy)
-        for f in (2, 3):
-            w, (ww, we, ws, wn) = solved[f], around[f]
-            spin = coriolis * solved[5 - f]
-            centre = (1.0 - 4.0 * viscosity) * w
-            centre = centre - spin if f == 2 else centre + spin
-            new.append(centre + viscosity * ((we + ww) + (wn + ws)))
-        for f in range(4):
-            outs[f][here, :] = new[f]
-        if not final:
-            for f in range(4):
-                place = k + (f % 2) * half
-                there = lane == place
-                accs[f // 2] = jnp.where(there, turn(new[f], place + 1), accs[f // 2])
-                accs[2 + f // 2] = jnp.where(there, turn(new[f], place), accs[2 + f // 2])
-        return (below, *accs)
-
-    zero = jnp.zeros((rows, cols), f32)
-    extra = () if final else (zero,) * 4
-    _, *accs = each_level(levels, one, (deeper, *extra))
+            if pair:
+                for place, mask in ((rows - 1, has_north), (0, has_south)):
+                    there = pl.ds(place, levels, stride=rows)
+                    outs[f][there, :] = outs[f][there, :] + mask * extra[f]
+            else:
+                there = pl.ds(at, levels, stride=rows)
+                outs[f][there, :] = outs[f][there, :] + (has_north if h == 0 else has_south) * extra[f]
+
     if not final:
-        for p in range(2):
-            to_east[p] = accs[p]
-            to_west[p] = accs[2 + p]
         for which, at in enumerate(row_choices(pair, rows, lat)):
             for f in range(4):
                 lat_msgs[which][f] = take_row(outs[f], at, levels, rows)
             lat_msgs[which][4] = late_out[...]
+        for p in range(2):
+            to_east[p], to_west[p] = edge_columns(levels, rows, outs[2 * p], outs[2 * p + 1], 2)
 
 
 def call(kernel, outs, args, smem=(0,), scratch=(), name=None, hbm=()):
@@ -550,37 +635,40 @@
         )
         theirs = to_depth(mine)
         if first:
-            (coef,) = call(
+            coef, factor, beside = call(
                 functools.partial(coef_kernel, dims),
-                [((STEPS, 4, n, cols), f32)],
-                (sea, east, north, flags, west_const, east_const),
+                [((STEPS, 4, n, cols), f32), ((STEPS, 5, n, cols), f32), ((4, n, cols), f32)],
+                (sea, east, north, flags, west_const, east_const, spike, spike_packed),
                 (),
                 name="coef",
             )
+        (base,) = call(
+            functools.partial(base_kernel, dims, step),
+            [((4, n, cols), f32)],
+            (ids, proj, side_proj, west_const, east_const, coef),
+            name="base",
+        )
+        rows_out = call(
+            functools.partial(rows_kernel, dims),
+            [((5,) + grid, f32)] * count + [(plane, f32)] * count,
+            (ids, *row_new, *row_const),
+            scratch=(pltpu.VMEM((5,) + grid, f32),),
+            name="rows",
+        )
         final = step == 0
-        state_shape = [((n, cols), f32)] * 4
-        if final:
-            outs, extra = state_shape, ()
-        else:
-            outs = state_shape + [((2,) + plane, f32)] * 2 + [((5,) + grid, f32)] * count
+        outs, extra = [((n, cols), f32)] * 4, ()
+        if not final:
+            outs = outs + [((2,) + plane, f32)] * 2 + [((5,) + grid, f32)] * count
             extra = (late,)
         result = call(
-            functools.partial(stencil_kernel, dims, step, final),
+            functools.partial(apply_kernel, dims, step, final),
             outs,
             (
-                ids, coupling, proj, spike, spike_packed, mine, theirs, side_proj, west_const, east_const,
-                coef, *row_new, *row_const, *row_new, *row_far, *extra,
+                ids, coupling, proj, spike, mine, theirs, base, coef, factor, beside,
+                *rows_out, *row_const, *row_new, *row_far, *extra,
             ),
             (0, 1),
-            (
-                pltpu.VMEM((4,) + grid, f32),
-                pltpu.VMEM((4,) + grid, f32),
-                pltpu.VMEM(grid, f32),
-                pltpu.VMEM(grid, f32),
-                pltpu.VMEM((5,) + grid, f32),
-                pltpu.VMEM((4,) + plane, f32),
-            ),
-            name="stencil",
+            name="apply",
         )
         state = result[:4]
         if not final:

time: 38.4 us -> 36.5 us (0.951)
  waiting for transfers between devices: 6.86 us -> 3.26 us
  Pallas kernels: 15 us -> 16.7 us
    ppermute x2, waiting for transfers between devices: 6.84 us -> 3.24 us  [to_lat(): return [lax.ppermute(m, ('lat', 'depth'), r) for m, r in zip(msgs, both)]]
    pallas_call x8 -> x12, Pallas kernels: 15 us -> 16.7 us  [call(): pl.pallas_call(kernel, out_shape=[jax.ShapeDtypeStruct(shape, kind) for s...]
    ppermute x2, starting transfers between devices: 3.47 us -> 2.49 us  [to_lat(): return [lax.ppermute(m, ('lat', 'depth'), r) for m, r in zip(msgs, both)]]
    ppermute x2, starting transfers between devices: 2.56 us -> 3.54 us  [to_depth(): lax.ppermute(msg, 'depth', [(d, depths - 1 - d) for d in range(depths)])]
  transfers between devices with their start and end apart: 10 -> 10, of which waited for: 2 -> 2; matrix products, arithmetic and copies ran while one was open for 0% -> 0% of each run, Pallas kernels for 14% -> 27%
where the time goes in v5:
time: 36.5 us; the launch traced here: 36.4 us
  Pallas kernels  16.7 us (46%)
  starting transfers between devices  15.6 us (43%)
  waiting for transfers between devices  3.26 us (9%)
  between operations  0.78 us (2%)
    pallas_call x12, Pallas kernels, call(): pl.pallas_call(kernel, out_shape=[jax.ShapeDtypeStruct(shape, kind) for s...  16.7 us
    ppermute x2, starting transfers between devices, to_lat(): return [lax.ppermute(m, 'lat', r) for m, r in zip(msgs, routes)]  4.2 us
    ppermute x2, starting transfers between devices, to_depth(): lax.ppermute(msg, 'depth', [(d, depths - 1 - d) for d in range(depths)])  3.54 us
    ppermute x2, waiting for transfers between devices, to_lat(): return [lax.ppermute(m, ('lat', 'depth'), r) for m, r in zip(msgs, both)]  3.24 us
    ppermute x1, starting transfers between devices, on_device(): east_const = lax.ppermute(to_west, 'lon', back)  2.64 us
    ppermute x1, starting transfers between devices, on_device(): east_in = lax.ppermute(result[5], 'lon', back)  2.63 us
    ppermute x2, starting transfers between devices, to_lat(): return [lax.ppermute(m, ('lat', 'depth'), r) for m, r in zip(msgs, both)]  2.49 us
  transfers between devices with their start and end apart: 10, of which 2 were waited for; matrix products, arithmetic and copies ran while one was open for 0% of the time, Pallas kernels for 27%

profile of v5, /device:TPU:0, one launch (start us, length us, event | category | flops | bytes accessed | tf_op | source)
XLA Modules:
  0.0 36.4 jit_solution(12532801351552675093)
XLA Ops:
  0.6 0.0 copy-start
  0.6 0.1 pad_add_fusion.ids
  0.7 2.9 %pack.1 = (f32[4,8,128]{2,1,0:T(8,128)S(1)}, f32[3,8,128]{2,1,0:T(8,128)S(1)}, f32[48,128]{1,0:T(8,128)S(1)}, f32[7,48,128]{2,1,0:T(8,128)S(1)}, f32[384,128]{1,...) custom-call(s32[4]{0:T(128)S(1)} %pad_add_fusion.ids, ...), custom_call_target="tpu_custom_call" | custom-call | tf_op jit(solution)/shard_map/pack/pallas_call | solution.py:537
  3.6 4.1 %collective-permute-start.3 = (f32[7,48,128]{2,1,0:T(8,128)S(1)}, f32[7,48,128]{2,1,0:T(8,128)S(1)}, u32[]{:S(2)}, u32[]{:S(2)}) collective-permute-start(f32[7,48,128]{2,1,0:T(8,128)S(1)} %get-tuple-element.76), channel_id=1, source_target_pairs={{0,2},{2,0},{1,3},{3,1},{4,6},{6,4},{5,7},{7,5},{8,10},{10,8},{9,1... | collective-permute-start | bytes 516104 | tf_op jit(solution)/shard_map/ppermute | solution.py:583
  7.7 0.0 collective-permute-start
  7.7 2.6 %collective-permute-start.1 = (f32[3,8,128]{2,1,0:T(8,128)S(1)}, f32[3,8,128]{2,1,0:T(8,128)S(1)}, u32[]{:S(2)}, u32[]{:S(2)}) collective-permute-start(f32[3,8,128]{2,1,0:T(8,128)S(1)} %get-tuple-element.62), channel_id=1, source_target_pairs={{4,0},{8,4},{12,8},{16,12},{20,16},{24,20},{28,24},{0,28},{5,1},{9... | collective-permute-start | bytes 36872 | tf_op jit(solution)/shard_map/ppermute | solution.py:608
  10.4 0.0 copy-done
  10.4 1.9 %project.2 = (f32[4,384,128]{2,1,0:T(8,128)S(1)}, f32[7,8,128]{2,1,0:T(8,128)S(1)}, f32[8,128]{1,0:T(8,128)S(1)}, f32[384,128]{1,0:T(8,128)S(1)}, bf16[384,384]{...) custom-call(s32[4]{0:T(128)S(1)} %pad_add_fusion.ids, ...), custom_call_target="tpu_custom_call" | custom-call | tf_op jit(solution)/shard_map/project/pallas_call | solution.py:537
  12.3 0.0 collective-permute-done.1.east.east_sea.east_const
  12.3 0.0 collective-permute-done.west.west_sea.west_const
  12.3 0.9 %sides.2 = (f32[8,8,128]{2,1,0:T(8,128)S(1)}, f32[4,8,128]{2,1,0:T(8,128)S(1)}) custom-call(s32[4]{0:T(128)S(1)} %pad_add_fusion.ids, f32[4,8,128]{2,1,0:T(8,128)S(1)} %collective-permute-done.west.west_sea.west_const, f32[3,8,128]{2,1,0:T(8,128)S(1)} %collective-permute-done.1.east.east_sea.east_const, ...), custom_call_target="tpu_custom_call" | custom-call | tf_op jit(solution)/shard_map/sides/pallas_call | solution.py:537
  13.1 1.6 %collective-permute-start.2 = (f32[8,8,128]{2,1,0:T(8,128)S(1)}, f32[8,8,128]{2,1,0:T(8,128)S(1)}, u32[]{:S(2)}, u32[]{:S(2)}) collective-permute-start(f32[8,8,128]{2,1,0:T(8,128)S(1)} %get-tuple-element.68.mine), channel_id=1, source_target_pairs={{0,1},{1,0},{2,3},{3,2},{4,5},{5,4},{6,7},{7,6},{8,9},{9,8},{10,11... | collective-permute-start | bytes 98312 | tf_op jit(solution)/shard_map/ppermute | solution.py:590
  14.8 0.0 collective-permute-start.4
  14.8 0.7 %coef.1 = (f32[2,4,384,128]{3,2,1,0:T(8,128)S(1)}, f32[2,5,384,128]{3,2,1,0:T(8,128)S(1)}, f32[4,384,128]{2,1,0:T(8,128)S(1)}) custom-call(s32[384,128]{1,0:T(8,128)S(1)} %get-tuple-element.57.sea, f32[384,128]{1,0:T(8,128)S(1)} %get-tuple-element.70.east, f32[384,128]{1,0:T(8,128)S(1)} %get-tuple-element.71.north, ...), custom_call_target="tpu_custom_call" | custom-call | tf_op jit(solution)/shard_map/coef/pallas_call | solution.py:537
  15.5 1.3 %base.2 = f32[4,384,128]{2,1,0:T(8,128)S(1)} custom-call(s32[4]{0:T(128)S(1)} %pad_add_fusion.ids, f32[4,384,128]{2,1,0:T(8,128)S(1)} %get-tuple-element.59.proj, f32[4,8,128]{2,1,0:T(8,128)S(1)} %get-tuple-element.69.side_proj, f32[4,8,128]{2,1,0:T(8,128)S(1)} %collective-permute-done.west.west_sea.west_const, ...), custom_call_target="tpu_custom_call" | custom-call | tf_op jit(solution)/shard_map/base/pallas_call | solution.py:537
  16.8 0.0 collective-permute-done.3.refs_0_.refs_1_.rest_2_.rest_3_
  16.8 0.9 %rows.2 = (f32[5,48,128]{2,1,0:T(8,128)S(1)}, f32[8,128]{1,0:T(8,128)S(1)}) custom-call(s32[4]{0:T(128)S(1)} %pad_add_fusion.ids, f32[7,48,128]{2,1,0:T(8,128)S(1)} %collective-permute-done.3.refs_0_.refs_1_.rest_2_.rest_3_, f32[7,48,128]{2,1,0:T(8,128)S(1)} %collective-permute-done.3.refs_0_.refs_1_.rest_2_.rest_3_), custom_call_target="tpu_custom_call" | custom-call | tf_op jit(solution)/shard_map/rows/pallas_call | solution.py:537
  17.7 2.5 %collective-permute-done.4.rest_4_ = f32[8,128]{1,0:T(8,128)S(1)} collective-permute-done((f32[8,128]{1,0:T(8,128)S(1)}, f32[8,128]{1,0:T(8,128)S(1)}, u32[]{:S(2)}, u32[]{:S(2)}) %collective-permute-start.4) | collective-permute-done | bytes 4128 | tf_op jit(solution)/shard_map/ppermute | solution.py:587
  20.2 0.0 collective-permute-done.2.theirs
  20.2 1.6 %apply.2 = (f32[384,128]{1,0:T(8,128)S(1)}, f32[384,128]{1,0:T(8,128)S(1)}, f32[384,128]{1,0:T(8,128)S(1)}, f32[384,128]{1,0:T(8,128)S(1)}, f32[2,8,128]{2,1,0:T...) custom-call(s32[4]{0:T(128)S(1)} %pad_add_fusion.ids, f32[8]{0:T(128)S(1)} %copy-done, ...), custom_call_target="tpu_custom_call" | custom-call | tf_op jit(solution)/shard_map/apply/pallas_call | solution.py:537
  21.8 0.1 collective-permute-start.8
  21.9 0.1 collective-permute-start.5
  22.0 2.6 %collective-permute-start.6 = (f32[2,8,128]{2,1,0:T(8,128)S(1)}, f32[2,8,128]{2,1,0:T(8,128)S(1)}, u32[]{:S(2)}, u32[]{:S(2)}) collective-permute-start(f32[2,8,128]{2,1,0:T(8,128)S(1)} %get-tuple-element.90), channel_id=1, source_target_pairs={{4,0},{8,4},{12,8},{16,12},{20,16},{24,20},{28,24},{0,28},{5,1},{9... | collective-permute-start | bytes 24584 | tf_op jit(solution)/shard_map/ppermute | solution.py:677
  24.6 1.4 %project.3 = (f32[4,384,128]{2,1,0:T(8,128)S(1)}, f32[7,8,128]{2,1,0:T(8,128)S(1)}, f32[8,128]{1,0:T(8,128)S(1)}) custom-call(s32[4]{0:T(128)S(1)} %pad_add_fusion.ids, f32[384,128]{1,0:T(8,128)S(1)} %get-tuple-element.81.t, f32[384,128]{1,0:T(8,128)S(1)} %get-tuple-element.82.s, f32[384,128]{1,0:T(8,128)S(1)} %get-tuple-element.83.u, ...), custom_call_target="tpu_custom_call" | custom-call | tf_op jit(solution)/shard_map/project/pallas_call | solution.py:537
  26.0 0.0 collective-permute-done.5.west
  26.0 0.0 collective-permute-done.6.east
  26.0 0.9 %sides.3 = (f32[8,8,128]{2,1,0:T(8,128)S(1)}, f32[4,8,128]{2,1,0:T(8,128)S(1)}) custom-call(s32[4]{0:T(128)S(1)} %pad_add_fusion.ids, f32[2,8,128]{2,1,0:T(8,128)S(1)} %collective-permute-done.5.west, f32[2,8,128]{2,1,0:T(8,128)S(1)} %collective-permute-done.6.east, f32[4,8,128]{2,1,0:T(8,128)S(1)} %collective-permute-done.west.west_sea.west_const, ...), custom_call_target="tpu_custom_call" | custom-call | tf_op jit(solution)/shard_map/sides/pallas_call | solution.py:537
  26.9 1.9 %collective-permute-start.7 = (f32[8,8,128]{2,1,0:T(8,128)S(1)}, f32[8,8,128]{2,1,0:T(8,128)S(1)}, u32[]{:S(2)}, u32[]{:S(2)}) collective-permute-start(f32[8,8,128]{2,1,0:T(8,128)S(1)} %get-tuple-element.92.mine), channel_id=1, source_target_pairs={{0,1},{1,0},{2,3},{3,2},{4,5},{5,4},{6,7},{7,6},{8,9},{9,8},{10,11... | collective-permute-start | bytes 98312 | tf_op jit(solution)/shard_map/ppermute | solution.py:590
  28.8 2.5 %collective-permute-start.9 = (f32[8,128]{1,0:T(8,128)S(1)}, f32[8,128]{1,0:T(8,128)S(1)}, u32[]{:S(2)}, u32[]{:S(2)}) collective-permute-start(f32[8,128]{1,0:T(8,128)S(1)} %get-tuple-element.97), channel_id=1, source_target_pairs={{0,3},{1,2},{2,1},{3,0},{4,7},{5,6},{6,5},{7,4},{8,11},{9,10},{10,... | collective-permute-start | bytes 12296 | tf_op jit(solution)/shard_map/ppermute | solution.py:587
  31.3 1.3 %base.3 = f32[4,384,128]{2,1,0:T(8,128)S(1)} custom-call(s32[4]{0:T(128)S(1)} %pad_add_fusion.ids, f32[4,384,128]{2,1,0:T(8,128)S(1)} %get-tuple-element.88.proj, f32[4,8,128]{2,1,0:T(8,128)S(1)} %get-tuple-element.93.side_proj, f32[4,8,128]{2,1,0:T(8,128)S(1)} %collective-permute-done.west.west_sea.west_const, ...), custom_call_target="tpu_custom_call" | custom-call | tf_op jit(solution)/shard_map/base/pallas_call | solution.py:537
  32.6 0.0 collective-permute-done.8.refs_0_.rest_3_
  32.6 0.9 %rows.3 = (f32[5,48,128]{2,1,0:T(8,128)S(1)}, f32[8,128]{1,0:T(8,128)S(1)}) custom-call(s32[4]{0:T(128)S(1)} %pad_add_fusion.ids, f32[5,48,128]{2,1,0:T(8,128)S(1)} %collective-permute-done.8.refs_0_.rest_3_, f32[7,48,128]{2,1,0:T(8,128)S(1)} %collective-permute-done.3.refs_0_.refs_1_.rest_2_.rest_3_), custom_call_target="tpu_custom_call" | custom-call | tf_op jit(solution)/shard_map/rows/pallas_call | solution.py:537
  33.5 0.7 %collective-permute-done.9.rest_4_ = f32[8,128]{1,0:T(8,128)S(1)} collective-permute-done((f32[8,128]{1,0:T(8,128)S(1)}, f32[8,128]{1,0:T(8,128)S(1)}, u32[]{:S(2)}, u32[]{:S(2)}) %collective-permute-start.9) | collective-permute-done | bytes 4128 | tf_op jit(solution)/shard_map/ppermute | solution.py:587
  34.2 0.0 collective-permute-done.7.theirs
  34.2 2.2 %apply.3 = (f32[384,128]{1,0:T(8,128)}, f32[384,128]{1,0:T(8,128)}, f32[384,128]{1,0:T(8,128)}, f32[384,128]{1,0:T(8,128)}) custom-call(s32[4]{0:T(128)S(1)} %pad_add_fusion.ids, f32[8]{0:T(128)S(1)} %copy-done, f32[4,384,128]{2,1,0:T(8,128)S(1)} %get-tuple-element.88.proj, f32[384,128]{1,0:T(8,128)S(1)} %get-tuple-element.60.spike, ...), custom_call_target="tpu_custom_call" | custom-call | tf_op jit(solution)/shard_map/apply/pallas_call | solution.py:537
Async XLA Ops:
  0.6 9.8 %copy-start = (f32[8]{0:T(128)S(1)}, f32[8]{0:T(128)}, u32[]{:S(2)}) copy-start(f32[8]{0:T(128)} %coup.3) | copy-start | bytes 100
  3.6 13.2 %collective-permute-start.3 = (f32[7,48,128]{2,1,0:T(8,128)S(1)}, f32[7,48,128]{2,1,0:T(8,128)S(1)}, u32[]{:S(2)}, u32[]{:S(2)}) collective-permute-start(f32[7,48,128]{2,1,0:T(8,128)S(1)} %get-tuple-element.76), channel_id=1, source_target_pairs={{0,2},{2,0},{1,3},{3,1},{4,6},{6,4},{5,7},{7,5},{8,10},{10,8},{9,1... | collective-permute-start | bytes 516104 | tf_op jit(solution)/shard_map/ppermute | solution.py:583
  7.7 4.5 %collective-permute-start = (f32[4,8,128]{2,1,0:T(8,128)S(1)}, f32[4,8,128]{2,1,0:T(8,128)S(1)}, u32[]{:S(2)}, u32[]{:S(2)}) collective-permute-start(f32[4,8,128]{2,1,0:T(8,128)S(1)} %get-tuple-element.61), channel_id=1, source_target_pairs={{0,4},{4,8},{8,12},{12,16},{16,20},{20,24},{24,28},{28,0},{1,5},{5... | collective-permute-start | bytes 49160 | tf_op jit(solution)/shard_map/ppermute | solution.py:607
  7.7 4.5 %collective-permute-start.1 = (f32[3,8,128]{2,1,0:T(8,128)S(1)}, f32[3,8,128]{2,1,0:T(8,128)S(1)}, u32[]{:S(2)}, u32[]{:S(2)}) collective-permute-start(f32[3,8,128]{2,1,0:T(8,128)S(1)} %get-tuple-element.62), channel_id=1, source_target_pairs={{4,0},{8,4},{12,8},{16,12},{20,16},{24,20},{28,24},{0,28},{5,1},{9... | collective-permute-start | bytes 36872 | tf_op jit(solution)/shard_map/ppermute | solution.py:608
  13.1 7.0 %collective-permute-start.2 = (f32[8,8,128]{2,1,0:T(8,128)S(1)}, f32[8,8,128]{2,1,0:T(8,128)S(1)}, u32[]{:S(2)}, u32[]{:S(2)}) collective-permute-start(f32[8,8,128]{2,1,0:T(8,128)S(1)} %get-tuple-element.68.mine), channel_id=1, source_target_pairs={{0,1},{1,0},{2,3},{3,2},{4,5},{5,4},{6,7},{7,6},{8,9},{9,8},{10,11... | collective-permute-start | bytes 98312 | tf_op jit(solution)/shard_map/ppermute | solution.py:590
  14.8 5.4 %collective-permute-start.4 = (f32[8,128]{1,0:T(8,128)S(1)}, f32[8,128]{1,0:T(8,128)S(1)}, u32[]{:S(2)}, u32[]{:S(2)}) collective-permute-start(f32[8,128]{1,0:T(8,128)S(1)} %get-tuple-element.79), channel_id=1, source_target_pairs={{0,3},{1,2},{2,1},{3,0},{4,7},{5,6},{6,5},{7,4},{8,11},{9,10},{10,... | collective-permute-start | bytes 12296 | tf_op jit(solution)/shard_map/ppermute | solution.py:587
  21.8 10.8 %collective-permute-start.8 = (f32[5,48,128]{2,1,0:T(8,128)S(1)}, f32[5,48,128]{2,1,0:T(8,128)S(1)}, u32[]{:S(2)}, u32[]{:S(2)}) collective-permute-start(f32[5,48,128]{2,1,0:T(8,128)S(1)} %get-tuple-element.94), channel_id=1, source_target_pairs={{0,2},{2,0},{1,3},{3,1},{4,6},{6,4},{5,7},{7,5},{8,10},{10,8},{9,1... | collective-permute-start | bytes 368648 | tf_op jit(solution)/shard_map/ppermute | solution.py:583
  21.9 4.1 %collective-permute-start.5 = (f32[2,8,128]{2,1,0:T(8,128)S(1)}, f32[2,8,128]{2,1,0:T(8,128)S(1)}, u32[]{:S(2)}, u32[]{:S(2)}) collective-permute-start(f32[2,8,128]{2,1,0:T(8,128)S(1)} %get-tuple-element.89), channel_id=1, source_target_pairs={{0,4},{4,8},{8,12},{12,16},{16,20},{20,24},{24,28},{28,0},{1,5},{5... | collective-permute-start | bytes 24584 | tf_op jit(solution)/shard_map/ppermute | solution.py:676
  22.0 4.1 %collective-permute-start.6 = (f32[2,8,128]{2,1,0:T(8,128)S(1)}, f32[2,8,128]{2,1,0:T(8,128)S(1)}, u32[]{:S(2)}, u32[]{:S(2)}) collective-permute-start(f32[2,8,128]{2,1,0:T(8,128)S(1)} %get-tuple-element.90), channel_id=1, source_target_pairs={{4,0},{8,4},{12,8},{16,12},{20,16},{24,20},{28,24},{0,28},{5,1},{9... | collective-permute-start | bytes 24584 | tf_op jit(solution)/shard_map/ppermute | solution.py:677
  26.9 7.3 %collective-permute-start.7 = (f32[8,8,128]{2,1,0:T(8,128)S(1)}, f32[8,8,128]{2,1,0:T(8,128)S(1)}, u32[]{:S(2)}, u32[]{:S(2)}) collective-permute-start(f32[8,8,128]{2,1,0:T(8,128)S(1)} %get-tuple-element.92.mine), channel_id=1, source_target_pairs={{0,1},{1,0},{2,3},{3,2},{4,5},{5,4},{6,7},{7,6},{8,9},{9,8},{10,11... | collective-permute-start | bytes 98312 | tf_op jit(solution)/shard_map/ppermute | solution.py:590
  28.8 5.4 %collective-permute-start.9 = (f32[8,128]{1,0:T(8,128)S(1)}, f32[8,128]{1,0:T(8,128)S(1)}, u32[]{:S(2)}, u32[]{:S(2)}) collective-permute-start(f32[8,128]{1,0:T(8,128)S(1)} %get-tuple-element.97), channel_id=1, source_target_pairs={{0,3},{1,2},{2,1},{3,0},{4,7},{5,6},{6,5},{7,4},{8,11},{9,10},{10,... | collective-permute-start | bytes 12296 | tf_op jit(solution)/shard_map/ppermute | solution.py:587

commit v6 on v5

--- a/solution.py
+++ b/solution.py
@@ -83,13 +83,24 @@
     return jnp.where(row == 0, low, high)
 
 
+def by_side(ids, near, far, j):
+    even = ids[4] == 0
+    return jnp.where(even, far[j], near[j]), jnp.where(even, near[j], far[j])
+
+
+def to_pairs(ids, near, far, j, to_east, to_west):
+    even = ids[4] == 0
+    near[j] = jnp.where(even, to_east, to_west)
+    far[j] = jnp.where(even, to_west, to_east)
+
+
 def row_choices(pair, rows, lat):
     return [jnp.where(lat == 0, rows - 1, 0)] if pair else [0, rows - 1]
 
 
 def pack_kernel(dims, ids, *refs):
     levels, rows, cols, half, pair = dims
-    sources, (to_east, to_west, nn_late), rest = refs[:9], refs[9:12], refs[12:]
+    coup, sources, (near, far, nn_late, coupled), rest = refs[0], refs[1:10], refs[10:14], refs[14:]
     count = 1 if pair else 2
     lat_msgs, copies, sems = rest[:count], rest[count : count + 9], rest[-1]
     moves = [pltpu.make_async_copy(a, b, sems.at[i]) for i, (a, b) in enumerate(zip(sources, copies))]
@@ -98,19 +109,23 @@
     t, s, u, v, sea, east, north, flags, inverse = copies
     lane = iota((rows, cols), 1)
     fields = (t, s, u, v)
+    index = iota((rows, cols), 0)
+    value = jnp.zeros((rows, cols), f32)
+    for y in range(rows):
+        value = jnp.where(index == y, coup[y], value)
+    coupled[...] = value
     for move in moves:
         move.wait()
     pairs = ((t, s, 2), (u, v, 2), (sea, east, 2), (flags.at[1], flags.at[0], 1))
     packed = [edge_columns(levels, rows, x, y, pieces) for x, y, pieces in pairs]
     for j in range(2):
-        to_east[j], to_west[j] = packed[j]
+        to_pairs(ids, near, far, j, *packed[j])
     wet_speed, flag = packed[2][0], packed[3][0]
     wet, speed = wet_speed, turn(wet_speed, half)
     zonal = branches(jnp.round(flag).astype(jnp.int32))[0]
     nexts = [wet * (speed * z - diffusion) for z in (zonal, turn(zonal, half))]
-    to_east[2] = jnp.where(lane < half, wet, turn(nexts[0], half))
-    to_east[3] = nexts[1]
-    to_west[2] = packed[2][1]
+    to_pairs(ids, near, far, 2, jnp.where(lane < half, wet, turn(nexts[0], half)), packed[2][1])
+    to_pairs(ids, near, far, 3, nexts[1], nexts[1])
     for which, row in enumerate(row_choices(pair, rows, ids[0])):
         msg = lat_msgs[which]
         for j, x in enumerate(fields):
@@ -167,15 +182,14 @@
     )
 
 
-def coef_kernel(dims, sea, east, north, flags, west_const, east_const, spike, spike_packed, out, factor, beside):
-    levels, rows, cols, half, pair = dims
+def coef_kernel(step, dims, ids, sea, east, north, flags, near, far, spike, spike_packed, out, factor, *beside):
+    levels, rows, cols, half, _ = dims
     lane, row = iota((rows, cols), 1), iota((rows, cols), 0)
-    sea_side = east_const[2]
-    sides = (west_const[3], west_const[2])
-
+    west_const, sea_side = by_side(ids, near, far, 2)
+    next_side = west_const if step else by_side(ids, near, far, 3)[0]
     spk = spike_packed[...]
-    spike_west = jnp.where(lane < half, west_const[2], 0.0) * spk
-    spike_east = jnp.where(lane < half, east_const[2], 0.0) * spk
+    spike_west = jnp.where(lane < half, west_const, 0.0) * spk
+    spike_east = jnp.where(lane < half, sea_side, 0.0) * spk
 
     def one(k, carry):
         wet = level(sea, k, rows).astype(f32)
@@ -187,47 +201,47 @@
         mid = level(spike, k, rows)
         west, east_ = insert(lane, mid, turn(spike_west, cols - k), turn(spike_east, cols - 1 - k))
         south, north_ = inner(row, mid)
-        for j, value in enumerate((east_, west, north_, south)):
-            beside[j, here, :] = value
-        for step in (1, 0):
-            zonal, merid = branches(level(flags.at[step], k, rows))
-            speed_z, speed_m = speed_e * zonal, speed_n * merid
-            east_own = part * (speed_e - speed_z + diffusion) * sea_east
-            next_west = jnp.where(
-                lane == 0, turn(sides[step], 2 * cols - step * half - k), turn(wet * (speed_z - diffusion), 1)
-            )
-            west_own = part * next_west
-            north_own = part * (speed_n - speed_m + diffusion) * sea_north
-            next_south = jnp.where(row == 0, 1.0, pltpu.roll(wet * (speed_m - diffusion), 1, 0))
-            south_own = part * next_south
-            for j, value in enumerate((east_own, west_own, north_own, south_own)):
-                out[step, j, here, :] = value
-            inside_n = jnp.where(row == rows - 1, 0.0, north_own)
-            inside_s = jnp.where(row == 0, 0.0, south_own)
-            factor[step, 0, here, :] = mid * (1.0 + ((west_own - east_own) + (inside_s - inside_n)))
-            factor[step, 1, here, :] = east_own * east_
-            factor[step, 2, here, :] = -west_own * west
-            factor[step, 3, here, :] = inside_n * north_
-            factor[step, 4, here, :] = -inside_s * south
+        for ref in beside:
+            for j, value in enumerate((east_, west, north_, south)):
+                ref[j, here, :] = value
+        zonal, merid = branches(level(flags.at[step], k, rows))
+        speed_z, speed_m = speed_e * zonal, speed_n * merid
+        east_own = part * (speed_e - speed_z + diffusion) * sea_east
+        next_west = jnp.where(
+            lane == 0, turn(next_side, 2 * cols - step * half - k), turn(wet * (speed_z - diffusion), 1)
+        )
+        west_own = part * next_west
+        north_own = part * (speed_n - speed_m + diffusion) * sea_north
+        next_south = jnp.where(row == 0, 1.0, pltpu.roll(wet * (speed_m - diffusion), 1, 0))
+        south_own = part * next_south
+        for j, value in enumerate((east_own, west_own, north_own, south_own)):
+            out[j, here, :] = value
+        inside_n = jnp.where(row == rows - 1, 0.0, north_own)
+        inside_s = jnp.where(row == 0, 0.0, south_own)
+        factor[0, here, :] = mid * (1.0 + ((west_own - east_own) + (inside_s - inside_n)))
+        factor[1, here, :] = east_own * east_
+        factor[2, here, :] = -west_own * west
+        factor[3, here, :] = inside_n * north_
+        factor[4, here, :] = -inside_s * south
         return carry
 
     each_level(levels, one, ())
 
 
 def coriolis_of(dims, ids):
-    levels, rows, cols, half, pair = dims
+    _, rows, cols, _, _ = dims
     index = (ids[0] * rows + iota((rows, cols), 0)).astype(f32)
-    return 0.2 + 0.6 * (index + 0.5) / (rows * ids[3]).astype(f32)
-
-
-def base_kernel(dims, step, ids, proj, side_proj, west_const, east_const, coef, out):
-    levels, rows, cols, half, pair = dims
+    return 0.2 + 0.6 * (index + 0.5) / (rows * ids[3])
+
+
+def base_kernel(dims, ids, proj, side_proj, near, far, coef, out):
+    levels, rows, cols, half, _ = dims
     lane, row = iota((rows, cols), 1), iota((rows, cols), 0)
     parts = []
     for p in range(2):
         line = []
-        for side, const in enumerate((west_const, east_const)):
-            wet = jnp.where(lane < half, const[2], turn(const[2], half))
+        for side, const in enumerate(by_side(ids, near, far, 2)):
+            wet = jnp.where(lane < half, const, turn(const, half))
             line.append(wet * side_proj[2 * side + p])
         parts.append(jnp.concatenate(line, axis=1))
     source, target = iota((2 * cols, 2 * cols), 0), iota((2 * cols, 2 * cols), 1)
@@ -244,9 +258,9 @@
     def one(j, below):
         k = levels - 1 - j
         here = level_at(k, rows)
-        east_own, west_own = coef[step, 0, here, :], coef[step, 1, here, :]
-        north_own = jnp.where(top, 0.0, coef[step, 2, here, :])
-        south_own = jnp.where(bottom, 0.0, coef[step, 3, here, :])
+        east_own, west_own = coef[0, here, :], coef[1, here, :]
+        north_own = jnp.where(top, 0.0, coef[2, here, :])
+        south_own = jnp.where(bottom, 0.0, coef[3, here, :])
         mids, around = [], []
         for f in range(4):
             w = proj[f, here, :]
@@ -270,32 +284,38 @@
     each_level(levels, one, jnp.zeros((rows, cols), f32))
 
 
-def rows_kernel(dims, ids, *refs):
-    levels, rows, cols, half, pair = dims
+def rows_kernel(first, dims, ids, *refs):
+    levels, _, cols, _, pair = dims
     count = 1 if pair else 2
-    new, const, outs, lines, (scratch,) = (refs[i * count : (i + 1) * count] for i in range(5))
-    eye = (iota((levels, levels), 0) == iota((levels, levels), 1)).astype(bf16)
-    pick = (iota((levels, cols), 0) == ids[2]).astype(bf16)
+    new, const, *refs = (refs[i * count : (i + 1) * count] for i in range(len(refs) // count + 1))
+    turned_high, turned_low, thin = refs[2:5] if first else refs[:3]
+    outs, lines = refs[:2] if first else refs[3:5]
+    (scratch,) = refs[5]
     at_edge = pl.ds(ids[2], 1)
     for h in range(count):
-        block = split(const[h][6][:, :levels])
-        turned = tuple(dot(eye, piece, ((1,), (1,))).astype(bf16) for piece in block)
-        scratch[4] = dot(turned[0], pick) + dot(turned[1], pick)
-        for p in range(2):
-            both = dot3(turned, split(jnp.concatenate([new[h][2 * p], new[h][2 * p + 1]], axis=1)))
-            scratch[2 * p] = both[:, :cols]
-            scratch[2 * p + 1] = both[:, cols:]
+        if first:
+            eye = (iota((levels, levels), 0) == iota((levels, levels), 1)).astype(bf16)
+            pick = (iota((levels, cols), 0) == ids[2]).astype(bf16)
+            turned = tuple(dot(eye, piece, ((1,), (1,))).astype(bf16) for piece in split(const[h][6][:, :levels]))
+            turned_high[h][...], turned_low[h][...] = turned
+            thin[h][...] = dot(turned[0], pick) + dot(turned[1], pick)
+        turned = (turned_high[h][...], turned_low[h][...])
+        both = dot3(turned, split(jnp.concatenate([new[h][f] for f in range(4)], axis=1)))
+        for f in range(4):
+            scratch[f] = both[:, f * cols : (f + 1) * cols]
         lines[h][...] = jnp.zeros_like(lines[h])
         wet = const[h][4]
-        for j in range(5):
+        for j in range(4):
             lines[h][pl.ds(j, 1), :] = scratch[j, at_edge, :]
             outs[h][j] = wet * scratch[j]
-
-
-def project_kernel(dims, setup, ids, t, s, u, v, sea, *rest):
+        lines[h][pl.ds(4, 1), :] = thin[h][at_edge, :]
+        outs[h][4] = wet * thin[h][...]
+
+
+def project_kernel(setup, dims, ids, t, s, u, v, sea, *rest):
     levels, rows, cols, half, pair = dims
     if setup:
-        inverse, coup, proj, planes, *rest = rest
+        inverse, coupled, proj, planes, *rest = rest
         lat_out, (spike, w_high, w_low, p_high, p_low, spike_packed, corner, b_plane, cells, wide) = rest[:-10], rest[-10:]
         n = levels * rows
         for y in range(rows):
@@ -319,7 +339,7 @@
             spike_packed[pl.ds(y, 1), pl.ds(0, levels)] = line
             spike_packed[pl.ds(y, 1), pl.ds(half, levels)] = line
     else:
-        coup, corner, b_plane, w_high, w_low, proj, planes, *lat_out = rest
+        coupled, corner, b_plane, w_high, w_low, proj, planes, *lat_out = rest
     w = (w_high[...], w_low[...])
     for f, (x, y) in enumerate(((t, s), (u, v))):
         both = dot3(w, split(jnp.concatenate([x[...], y[...]], axis=1)))
@@ -354,11 +374,7 @@
     sums = [sums[0], sums[1], b_plane[...]]
     for j in range(3):
         planes[4 + j] = sums[j]
-    lane_row = iota((rows, cols), 0)
-    coupled = jnp.zeros((rows, cols), f32)
-    for y in range(rows):
-        coupled = jnp.where(lane_row == y, coup[y], coupled)
-    lines = [planes[f] for f in range(4)] + [sums[1], sums[2], corner[...], coupled]
+    lines = [planes[f] for f in range(4)] + [sums[1], sums[2], corner[...], coupled[...]]
     for which, row in enumerate(row_choices(pair, rows, ids[0])):
         for j, value in enumerate(lines):
             if pair:
@@ -368,11 +384,12 @@
             lat_out[which][pl.ds(j, 1), :] = line
 
 
-def side_kernel(dims, ids, west, east, west_sea, east_sea, planes, corner, spike_packed, p_high, p_low, msg, proj):
-    levels, rows, cols, half, pair = dims
+def side_kernel(dims, ids, near, far, near_const, far_const, planes, corner, spike_packed, p_high, p_low, msg, proj):
+    _, rows, cols, half, _ = dims
     lane = iota((rows, cols), 1)
     row = iota((rows, cols), 0)
-    packed = (west[0], west[1], east[0], east[1])
+    (west0, east0), (west1, east1) = (by_side(ids, near, far, j) for j in range(2))
+    packed = (west0, west1, east0, east1)
     chunks = []
     for y in range(rows):
         chunks.append(jnp.concatenate([jnp.where(row == y, x, 0.0) for x in packed], axis=0))
@@ -385,8 +402,8 @@
     edge = ids[2]
     misc = jnp.zeros((rows, cols), f32)
     spk = spike_packed[...]
-    for side, wet in enumerate((west_sea, east_sea)):
-        wet = jnp.where(lane < half, wet[2], 0.0)
+    for side, wet in enumerate(by_side(ids, near_const, far_const, 2)):
+        wet = jnp.where(lane < half, wet, 0.0)
         for p in range(2):
             value = out[(2 * side + p) * rows : (2 * side + p + 1) * rows]
             for i in range(2):
@@ -400,24 +417,22 @@
     msg[7] = jnp.where(lane == CORNER_LANE, corner[...], misc)
 
 
-def apply_kernel(dims, step, final, ids, coup, proj, spike, mine, theirs, base, coef, factor, beside, *rest):
-    levels, rows, cols, half, pair = dims
+def apply_kernel(step, final, dims, ids, coupled, proj, spike, mine, theirs, base, coef, factor, beside, *rest):
+    levels, rows, cols, _, pair = dims
     count = 1 if pair else 2
     row_proj, row_line, row_const, row_late, row_far = (rest[i * count : (i + 1) * count] for i in range(5))
     rest = rest[5 * count :]
     if final:
         outs = rest
     else:
-        late_out, outs, (to_east, to_west), lat_msgs = rest[0], rest[1:5], rest[5:7], rest[7:]
+        late_out, outs, (to_near, to_far), lat_msgs = rest[0], rest[1:5], rest[5:7], rest[7:]
     lat, depth, parts = ids[0], ids[1], ids[3]
     lane = iota((rows, cols), 1)
     row = iota((rows, cols), 0)
     has_north = jnp.where(lat < parts - 1, 1.0, 0.0)
     has_south = jnp.where(lat > 0, 1.0, 0.0)
 
-    c = jnp.zeros((rows, cols), f32)
-    for y in range(rows):
-        c = jnp.where(row == y, coup[y], c)
+    c = coupled[...]
     own_corner = lane_of(mine[7], CORNER_LANE)
     other_corner = lane_of(theirs[7], CORNER_LANE)
     scaled = c / (1.0 - c * c * own_corner * other_corner)
@@ -463,7 +478,7 @@
         moved = [[side * plane for side, plane in zip(sides, around[f])] for f in (2, 3)]
         below = below + ((moved[0][1] - moved[0][0]) + (moved[1][3] - moved[1][2]))
         buoyancy = push * below
-        factors = [factor[step, j, here, :] for j in range(5)]
+        factors = [factor[j, here, :] for j in range(5)]
         for f in range(2):
             q = base[f, here, :] + factors[0] * carried[f]
             q = q + (
@@ -488,10 +503,10 @@
         take = lambda ref: take_row(ref, at, levels, rows)
         beyond = row_solved[h]
         if pair:
-            own = jnp.where(lat == 0, coef[step, 2, pl.ds(rows - 1, levels, stride=rows), :],
-                            coef[step, 3, pl.ds(0, levels, stride=rows), :])
+            own = jnp.where(lat == 0, coef[2, pl.ds(rows - 1, levels, stride=rows), :],
+                            coef[3, pl.ds(0, levels, stride=rows), :])
         else:
-            own = coef[step, 2 + h, pl.ds(at, levels, stride=rows), :]
+            own = coef[2 + h, pl.ds(at, levels, stride=rows), :]
         late = row_const[h][5] if step else row_late[h][4]
         here_north = row_const[h][4]
         if pair:
@@ -528,20 +543,27 @@
                 lat_msgs[which][f] = take_row(outs[f], at, levels, rows)
             lat_msgs[which][4] = late_out[...]
         for p in range(2):
-            to_east[p], to_west[p] = edge_columns(levels, rows, outs[2 * p], outs[2 * p + 1], 2)
-
-
-def call(kernel, outs, args, smem=(0,), scratch=(), name=None, hbm=()):
-    places = [pltpu.SMEM if i in smem else pltpu.HBM if i in hbm else pltpu.VMEM for i in range(len(args))]
-    specs = [pl.BlockSpec(memory_space=place) for place in places]
+            to_pairs(ids, to_near, to_far, p, *edge_columns(levels, rows, outs[2 * p], outs[2 * p + 1], 2))
+
+
+def places(levels):
+    lat, depth, lon = (lax.axis_index(a) for a in ("lat", "depth", "lon"))
+    return lat, depth, (levels - 1) * (1 - depth), lax.axis_size("lat"), lax.rem(lon, 2)
+
+
+def call(kernel, dims, outs, args, smem=(), scratch=(), hbm=()):
+    spaces = [pltpu.SMEM if i in smem else pltpu.HBM if i in hbm else pltpu.VMEM for i in range(len(args))]
+
+    def run(*refs):
+        kernel(dims, places(dims[0]), *refs)
+
     return pl.pallas_call(
-        kernel,
+        run,
         out_shape=[jax.ShapeDtypeStruct(shape, kind) for shape, kind in outs],
-        in_specs=specs,
+        in_specs=[pl.BlockSpec(memory_space=space) for space in spaces],
         out_specs=[pl.BlockSpec(memory_space=pltpu.VMEM)] * len(outs),
         scratch_shapes=list(scratch),
         compiler_params=pltpu.CompilerParams(vmem_limit_bytes=VMEM_BYTES),
-        name=name,
     )(*args)
 
 
@@ -564,16 +586,15 @@
     dims = (levels, rows, cols, half, pair)
     count = 1 if pair else 2
     n = levels * rows
-    lat, depth = lax.axis_index("lat"), lax.axis_index("depth")
-    ids = jnp.stack([lat, depth, (levels - 1) * (1 - depth), jnp.int32(lats)]).astype(jnp.int32)
     flat = lambda x: x.reshape(x.shape[:-3] + (n, cols))
     sea, east, north, flags = flat(sea_mask), flat(east_speed), flat(north_speed), flat(branch_flags)
     state = [flat(x) for x in (adj_temp, adj_salt, adj_zonal, adj_merid)]
     plane = (rows, cols)
     grid = (levels, cols)
 
-    ring = [(i, (i + 1) % lons) for i in range(lons)]
-    back = [(b, a) for a, b in ring]
+    assert lons % 2 == 0
+    close = [(i, i ^ 1) for i in range(lons)]
+    apart = [(i, (i + 1 if i % 2 else i - 1) % lons) for i in range(lons)]
     up = [(i, i + 1) for i in range(lats - 1)]
     down = [(b, a) for a, b in up]
 
@@ -591,90 +612,87 @@
 
     sources = (*state, sea, east, north, flags, block_inverse)
     sources = tuple(pltpu.with_memory_space_constraint(x, pltpu.HBM) for x in sources)
-    to_east, to_west, late, *rest = call(
-        functools.partial(pack_kernel, dims),
-        [((4,) + plane, f32), ((3,) + plane, f32), (grid, f32)]
+    near, far, late, coupled, *rest = call(
+        pack_kernel,
+        dims,
+        [((4,) + plane, f32)] * 2
+        + [(grid, f32), (plane, f32)]
         + [((7,) + grid, f32)] * count
         + [(x.shape, x.dtype) for x in sources],
-        (ids, *sources),
-        scratch=(pltpu.SemaphoreType.DMA((9,)),),
-        name="pack",
-        hbm=range(1, 10),
+        (pltpu.with_memory_space_constraint(coupling, pltpu.HBM), *sources),
+        (0,),
+        (pltpu.SemaphoreType.DMA((9,)),),
+        range(1, 10),
     )
     lat_msgs, rest = rest[:count], rest[count:]
     state, (sea, east, north, flags, block_inverse) = rest[:4], rest[4:]
-    row_const = to_lat(lat_msgs, False)
-    west_const = lax.ppermute(to_east, "lon", ring)
-    east_const = lax.ppermute(to_west, "lon", back)
-    row_new, west, east_in = row_const, west_const, east_const
+    row_const = row_new = to_lat(lat_msgs, False)
+    near_const = near = lax.ppermute(near, "lon", close)
+    far_const = far = lax.ppermute(far, "lon", apart)
 
     for step in reversed(range(STEPS)):
         first = step == STEPS - 1
         outs = [((4, n, cols), f32), ((7,) + plane, f32)] + [(plane, f32)] * count
         if first:
             outs += [((n, cols), f32)] + [((n, n), bf16)] * 2 + [((rows * cols, cols), bf16)] * 2 + [(plane, f32)] * 3
-            args = (ids, *state, sea, block_inverse, coupling)
-            smem = (0, 7)
+            args = (*state, sea, block_inverse, coupled)
             scratch = (pltpu.VMEM((n, levels), f32), pltpu.VMEM((rows, cols, cols), f32))
         else:
-            args = (ids, *state, sea, coupling, corner, b_plane, w_high, w_low)
-            smem = (0, 6)
+            args = (*state, sea, coupled, corner, b_plane, w_high, w_low)
             scratch = ()
-        proj, planes, *more = call(
-            functools.partial(project_kernel, dims, first), outs, args, smem, scratch, name="project"
-        )
+        proj, planes, *more = call(functools.partial(project_kernel, first), dims, outs, args, (), scratch)
         far_msgs = more[:count]
         if first:
             spike, w_high, w_low, p_high, p_low, spike_packed, corner, b_plane = more[count:]
         row_far = to_lat(far_msgs, True)
         mine, side_proj = call(
-            functools.partial(side_kernel, dims),
+            side_kernel,
+            dims,
             [((8,) + plane, f32), ((4,) + plane, f32)],
-            (ids, west, east_in, west_const, east_const, planes, corner, spike_packed, p_high, p_low),
-            name="sides",
+            (near, far, near_const, far_const, planes, corner, spike_packed, p_high, p_low),
         )
         theirs = to_depth(mine)
+        coef, factor, *more = call(
+            functools.partial(coef_kernel, step),
+            dims,
+            [((4, n, cols), f32), ((5, n, cols), f32)] + [((4, n, cols), f32)] * first,
+            (sea, east, north, flags, near_const, far_const, spike, spike_packed),
+        )
         if first:
-            coef, factor, beside = call(
-                functools.partial(coef_kernel, dims),
-                [((STEPS, 4, n, cols), f32), ((STEPS, 5, n, cols), f32), ((4, n, cols), f32)],
-                (sea, east, north, flags, west_const, east_const, spike, spike_packed),
-                (),
-                name="coef",
-            )
-        (base,) = call(
-            functools.partial(base_kernel, dims, step),
-            [((4, n, cols), f32)],
-            (ids, proj, side_proj, west_const, east_const, coef),
-            name="base",
+            (beside,) = more
+        (base,) = call(base_kernel, dims, [((4, n, cols), f32)], (proj, side_proj, near_const, far_const, coef))
+        block = ((levels, levels), bf16)
+        rows_out = call(
+            functools.partial(rows_kernel, first),
+            dims,
+            [((5,) + grid, f32)] * count
+            + [(plane, f32)] * count
+            + ([block] * (2 * count) + [(grid, f32)] * count) * first,
+            (*row_new, *row_const, *(() if first else row_block)),
+            scratch=(pltpu.VMEM((4,) + grid, f32),),
         )
-        rows_out = call(
-            functools.partial(rows_kernel, dims),
-            [((5,) + grid, f32)] * count + [(plane, f32)] * count,
-            (ids, *row_new, *row_const),
-            scratch=(pltpu.VMEM((5,) + grid, f32),),
-            name="rows",
-        )
+        if first:
+            row_block = rows_out[2 * count :]
+        rows_out = rows_out[: 2 * count]
         final = step == 0
         outs, extra = [((n, cols), f32)] * 4, ()
         if not final:
             outs = outs + [((2,) + plane, f32)] * 2 + [((5,) + grid, f32)] * count
             extra = (late,)
         result = call(
-            functools.partial(apply_kernel, dims, step, final),
+            functools.partial(apply_kernel, step, final),
+            dims,
             outs,
             (
-                ids, coupling, proj, spike, mine, theirs, base, coef, factor, beside,
+                coupled, proj, spike, mine, theirs, base, coef, factor, beside,
                 *rows_out, *row_const, *row_new, *row_far, *extra,
             ),
-            (0, 1),
-            name="apply",
         )
         state = result[:4]
         if not final:
             row_new = to_lat(result[6:], False)
-            west = lax.ppermute(result[4], "lon", ring)
-            east_in = lax.ppermute(result[5], "lon", back)
+            near = lax.ppermute(result[4], "lon", close)
+            far = lax.ppermute(result[5], "lon", apart)
     return tuple(x.reshape(levels, rows, cols) for x in state)
 
 
@@ -697,6 +715,5 @@
         P("depth", "lat", "lon"),
         P("depth", "lat", "lon"),
     )
-    return jax.shard_map(
-        on_device, mesh=mesh, in_specs=in_specs, out_specs=out_specs, check_vma=False
-    )
+
+    return jax.shard_map(on_device, mesh=mesh, in_specs=in_specs, out_specs=out_specs, check_vma=False)

time: 36.5 us -> 33.5 us (0.918)
  Pallas kernels: 16.7 us -> 11.4 us
  waiting for transfers between devices: 3.26 us -> 6.23 us
  starting transfers between devices: 15.6 us -> 14.9 us
    pallas_call x12 -> x13, Pallas kernels: 16.7 us -> 11.4 us  [call(): pl.pallas_call(run, out_shape=[jax.ShapeDtypeStruct(shape, kind) for shap...]
    ppermute x4, waiting for transfers between devices: 0.01 us -> 1.52 us  [the longest x1 1.27 us: on_device(): far = lax.ppermute(result[5], 'lon', apart)]
    ppermute x2, waiting for transfers between devices: 3.24 us -> 4.01 us  [to_lat(): return [lax.ppermute(m, ('lat', 'depth'), r) for m, r in zip(msgs, both)]]
    ppermute x4, starting transfers between devices: 5.33 us -> 4.58 us  [the longest x1 2.56 us: on_device(): far_const = far = lax.ppermute(far, 'lon', apart)]
    ppermute x2, waiting for transfers between devices: 0.01 us -> 0.7 us  [to_lat(): return [lax.ppermute(m, 'lat', r) for m, r in zip(msgs, routes)]]
    ppermute x2, starting transfers between devices: 2.49 us -> 3.04 us  [to_lat(): return [lax.ppermute(m, ('lat', 'depth'), r) for m, r in zip(msgs, both)]]
    ppermute x2, starting transfers between devices: 3.54 us -> 3.06 us  [to_depth(): lax.ppermute(msg, 'depth', [(d, depths - 1 - d) for d in range(depths)])]
  transfers between devices with their start and end apart: 10 -> 10, of which waited for: 2 -> 5; matrix products, arithmetic and copies ran while one was open for 0% -> 0% of each run, Pallas kernels for 27% -> 17%
where the time goes in v6:
time: 33.5 us; the launch traced here: 33.3 us
  starting transfers between devices  14.9 us (44%)
  Pallas kernels  11.4 us (34%)
  waiting for transfers between devices  6.23 us (19%)
  between operations  0.74 us (2%)
    pallas_call x13, Pallas kernels, call(): pl.pallas_call(run, out_shape=[jax.ShapeDtypeStruct(shape, kind) for shap...  11.4 us
    ppermute x2, starting transfers between devices, to_lat(): return [lax.ppermute(m, 'lat', r) for m, r in zip(msgs, routes)]  4.2 us
    ppermute x2, waiting for transfers between devices, to_lat(): return [lax.ppermute(m, ('lat', 'depth'), r) for m, r in zip(msgs, both)]  4.01 us
    ppermute x2, starting transfers between devices, to_depth(): lax.ppermute(msg, 'depth', [(d, depths - 1 - d) for d in range(depths)])  3.06 us
    ppermute x2, starting transfers between devices, to_lat(): return [lax.ppermute(m, ('lat', 'depth'), r) for m, r in zip(msgs, both)]  3.04 us
    ppermute x1, starting transfers between devices, on_device(): far_const = far = lax.ppermute(far, 'lon', apart)  2.56 us
    ppermute x1, starting transfers between devices, on_device(): far = lax.ppermute(result[5], 'lon', apart)  1.95 us
    ppermute x1, waiting for transfers between devices, on_device(): far = lax.ppermute(result[5], 'lon', apart)  1.27 us
  transfers between devices with their start and end apart: 10, of which 5 were waited for; matrix products, arithmetic and copies ran while one was open for 0% of the time, Pallas kernels for 17%

profile of v6, /device:TPU:0, one launch (start us, length us, event | category | flops | bytes accessed | tf_op | source)
XLA Modules:
  0.0 33.3 jit_solution(10116604846719551426)
XLA Ops:
  0.6 3.0 %shard_map.129 = (f32[4,8,128]{2,1,0:T(8,128)S(1)}, f32[4,8,128]{2,1,0:T(8,128)S(1)}, f32[48,128]{1,0:T(8,128)S(1)}, f32[8,128]{1,0:T(8,128)S(1)}, f32[7,48,128]...) custom-call(f32[8]{0:T(128)} %refs_0_.1, ...), custom_call_target="tpu_custom_call" | custom-call | tf_op jit(solution)/shard_map/pallas_call | solution.py:560
  3.7 4.1 %collective-permute-start.3 = (f32[7,48,128]{2,1,0:T(8,128)S(1)}, f32[7,48,128]{2,1,0:T(8,128)S(1)}, u32[]{:S(2)}, u32[]{:S(2)}) collective-permute-start(f32[7,48,128]{2,1,0:T(8,128)S(1)} %get-tuple-element.83), channel_id=1, source_target_pairs={{0,2},{2,0},{1,3},{3,1},{4,6},{6,4},{5,7},{7,5},{8,10},{10,8},{9,1... | collective-permute-start | bytes 516104 | tf_op jit(solution)/shard_map/ppermute | solution.py:604
  7.8 0.0 collective-permute-start
  7.8 2.6 %collective-permute-start.1 = (f32[4,8,128]{2,1,0:T(8,128)S(1)}, f32[4,8,128]{2,1,0:T(8,128)S(1)}, u32[]{:S(2)}, u32[]{:S(2)}) collective-permute-start(f32[4,8,128]{2,1,0:T(8,128)S(1)} %get-tuple-element.69), channel_id=1, source_target_pairs={{0,28},{4,8},{8,4},{12,16},{16,12},{20,24},{24,20},{28,0},{1,29},{... | collective-permute-start | bytes 49160 | tf_op jit(solution)/shard_map/ppermute | solution.py:631
  10.4 1.2 %shard_map.130 = (f32[4,384,128]{2,1,0:T(8,128)S(1)}, f32[7,8,128]{2,1,0:T(8,128)S(1)}, f32[8,128]{1,0:T(8,128)S(1)}, f32[384,128]{1,0:T(8,128)S(1)}, bf16[384,3...) custom-call(f32[384,128]{1,0:T(8,128)S(1)} %get-tuple-element.60.ref, ...), custom_call_target="tpu_custom_call" | custom-call | tf_op jit(solution)/shard_map/pallas_call | solution.py:560
  11.6 0.0 collective-permute-done.refs_0_.refs_2_.refs_4_
  11.6 0.2 collective-permute-done.1.refs_1_.refs_3_.refs_5_
  11.9 0.3 shard_map.131
  12.2 1.6 %collective-permute-start.2 = (f32[8,8,128]{2,1,0:T(8,128)S(1)}, f32[8,8,128]{2,1,0:T(8,128)S(1)}, u32[]{:S(2)}, u32[]{:S(2)}) collective-permute-start(f32[8,8,128]{2,1,0:T(8,128)S(1)} %get-tuple-element.75.refs_3_), channel_id=1, source_target_pairs={{0,1},{1,0},{2,3},{3,2},{4,5},{5,4},{6,7},{7,6},{8,9},{9,8},{10,11... | collective-permute-start | bytes 98312 | tf_op jit(solution)/shard_map/ppermute | solution.py:611
  13.8 0.2 collective-permute-start.4
  14.0 0.5 %shard_map.132 = (f32[4,384,128]{2,1,0:T(8,128)S(1)}, f32[5,384,128]{2,1,0:T(8,128)S(1)}, f32[4,384,128]{2,1,0:T(8,128)S(1)}) custom-call(s32[384,128]{1,0:T(8,128)S(1)} %get-tuple-element.64.refs_4_.refs_0_, f32[384,128]{1,0:T(8,128)S(1)} %get-tuple-element.77.refs_1_, f32[384,128]{1,0:T(8,128)S(1)} %get-tuple-element.78.refs_2_, ...), custom_call_target="tpu_custom_call" | custom-call | tf_op jit(solution)/shard_map/pallas_call | solution.py:560
  14.5 0.8 %shard_map.133.refs_5_ = f32[4,384,128]{2,1,0:T(8,128)S(1)} custom-call(f32[4,384,128]{2,1,0:T(8,128)S(1)} %get-tuple-element.66.refs_0_.refs_1_, f32[4,8,128]{2,1,0:T(8,128)S(1)} %get-tuple-element.76.refs_1_, f32[4,8,128]{2,1,0:T(8,128)S(1)} %collective-permute-done.refs_0_.refs_2_.refs_4_, ...), custom_call_target="tpu_custom_call" | custom-call | tf_op jit(solution)/shard_map/pallas_call | solution.py:560
  15.3 0.7 %collective-permute-done.3.refs_0_.refs_1_.refs_11_.refs_12_ = f32[7,48,128]{2,1,0:T(8,128)S(1)} collective-permute-done((f32[7,48,128]{2,1,0:T(8,128)S(1)}, f32[7,48,128]{2,1,0:T(8,128)S(1)}, u32[]{:S(2)}, u32[]{:S(2)}) %collective-permute-start.3) | collective-permute-done | bytes 172064 | tf_op jit(solution)/shard_map/ppermute | solution.py:604
  16.0 0.3 %shard_map.134 = (f32[5,48,128]{2,1,0:T(8,128)S(1)}, f32[8,128]{1,0:T(8,128)S(1)}, bf16[48,48]{1,0:T(8,128)(2,1)S(1)}, bf16[48,48]{1,0:T(8,128)(2,1)S(1)}, f32[48,128]{1,0:T(8,128)S(1)}) custom-call(f32[7,48,128]{2,1,0:T(8,128)S(1)} %collective-permute-done.3.refs_0_.refs_1_.refs_11_.refs_12_, ...), custom_call_target="tpu_custom_call" | custom-call | tf_op jit(solution)/shard_map/pallas_call | solution.py:560
  16.3 2.9 %collective-permute-done.4.refs_13_ = f32[8,128]{1,0:T(8,128)S(1)} collective-permute-done((f32[8,128]{1,0:T(8,128)S(1)}, f32[8,128]{1,0:T(8,128)S(1)}, u32[]{:S(2)}, u32[]{:S(2)}) %collective-permute-start.4) | collective-permute-done | bytes 4128 | tf_op jit(solution)/shard_map/ppermute | solution.py:608
  19.2 0.0 collective-permute-done.2.refs_4_
  19.2 1.1 %shard_map.135 = (f32[384,128]{1,0:T(8,128)S(1)}, f32[384,128]{1,0:T(8,128)S(1)}, f32[384,128]{1,0:T(8,128)S(1)}, f32[384,128]{1,0:T(8,128)S(1)}, f32[2,8,128]{2...) custom-call(f32[8,128]{1,0:T(8,128)S(1)} %get-tuple-element.59.refs_6_.refs_0_.refs_5_, ...), custom_call_target="tpu_custom_call" | custom-call | tf_op jit(solution)/shard_map/pallas_call | solution.py:560
  20.3 0.1 collective-permute-start.8
  20.4 0.1 collective-permute-start.5
  20.5 2.0 %collective-permute-start.6 = (f32[2,8,128]{2,1,0:T(8,128)S(1)}, f32[2,8,128]{2,1,0:T(8,128)S(1)}, u32[]{:S(2)}, u32[]{:S(2)}) collective-permute-start(f32[2,8,128]{2,1,0:T(8,128)S(1)} %get-tuple-element.97), channel_id=1, source_target_pairs={{0,28},{4,8},{8,4},{12,16},{16,12},{20,24},{24,20},{28,0},{1,29},{... | collective-permute-start | bytes 24584 | tf_op jit(solution)/shard_map/ppermute | solution.py:695
  22.4 0.8 %shard_map.136 = (f32[4,384,128]{2,1,0:T(8,128)S(1)}, f32[7,8,128]{2,1,0:T(8,128)S(1)}, f32[8,128]{1,0:T(8,128)S(1)}) custom-call(f32[384,128]{1,0:T(8,128)S(1)} %get-tuple-element.88.refs_0_, f32[384,128]{1,0:T(8,128)S(1)} %get-tuple-element.89.refs_1_, f32[384,128]{1,0:T(8,128)S(1)} %get-tuple-element.90.refs_2_, ...), custom_call_target="tpu_custom_call" | custom-call | tf_op jit(solution)/shard_map/pallas_call | solution.py:560
  23.2 0.0 collective-permute-done.5.refs_0_
  23.2 1.3 %collective-permute-done.6.refs_1_ = f32[2,8,128]{2,1,0:T(8,128)S(1)} collective-permute-done((f32[2,8,128]{2,1,0:T(8,128)S(1)}, f32[2,8,128]{2,1,0:T(8,128)S(1)}, u32[]{:S(2)}, u32[]{:S(2)}) %collective-permute-start.6) | collective-permute-done | bytes 8224 | tf_op jit(solution)/shard_map/ppermute | solution.py:695
  24.5 0.3 shard_map.137
  24.8 1.4 %collective-permute-start.7 = (f32[8,8,128]{2,1,0:T(8,128)S(1)}, f32[8,8,128]{2,1,0:T(8,128)S(1)}, u32[]{:S(2)}, u32[]{:S(2)}) collective-permute-start(f32[8,8,128]{2,1,0:T(8,128)S(1)} %get-tuple-element.99.refs_3_), channel_id=1, source_target_pairs={{0,1},{1,0},{2,3},{3,2},{4,5},{5,4},{6,7},{7,6},{8,9},{9,8},{10,11... | collective-permute-start | bytes 98312 | tf_op jit(solution)/shard_map/ppermute | solution.py:611
  26.3 2.9 %collective-permute-start.9 = (f32[8,128]{1,0:T(8,128)S(1)}, f32[8,128]{1,0:T(8,128)S(1)}, u32[]{:S(2)}, u32[]{:S(2)}) collective-permute-start(f32[8,128]{1,0:T(8,128)S(1)} %get-tuple-element.109), channel_id=1, source_target_pairs={{0,3},{1,2},{2,1},{3,0},{4,7},{5,6},{6,5},{7,4},{8,11},{9,10},{10,... | collective-permute-start | bytes 12296 | tf_op jit(solution)/shard_map/ppermute | solution.py:608
  29.1 0.5 %shard_map.138 = (f32[4,384,128]{2,1,0:T(8,128)S(1)}, f32[5,384,128]{2,1,0:T(8,128)S(1)}) custom-call(s32[384,128]{1,0:T(8,128)S(1)} %get-tuple-element.64.refs_4_.refs_0_, f32[384,128]{1,0:T(8,128)S(1)} %get-tuple-element.77.refs_1_, f32[384,128]{1,0:T(8,128)S(1)} %get-tuple-element.78.refs_2_, s32[2,384,128]{2,1,0:T(8,128)S(1)} %get-tuple-element.79.refs_3_, ...), custom_call_target="tpu_custom_call" | custom-call | tf_op jit(solution)/shard_map/pallas_call | solution.py:560
  29.6 0.8 %shard_map.139.refs_5_ = f32[4,384,128]{2,1,0:T(8,128)S(1)} custom-call(f32[4,384,128]{2,1,0:T(8,128)S(1)} %get-tuple-element.95.refs_0_.refs_1_, f32[4,8,128]{2,1,0:T(8,128)S(1)} %get-tuple-element.100.refs_1_, f32[4,8,128]{2,1,0:T(8,128)S(1)} %collective-permute-done.refs_0_.refs_2_.refs_4_, ...), custom_call_target="tpu_custom_call" | custom-call | tf_op jit(solution)/shard_map/pallas_call | solution.py:560
  30.4 0.0 collective-permute-done.8.refs_0_.refs_12_
  30.4 0.2 shard_map.140
  30.6 1.1 %collective-permute-done.9.refs_13_ = f32[8,128]{1,0:T(8,128)S(1)} collective-permute-done((f32[8,128]{1,0:T(8,128)S(1)}, f32[8,128]{1,0:T(8,128)S(1)}, u32[]{:S(2)}, u32[]{:S(2)}) %collective-permute-start.9) | collective-permute-done | bytes 4128 | tf_op jit(solution)/shard_map/ppermute | solution.py:608
  31.7 0.0 collective-permute-done.7.refs_4_
  31.7 1.6 %shard_map.141 = (f32[384,128]{1,0:T(8,128)}, f32[384,128]{1,0:T(8,128)}, f32[384,128]{1,0:T(8,128)}, f32[384,128]{1,0:T(8,128)}) custom-call(f32[8,128]{1,0:T(8,128)S(1)} %get-tuple-element.59.refs_6_.refs_0_.refs_5_, f32[4,384,128]{2,1,0:T(8,128)S(1)} %get-tuple-element.95.refs_0_.refs_1_, f32[384,128]{1,0:T(8,128)S(1)} %get-tuple-element.67.refs_6_.refs_2_, ...), custom_call_target="tpu_custom_call" | custom-call | tf_op jit(solution)/shard_map/pallas_call | solution.py:560
Async XLA Ops:
  3.7 12.3 %collective-permute-start.3 = (f32[7,48,128]{2,1,0:T(8,128)S(1)}, f32[7,48,128]{2,1,0:T(8,128)S(1)}, u32[]{:S(2)}, u32[]{:S(2)}) collective-permute-start(f32[7,48,128]{2,1,0:T(8,128)S(1)} %get-tuple-element.83), channel_id=1, source_target_pairs={{0,2},{2,0},{1,3},{3,1},{4,6},{6,4},{5,7},{7,5},{8,10},{10,8},{9,1... | collective-permute-start | bytes 516104 | tf_op jit(solution)/shard_map/ppermute | solution.py:604
  7.8 3.8 %collective-permute-start = (f32[4,8,128]{2,1,0:T(8,128)S(1)}, f32[4,8,128]{2,1,0:T(8,128)S(1)}, u32[]{:S(2)}, u32[]{:S(2)}) collective-permute-start(f32[4,8,128]{2,1,0:T(8,128)S(1)} %get-tuple-element.68), channel_id=1, source_target_pairs={{0,4},{4,0},{8,12},{12,8},{16,20},{20,16},{24,28},{28,24},{1,5},{5... | collective-permute-start | bytes 49160 | tf_op jit(solution)/shard_map/ppermute | solution.py:630
  7.8 4.1 %collective-permute-start.1 = (f32[4,8,128]{2,1,0:T(8,128)S(1)}, f32[4,8,128]{2,1,0:T(8,128)S(1)}, u32[]{:S(2)}, u32[]{:S(2)}) collective-permute-start(f32[4,8,128]{2,1,0:T(8,128)S(1)} %get-tuple-element.69), channel_id=1, source_target_pairs={{0,28},{4,8},{8,4},{12,16},{16,12},{20,24},{24,20},{28,0},{1,29},{... | collective-permute-start | bytes 49160 | tf_op jit(solution)/shard_map/ppermute | solution.py:631
  12.2 7.1 %collective-permute-start.2 = (f32[8,8,128]{2,1,0:T(8,128)S(1)}, f32[8,8,128]{2,1,0:T(8,128)S(1)}, u32[]{:S(2)}, u32[]{:S(2)}) collective-permute-start(f32[8,8,128]{2,1,0:T(8,128)S(1)} %get-tuple-element.75.refs_3_), channel_id=1, source_target_pairs={{0,1},{1,0},{2,3},{3,2},{4,5},{5,4},{6,7},{7,6},{8,9},{9,8},{10,11... | collective-permute-start | bytes 98312 | tf_op jit(solution)/shard_map/ppermute | solution.py:611
  13.8 5.4 %collective-permute-start.4 = (f32[8,128]{1,0:T(8,128)S(1)}, f32[8,128]{1,0:T(8,128)S(1)}, u32[]{:S(2)}, u32[]{:S(2)}) collective-permute-start(f32[8,128]{1,0:T(8,128)S(1)} %get-tuple-element.86), channel_id=1, source_target_pairs={{0,3},{1,2},{2,1},{3,0},{4,7},{5,6},{6,5},{7,4},{8,11},{9,10},{10,... | collective-permute-start | bytes 12296 | tf_op jit(solution)/shard_map/ppermute | solution.py:608
  20.3 10.1 %collective-permute-start.8 = (f32[5,48,128]{2,1,0:T(8,128)S(1)}, f32[5,48,128]{2,1,0:T(8,128)S(1)}, u32[]{:S(2)}, u32[]{:S(2)}) collective-permute-start(f32[5,48,128]{2,1,0:T(8,128)S(1)} %get-tuple-element.103), channel_id=1, source_target_pairs={{0,2},{2,0},{1,3},{3,1},{4,6},{6,4},{5,7},{7,5},{8,10},{10,8},{9,1... | collective-permute-start | bytes 368648 | tf_op jit(solution)/shard_map/ppermute | solution.py:604
  20.4 2.8 %collective-permute-start.5 = (f32[2,8,128]{2,1,0:T(8,128)S(1)}, f32[2,8,128]{2,1,0:T(8,128)S(1)}, u32[]{:S(2)}, u32[]{:S(2)}) collective-permute-start(f32[2,8,128]{2,1,0:T(8,128)S(1)} %get-tuple-element.96), channel_id=1, source_target_pairs={{0,4},{4,0},{8,12},{12,8},{16,20},{20,16},{24,28},{28,24},{1,5},{5... | collective-permute-start | bytes 24584 | tf_op jit(solution)/shard_map/ppermute | solution.py:694
  20.5 4.0 %collective-permute-start.6 = (f32[2,8,128]{2,1,0:T(8,128)S(1)}, f32[2,8,128]{2,1,0:T(8,128)S(1)}, u32[]{:S(2)}, u32[]{:S(2)}) collective-permute-start(f32[2,8,128]{2,1,0:T(8,128)S(1)} %get-tuple-element.97), channel_id=1, source_target_pairs={{0,28},{4,8},{8,4},{12,16},{16,12},{20,24},{24,20},{28,0},{1,29},{... | collective-permute-start | bytes 24584 | tf_op jit(solution)/shard_map/ppermute | solution.py:695
  24.8 6.8 %collective-permute-start.7 = (f32[8,8,128]{2,1,0:T(8,128)S(1)}, f32[8,8,128]{2,1,0:T(8,128)S(1)}, u32[]{:S(2)}, u32[]{:S(2)}) collective-permute-start(f32[8,8,128]{2,1,0:T(8,128)S(1)} %get-tuple-element.99.refs_3_), channel_id=1, source_target_pairs={{0,1},{1,0},{2,3},{3,2},{4,5},{5,4},{6,7},{7,6},{8,9},{9,8},{10,11... | collective-permute-start | bytes 98312 | tf_op jit(solution)/shard_map/ppermute | solution.py:611
  26.3 5.4 %collective-permute-start.9 = (f32[8,128]{1,0:T(8,128)S(1)}, f32[8,128]{1,0:T(8,128)S(1)}, u32[]{:S(2)}, u32[]{:S(2)}) collective-permute-start(f32[8,128]{1,0:T(8,128)S(1)} %get-tuple-element.109), channel_id=1, source_target_pairs={{0,3},{1,2},{2,1},{3,0},{4,7},{5,6},{6,5},{7,4},{8,11},{9,10},{10,... | collective-permute-start | bytes 12296 | tf_op jit(solution)/shard_map/ppermute | solution.py:608

commit v7 on v6

--- a/solution.py
+++ b/solution.py
@@ -19,6 +19,7 @@
 BLOCK = 48
 VMEM_BYTES = 16 * 1024 * 1024
 f32 = jnp.float32
+CHUNKS = 3
 bf16 = jnp.bfloat16
 CORNER_LANE = 16
 
@@ -98,54 +99,68 @@
     return [jnp.where(lat == 0, rows - 1, 0)] if pair else [0, rows - 1]
 
 
-def pack_kernel(dims, ids, *refs):
+def block_shape(levels):
+    return levels // 2
+
+
+def fetch_kernel(dims, ids, *refs):
     levels, rows, cols, half, pair = dims
-    coup, sources, (near, far, nn_late, coupled), rest = refs[0], refs[1:10], refs[10:14], refs[14:]
+    coup, sources, (nn_late, coupled), rest = refs[0], refs[1:10], refs[10:12], refs[12:]
     count = 1 if pair else 2
-    lat_msgs, copies, sems = rest[:count], rest[count : count + 9], rest[-1]
+    lat_msgs, copies, (coup_here, sems) = rest[:count], rest[count : count + 9], rest[count + 9 :]
     moves = [pltpu.make_async_copy(a, b, sems.at[i]) for i, (a, b) in enumerate(zip(sources, copies))]
+    moves.append(pltpu.make_async_copy(coup, coup_here, sems.at[9]))
     for move in moves:
         move.start()
-    t, s, u, v, sea, east, north, flags, inverse = copies
-    lane = iota((rows, cols), 1)
-    fields = (t, s, u, v)
-    index = iota((rows, cols), 0)
-    value = jnp.zeros((rows, cols), f32)
-    for y in range(rows):
-        value = jnp.where(index == y, coup[y], value)
-    coupled[...] = value
+    t, s, u, v, sea, _, north, flags, inverse = copies
     for move in moves:
         move.wait()
-    pairs = ((t, s, 2), (u, v, 2), (sea, east, 2), (flags.at[1], flags.at[0], 1))
-    packed = [edge_columns(levels, rows, x, y, pieces) for x, y, pieces in pairs]
-    for j in range(2):
-        to_pairs(ids, near, far, j, *packed[j])
-    wet_speed, flag = packed[2][0], packed[3][0]
-    wet, speed = wet_speed, turn(wet_speed, half)
-    zonal = branches(jnp.round(flag).astype(jnp.int32))[0]
-    nexts = [wet * (speed * z - diffusion) for z in (zonal, turn(zonal, half))]
-    to_pairs(ids, near, far, 2, jnp.where(lane < half, wet, turn(nexts[0], half)), packed[2][1])
-    to_pairs(ids, near, far, 3, nexts[1], nexts[1])
+    spot = iota((rows, rows), 0) == iota((rows, rows), 1)
+    value = jnp.sum(jnp.where(spot, coup_here[...], 0.0), axis=1, keepdims=True)
+    coupled[...] = jnp.broadcast_to(value, (rows, cols))
     for which, row in enumerate(row_choices(pair, rows, ids[0])):
         msg = lat_msgs[which]
-        for j, x in enumerate(fields):
-            msg[j] = take_row(x, row, levels, rows)
+
+        def put(j, value):
+            msg[pl.ds(j * levels, levels), :] = value
+
+        for j, x in enumerate((t, s, u, v)):
+            put(j, take_row(x, row, levels, rows))
         wet = take_row(sea, row, levels, rows).astype(f32)
         speed = take_row(north, row, levels, rows)
-        msg[4] = wet
+        put(4, wet)
         for step in (1, 0):
             _, merid = branches(take_row(flags.at[step], row, levels, rows))
             value = wet * (speed * merid - diffusion)
             if step:
-                msg[5] = value
+                put(5, value)
             elif pair or row:
                 nn_late[...] = value
-        msg[6] = jnp.zeros((levels, cols), f32)
         if pair:
             block = jnp.where(row == 0, inverse[0], inverse[rows - 1])
         else:
             block = inverse[row]
-        msg[6, :, pl.ds(0, levels)] = block
+        size = block_shape(levels)
+        last = pl.ds(6 * levels, size)
+        msg[last, :] = jnp.zeros((size, cols), f32)
+        msg[last, pl.ds(0, levels)] = block[:size]
+        msg[last, pl.ds(half, levels)] = block[size:]
+
+
+def edges_kernel(first, dims, ids, t, s, u, v, *refs):
+    levels, rows, cols, half, _ = dims
+    lane = iota((rows, cols), 1)
+    sea, east, flags, near, far = refs if first else (None, None, None, *refs)
+    to_pairs(ids, near, far, 0, *edge_columns(levels, rows, t, s, 2))
+    to_pairs(ids, near, far, 1, *edge_columns(levels, rows, u, v, 2))
+    if first:
+        wet, first_wet = edge_columns(levels, rows, sea, east, 2)
+        flag, _ = edge_columns(levels, rows, flags.at[1], flags.at[0], 1)
+        speed = turn(wet, half)
+        zonal = branches(jnp.round(flag).astype(jnp.int32))[0]
+        nexts = [wet * (speed * z - diffusion) for z in (zonal, turn(zonal, half))]
+        to_pairs(ids, near, far, 2, jnp.where(lane < half, wet, turn(nexts[0], half)), first_wet)
+        to_pairs(ids, near, far, 3, nexts[1], nexts[1])
 
 
 def edge_columns(levels, rows, x, y, pieces):
@@ -284,8 +299,12 @@
     each_level(levels, one, jnp.zeros((rows, cols), f32))
 
 
+def plane_of(ref, j, levels):
+    return ref[pl.ds(j * levels, levels), :]
+
+
 def rows_kernel(first, dims, ids, *refs):
-    levels, _, cols, _, pair = dims
+    levels, _, cols, half, pair = dims
     count = 1 if pair else 2
     new, const, *refs = (refs[i * count : (i + 1) * count] for i in range(len(refs) // count + 1))
     turned_high, turned_low, thin = refs[2:5] if first else refs[:3]
@@ -294,17 +313,20 @@
     at_edge = pl.ds(ids[2], 1)
     for h in range(count):
         if first:
+            size = block_shape(levels)
+            packed = const[h][pl.ds(6 * levels, size), :]
+            square = jnp.concatenate([packed[:, :levels], turn(packed, half)[:, :levels]], axis=0)
             eye = (iota((levels, levels), 0) == iota((levels, levels), 1)).astype(bf16)
             pick = (iota((levels, cols), 0) == ids[2]).astype(bf16)
-            turned = tuple(dot(eye, piece, ((1,), (1,))).astype(bf16) for piece in split(const[h][6][:, :levels]))
+            turned = tuple(dot(eye, piece, ((1,), (1,))).astype(bf16) for piece in split(square))
             turned_high[h][...], turned_low[h][...] = turned
             thin[h][...] = dot(turned[0], pick) + dot(turned[1], pick)
         turned = (turned_high[h][...], turned_low[h][...])
-        both = dot3(turned, split(jnp.concatenate([new[h][f] for f in range(4)], axis=1)))
+        both = dot3(turned, split(jnp.concatenate([plane_of(new[h], f, levels) for f in range(4)], axis=1)))
         for f in range(4):
             scratch[f] = both[:, f * cols : (f + 1) * cols]
         lines[h][...] = jnp.zeros_like(lines[h])
-        wet = const[h][4]
+        wet = plane_of(const[h], 4, levels)
         for j in range(4):
             lines[h][pl.ds(j, 1), :] = scratch[j, at_edge, :]
             outs[h][j] = wet * scratch[j]
@@ -423,9 +445,10 @@
     row_proj, row_line, row_const, row_late, row_far = (rest[i * count : (i + 1) * count] for i in range(5))
     rest = rest[5 * count :]
     if final:
-        outs = rest
+        outs, (extras, work, sems) = rest[:4], rest[4:]
     else:
-        late_out, outs, (to_near, to_far), lat_msgs = rest[0], rest[1:5], rest[5:7], rest[7:]
+        late_out, outs, lat_msgs, extras = rest[0], rest[1:5], rest[5:-1], rest[-1]
+        work = outs
     lat, depth, parts = ids[0], ids[1], ids[3]
     lane = iota((rows, cols), 1)
     row = iota((rows, cols), 0)
@@ -471,8 +494,39 @@
     plain = 1.0 - 4.0 * viscosity
     mids = (plain * carried[2] - coriolis * carried[3], plain * carried[3] + coriolis * carried[2])
 
-    def one(j, below):
-        k = levels - 1 - j
+    later = (iota((levels, levels), 1) >= iota((levels, levels), 0)).astype(bf16)
+    for h in range(count):
+        if pair:
+            at, sign = jnp.where(lat == 0, rows - 1, 0), jnp.where(lat == 0, -1.0, 1.0)
+        else:
+            at, sign = ((rows - 1, -1.0), (0, 1.0))[h]
+        take = lambda ref: take_row(ref, at, levels, rows)
+        pick = lambda plane: (
+            jnp.where(lat == 0, plane[rows - 1 : rows], plane[0:1]) if pair else plane[at : at + 1]
+        )
+        beyond = row_solved[h]
+        wet = plane_of(row_const[h], 4, levels)
+        late = plane_of(row_const[h], 5, levels) if step else plane_of(row_late[h], 4, levels)
+        if pair:
+            own = jnp.where(
+                lat == 0,
+                coef[2, pl.ds(rows - 1, levels, stride=rows), :],
+                coef[3, pl.ds(0, levels, stride=rows), :],
+            )
+            gate = own * jnp.where(lat == 0, wet, -late)
+        else:
+            gate = coef[2 + h, pl.ds(at, levels, stride=rows), :] * (-late if h else wet)
+        high, low = split(push * sign * beyond[3])
+        rise = dot(later, high) + dot(later, low)
+        spk = take(spike)
+        for f in range(2):
+            mid = take(proj.at[f]) + spk * pick(carried[f])
+            flow = gate * (beyond[f] - mid)
+            extras[h, f] = flow + rise if f == 0 else flow - haline * rise
+        for f in (2, 3):
+            extras[h, f] = viscosity * beyond[f]
+
+    def one(k, below):
         here = level_at(k, rows)
         sides = [beside[j, here, :] for j in range(4)]
         moved = [[side * plane for side, plane in zip(sides, around[f])] for f in (2, 3)]
@@ -485,65 +539,41 @@
                 (factors[1] * around[f][0] + factors[2] * around[f][1])
                 + (factors[3] * around[f][2] + factors[4] * around[f][3])
             )
-            outs[f][here, :] = q + buoyancy if f == 0 else q - haline * buoyancy
+            place(f)[here, :] = q + buoyancy if f == 0 else q - haline * buoyancy
         spk = spike[here, :]
         for i in range(2):
             total = (moved[i][0] + moved[i][1]) + (moved[i][2] + moved[i][3])
-            outs[2 + i][here, :] = base[2 + i, here, :] + (spk * mids[i] + viscosity * total)
+            place(2 + i)[here, :] = base[2 + i, here, :] + (spk * mids[i] + viscosity * total)
         return below
 
-    each_level(levels, one, deeper)
-
-    later = (iota((levels, levels), 1) >= iota((levels, levels), 0)).astype(bf16)
-    for h in range(count):
-        if pair:
-            at, sign = jnp.where(lat == 0, rows - 1, 0), jnp.where(lat == 0, -1.0, 1.0)
-        else:
-            at, sign = ((rows - 1, -1.0), (0, 1.0))[h]
-        take = lambda ref: take_row(ref, at, levels, rows)
-        beyond = row_solved[h]
-        if pair:
-            own = jnp.where(lat == 0, coef[2, pl.ds(rows - 1, levels, stride=rows), :],
-                            coef[3, pl.ds(0, levels, stride=rows), :])
-        else:
-            own = coef[2 + h, pl.ds(at, levels, stride=rows), :]
-        late = row_const[h][5] if step else row_late[h][4]
-        here_north = row_const[h][4]
-        if pair:
-            other = jnp.where(lat == 0, here_north, -late)
-        else:
-            other = here_north if h == 0 else -late
-        gate = own * other
-        above = push * sign * beyond[3]
-        high, low = split(above)
-        rise = dot(later, high) + dot(later, low)
-        spk = take(spike)
-        pick = lambda plane: (
-            jnp.where(lat == 0, plane[rows - 1 : rows], plane[0:1]) if pair else plane[at : at + 1]
-        )
-        extra = []
-        for f in range(2):
-            mid = take(proj.at[f]) + spk * pick(carried[f])
-            flow = gate * (beyond[f] - mid)
-            extra.append(flow + rise if f == 0 else flow - haline * rise)
-        for f in (2, 3):
-            extra.append(viscosity * beyond[f])
-        for f in range(4):
-            if pair:
-                for place, mask in ((rows - 1, has_north), (0, has_south)):
-                    there = pl.ds(place, levels, stride=rows)
-                    outs[f][there, :] = outs[f][there, :] + mask * extra[f]
-            else:
-                there = pl.ds(at, levels, stride=rows)
-                outs[f][there, :] = outs[f][there, :] + (has_north if h == 0 else has_south) * extra[f]
+    place = (lambda f: work.at[f]) if final else (lambda f: outs[f])
+    below, moves = deeper, []
+    parts_of = CHUNKS if final else 1
+    size = levels // parts_of
+    for part in reversed(range(parts_of)):
+        for k in reversed(range(part * size, (part + 1) * size)):
+            below = one(k, below)
+        for h in range(count):
+            ends = ((rows - 1, has_north), (0, has_south))
+            for spot, mask in ends if pair else ends[h : h + 1]:
+                there = pl.ds(part * size * rows + spot, size, stride=rows)
+                for f in range(4):
+                    target = place(f)
+                    target[there, :] = target[there, :] + mask * extras[h, f, pl.ds(part * size, size), :]
+        if final:
+            there = pl.ds(part * size * rows, size * rows)
+            for f in range(4):
+                move = pltpu.make_async_copy(work.at[f, there], outs[f].at[there], sems.at[4 * part + f])
+                move.start()
+                moves.append(move)
+    for move in moves:
+        move.wait()
 
     if not final:
         for which, at in enumerate(row_choices(pair, rows, lat)):
             for f in range(4):
-                lat_msgs[which][f] = take_row(outs[f], at, levels, rows)
-            lat_msgs[which][4] = late_out[...]
-        for p in range(2):
-            to_pairs(ids, to_near, to_far, p, *edge_columns(levels, rows, outs[2 * p], outs[2 * p + 1], 2))
+                lat_msgs[which][pl.ds(f * levels, levels), :] = take_row(outs[f], at, levels, rows)
+            lat_msgs[which][pl.ds(4 * levels, levels), :] = late_out[...]
 
 
 def places(levels):
@@ -551,7 +581,7 @@
     return lat, depth, (levels - 1) * (1 - depth), lax.axis_size("lat"), lax.rem(lon, 2)
 
 
-def call(kernel, dims, outs, args, smem=(), scratch=(), hbm=()):
+def call(kernel, dims, outs, args, smem=(), scratch=(), hbm=(), out_space=pltpu.VMEM):
     spaces = [pltpu.SMEM if i in smem else pltpu.HBM if i in hbm else pltpu.VMEM for i in range(len(args))]
 
     def run(*refs):
@@ -561,7 +591,7 @@
         run,
         out_shape=[jax.ShapeDtypeStruct(shape, kind) for shape, kind in outs],
         in_specs=[pl.BlockSpec(memory_space=space) for space in spaces],
-        out_specs=[pl.BlockSpec(memory_space=pltpu.VMEM)] * len(outs),
+        out_specs=[pl.BlockSpec(memory_space=out_space)] * len(outs),
         scratch_shapes=list(scratch),
         compiler_params=pltpu.CompilerParams(vmem_limit_bytes=VMEM_BYTES),
     )(*args)
@@ -612,23 +642,34 @@
 
     sources = (*state, sea, east, north, flags, block_inverse)
     sources = tuple(pltpu.with_memory_space_constraint(x, pltpu.HBM) for x in sources)
-    near, far, late, coupled, *rest = call(
-        pack_kernel,
+    full = 6 * levels + block_shape(levels)
+    late, coupled, *rest = call(
+        fetch_kernel,
         dims,
-        [((4,) + plane, f32)] * 2
-        + [(grid, f32), (plane, f32)]
-        + [((7,) + grid, f32)] * count
+        [(grid, f32), (plane, f32)]
+        + [((full, cols), f32)] * count
         + [(x.shape, x.dtype) for x in sources],
-        (pltpu.with_memory_space_constraint(coupling, pltpu.HBM), *sources),
-        (0,),
-        (pltpu.SemaphoreType.DMA((9,)),),
-        range(1, 10),
+        (pltpu.with_memory_space_constraint(coupling.reshape(1, rows), pltpu.HBM), *sources),
+        (),
+        (pltpu.VMEM((1, rows), f32), pltpu.SemaphoreType.DMA((10,))),
+        range(10),
     )
     lat_msgs, rest = rest[:count], rest[count:]
     state, (sea, east, north, flags, block_inverse) = rest[:4], rest[4:]
+
+    def to_lon(step, state, *more):
+        near, far = call(
+            functools.partial(edges_kernel, step == STEPS - 1),
+            dims,
+            [((4 if more else 2,) + plane, f32)] * 2,
+            (*state, *more),
+        )
+        near = lax.ppermute(near, "lon", close)
+        far = lax.ppermute(far, "lon", apart)
+        return near, far
+
     row_const = row_new = to_lat(lat_msgs, False)
-    near_const = near = lax.ppermute(near, "lon", close)
-    far_const = far = lax.ppermute(far, "lon", apart)
+    near_const, far_const = near, far = to_lon(STEPS - 1, state, sea, east, flags)
 
     for step in reversed(range(STEPS)):
         first = step == STEPS - 1
@@ -677,7 +718,7 @@
         final = step == 0
         outs, extra = [((n, cols), f32)] * 4, ()
         if not final:
-            outs = outs + [((2,) + plane, f32)] * 2 + [((5,) + grid, f32)] * count
+            outs = outs + [((5 * levels, cols), f32)] * count
             extra = (late,)
         result = call(
             functools.partial(apply_kernel, step, final),
@@ -687,12 +728,14 @@
                 coupled, proj, spike, mine, theirs, base, coef, factor, beside,
                 *rows_out, *row_const, *row_new, *row_far, *extra,
             ),
+            scratch=(pltpu.VMEM((count, 4) + grid, f32),)
+            + ((pltpu.VMEM((4, n, cols), f32), pltpu.SemaphoreType.DMA((4 * CHUNKS,))) if final else ()),
+            out_space=pltpu.HBM if final else pltpu.VMEM,
         )
         state = result[:4]
         if not final:
-            row_new = to_lat(result[6:], False)
-            near = lax.ppermute(result[4], "lon", close)
-            far = lax.ppermute(result[5], "lon", apart)
+            row_new = to_lat(result[4:], False)
+            near, far = to_lon(0, state)
     return tuple(x.reshape(levels, rows, cols) for x in state)
 
 

time: 33.5 us -> 32.4 us (0.967)
  Pallas kernels: 11.4 us -> 10.9 us
  waiting for transfers between devices: 6.23 us -> 5.85 us
    ppermute x2, waiting for transfers between devices: 0.7 us -> 0.01 us  [to_lat(): return [lax.ppermute(m, 'lat', r) for m, r in zip(msgs, routes)]]
    ppermute x2, starting transfers between devices: 3.04 us -> 3.63 us  [to_lat(): return [lax.ppermute(m, ('lat', 'depth'), r) for m, r in zip(msgs, both)]]
    pallas_call x13 -> x15, Pallas kernels: 11.4 us -> 10.9 us  [call(): pl.pallas_call(run, out_shape=[jax.ShapeDtypeStruct(shape, kind) for shap...]
    ppermute x2, starting transfers between devices: 3.06 us -> 2.61 us  [to_depth(): lax.ppermute(msg, 'depth', [(d, depths - 1 - d) for d in range(depths)])]
  transfers between devices with their start and end apart: 10 -> 10, of which waited for: 5 -> 4; matrix products, arithmetic and copies ran while one was open for 0% -> 0% of each run, Pallas kernels for 17% -> 21%
where the time goes in v7:
time: 32.4 us; the launch traced here: 32.3 us
  starting transfers between devices  14.7 us (45%)
  Pallas kernels  10.9 us (34%)
  waiting for transfers between devices  5.85 us (18%)
  between operations  0.76 us (2%)
    pallas_call x15, Pallas kernels, call(): pl.pallas_call(run, out_shape=[jax.ShapeDtypeStruct(shape, kind) for shap...  10.9 us
    ppermute x2, starting transfers between devices, to_lon(): far = lax.ppermute(far, 'lon', apart)  4.22 us
    ppermute x2, starting transfers between devices, to_lat(): return [lax.ppermute(m, 'lat', r) for m, r in zip(msgs, routes)]  4.2 us
    ppermute x2, waiting for transfers between devices, to_lat(): return [lax.ppermute(m, ('lat', 'depth'), r) for m, r in zip(msgs, both)]  4.05 us
    ppermute x2, starting transfers between devices, to_lat(): return [lax.ppermute(m, ('lat', 'depth'), r) for m, r in zip(msgs, both)]  3.63 us
    ppermute x2, starting transfers between devices, to_depth(): lax.ppermute(msg, 'depth', [(d, depths - 1 - d) for d in range(depths)])  2.61 us
    ppermute x2, waiting for transfers between devices, to_lon(): far = lax.ppermute(far, 'lon', apart)  1.79 us
  transfers between devices with their start and end apart: 10, of which 4 were waited for; matrix products, arithmetic and copies ran while one was open for 0% of the time, Pallas kernels for 21%

profile of v7, /device:TPU:0, one launch (start us, length us, event | category | flops | bytes accessed | tf_op | source)
XLA Modules:
  0.0 32.3 jit_solution(15163375502243548261)
XLA Ops:
  0.6 1.8 %shard_map.129 = (f32[48,128]{1,0:T(8,128)S(1)}, f32[8,128]{1,0:T(8,128)S(1)}, f32[312,128]{1,0:T(8,128)S(1)}, f32[384,128]{1,0:T(8,128)S(1)}, f32[384,128]{1,0:...) custom-call(f32[1,8]{1,0:T(1,128)} %bitcast.21, ...), custom_call_target="tpu_custom_call" | custom-call | tf_op jit(solution)/shard_map/pallas_call | solution.py:590
  2.4 4.1 %collective-permute-start.3 = (f32[312,128]{1,0:T(8,128)S(1)}, f32[312,128]{1,0:T(8,128)S(1)}, u32[]{:S(2)}, u32[]{:S(2)}) collective-permute-start(f32[312,128]{1,0:T(8,128)S(1)} %get-tuple-element.83), channel_id=1, source_target_pairs={{0,2},{2,0},{1,3},{3,1},{4,6},{6,4},{5,7},{7,5},{8,10},{10,8},{9,1... | collective-permute-start | bytes 479240 | tf_op jit(solution)/shard_map/ppermute | solution.py:634
  6.6 0.7 %shard_map.131 = (f32[4,8,128]{2,1,0:T(8,128)S(1)}, f32[4,8,128]{2,1,0:T(8,128)S(1)}) custom-call(f32[384,128]{1,0:T(8,128)S(1)} %get-tuple-element.60.refs_0_, f32[384,128]{1,0:T(8,128)S(1)} %get-tuple-element.61.refs_1_, f32[384,128]{1,0:T(8,128)S(1)} %get-tuple-element.62.refs_2_, f32[384,128]{1,0:T(8,128)S(1)} %get-tuple-element.63.refs_3_, ...), custom_call_target="tpu_custom_call" | custom-call | tf_op jit(solution)/shard_map/pallas_call | solution.py:590
  7.2 0.0 collective-permute-start
  7.3 2.6 %collective-permute-start.1 = (f32[4,8,128]{2,1,0:T(8,128)S(1)}, f32[4,8,128]{2,1,0:T(8,128)S(1)}, u32[]{:S(2)}, u32[]{:S(2)}) collective-permute-start(f32[4,8,128]{2,1,0:T(8,128)S(1)} %get-tuple-element.71), channel_id=1, source_target_pairs={{0,28},{4,8},{8,4},{12,16},{16,12},{20,24},{24,20},{28,0},{1,29},{... | collective-permute-start | bytes 49160 | tf_op jit(solution)/shard_map/ppermute | solution.py:668
  9.8 1.3 %shard_map.130 = (f32[4,384,128]{2,1,0:T(8,128)S(1)}, f32[7,8,128]{2,1,0:T(8,128)S(1)}, f32[8,128]{1,0:T(8,128)S(1)}, f32[384,128]{1,0:T(8,128)S(1)}, bf16[384,3...) custom-call(f32[384,128]{1,0:T(8,128)S(1)} %get-tuple-element.60.ref, ...), custom_call_target="tpu_custom_call" | custom-call | tf_op jit(solution)/shard_map/pallas_call | solution.py:590
  11.1 0.0 collective-permute-done.refs_0_.refs_2_.refs_4_
  11.1 0.2 collective-permute-done.1.refs_1_.refs_3_.refs_5_
  11.3 0.3 shard_map.132
  11.7 1.6 %collective-permute-start.2 = (f32[8,8,128]{2,1,0:T(8,128)S(1)}, f32[8,8,128]{2,1,0:T(8,128)S(1)}, u32[]{:S(2)}, u32[]{:S(2)}) collective-permute-start(f32[8,8,128]{2,1,0:T(8,128)S(1)} %get-tuple-element.77.refs_3_), channel_id=1, source_target_pairs={{0,1},{1,0},{2,3},{3,2},{4,5},{5,4},{6,7},{7,6},{8,9},{9,8},{10,11... | collective-permute-start | bytes 98312 | tf_op jit(solution)/shard_map/ppermute | solution.py:641
  13.3 0.1 collective-permute-start.4
  13.5 0.5 %shard_map.133 = (f32[4,384,128]{2,1,0:T(8,128)S(1)}, f32[5,384,128]{2,1,0:T(8,128)S(1)}, f32[4,384,128]{2,1,0:T(8,128)S(1)}) custom-call(s32[384,128]{1,0:T(8,128)S(1)} %get-tuple-element.64.refs_4_.refs_0_, f32[384,128]{1,0:T(8,128)S(1)} %get-tuple-element.68.refs_5_.refs_1_, f32[384,128]{1,0:T(8,128)S(1)} %get-tuple-element.79.refs_2_, ...), custom_call_target="tpu_custom_call" | custom-call | tf_op jit(solution)/shard_map/pallas_call | solution.py:590
  13.9 0.8 %shard_map.134.refs_5_ = f32[4,384,128]{2,1,0:T(8,128)S(1)} custom-call(f32[4,384,128]{2,1,0:T(8,128)S(1)} %get-tuple-element.66.refs_0_.refs_1_, f32[4,8,128]{2,1,0:T(8,128)S(1)} %get-tuple-element.78.refs_1_, f32[4,8,128]{2,1,0:T(8,128)S(1)} %collective-permute-done.refs_0_.refs_2_.refs_4_, ...), custom_call_target="tpu_custom_call" | custom-call | tf_op jit(solution)/shard_map/pallas_call | solution.py:590
  14.7 0.0 collective-permute-done.3.refs_0_.refs_1_.refs_11_.refs_12_
  14.7 0.4 %shard_map.135 = (f32[5,48,128]{2,1,0:T(8,128)S(1)}, f32[8,128]{1,0:T(8,128)S(1)}, bf16[48,48]{1,0:T(8,128)(2,1)S(1)}, bf16[48,48]{1,0:T(8,128)(2,1)S(1)}, f32[48,128]{1,0:T(8,128)S(1)}) custom-call(f32[312,128]{1,0:T(8,128)S(1)} %collective-permute-done.3.refs_0_.refs_1_.refs_11_.refs_12_, ...), custom_call_target="tpu_custom_call" | custom-call | tf_op jit(solution)/shard_map/pallas_call | solution.py:590
  15.1 3.6 %collective-permute-done.4.refs_13_ = f32[8,128]{1,0:T(8,128)S(1)} collective-permute-done((f32[8,128]{1,0:T(8,128)S(1)}, f32[8,128]{1,0:T(8,128)S(1)}, u32[]{:S(2)}, u32[]{:S(2)}) %collective-permute-start.4) | collective-permute-done | bytes 4128 | tf_op jit(solution)/shard_map/ppermute | solution.py:638
  18.7 0.0 collective-permute-done.2.refs_4_
  18.7 0.7 %shard_map.136 = (f32[384,128]{1,0:T(8,128)S(1)}, f32[384,128]{1,0:T(8,128)S(1)}, f32[384,128]{1,0:T(8,128)S(1)}, f32[384,128]{1,0:T(8,128)S(1)}, f32[240,128]{1,0:T(8,128)S(1)}) custom-call(f32[8,128]{1,0:T(8,128)S(1)} %get-tuple-element.59.refs_6_.refs_0_.refs_5_, f32[4,384,128]{2,1,0:T(8,128)S(1)} %get-tuple-element.66.refs_0_.refs_1_, ...), custom_call_target="tpu_custom_call" | custom-call | tf_op jit(solution)/shard_map/pallas_call | solution.py:590
  19.4 0.1 collective-permute-start.8
  19.5 0.4 %shard_map.138 = (f32[2,8,128]{2,1,0:T(8,128)S(1)}, f32[2,8,128]{2,1,0:T(8,128)S(1)}) custom-call(f32[384,128]{1,0:T(8,128)S(1)} %get-tuple-element.88.refs_0_, f32[384,128]{1,0:T(8,128)S(1)} %get-tuple-element.89.refs_1_, f32[384,128]{1,0:T(8,128)S(1)} %get-tuple-element.90.refs_2_, f32[384,128]{1,0:T(8,128)S(1)} %get-tuple-element.91.refs_3_), custom_call_target="tpu_custom_call" | custom-call | tf_op jit(solution)/shard_map/pallas_call | solution.py:590
  19.9 0.1 collective-permute-start.5
  20.0 1.7 %collective-permute-start.6 = (f32[2,8,128]{2,1,0:T(8,128)S(1)}, f32[2,8,128]{2,1,0:T(8,128)S(1)}, u32[]{:S(2)}, u32[]{:S(2)}) collective-permute-start(f32[2,8,128]{2,1,0:T(8,128)S(1)} %get-tuple-element.97), channel_id=1, source_target_pairs={{0,28},{4,8},{8,4},{12,16},{16,12},{20,24},{24,20},{28,0},{1,29},{... | collective-permute-start | bytes 24584 | tf_op jit(solution)/shard_map/ppermute | solution.py:668
  21.6 0.8 %shard_map.137 = (f32[4,384,128]{2,1,0:T(8,128)S(1)}, f32[7,8,128]{2,1,0:T(8,128)S(1)}, f32[8,128]{1,0:T(8,128)S(1)}) custom-call(f32[384,128]{1,0:T(8,128)S(1)} %get-tuple-element.88.refs_0_, f32[384,128]{1,0:T(8,128)S(1)} %get-tuple-element.89.refs_1_, f32[384,128]{1,0:T(8,128)S(1)} %get-tuple-element.90.refs_2_, ...), custom_call_target="tpu_custom_call" | custom-call | tf_op jit(solution)/shard_map/pallas_call | solution.py:590
  22.4 0.0 collective-permute-done.5.refs_0_
  22.4 1.6 %collective-permute-done.6.refs_1_ = f32[2,8,128]{2,1,0:T(8,128)S(1)} collective-permute-done((f32[2,8,128]{2,1,0:T(8,128)S(1)}, f32[2,8,128]{2,1,0:T(8,128)S(1)}, u32[]{:S(2)}, u32[]{:S(2)}) %collective-permute-start.6) | collective-permute-done | bytes 8224 | tf_op jit(solution)/shard_map/ppermute | solution.py:668
  24.0 0.3 shard_map.139
  24.3 1.0 %collective-permute-start.7 = (f32[8,8,128]{2,1,0:T(8,128)S(1)}, f32[8,8,128]{2,1,0:T(8,128)S(1)}, u32[]{:S(2)}, u32[]{:S(2)}) collective-permute-start(f32[8,8,128]{2,1,0:T(8,128)S(1)} %get-tuple-element.99.refs_3_), channel_id=1, source_target_pairs={{0,1},{1,0},{2,3},{3,2},{4,5},{5,4},{6,7},{7,6},{8,9},{9,8},{10,11... | collective-permute-start | bytes 98312 | tf_op jit(solution)/shard_map/ppermute | solution.py:641
  25.3 3.5 %collective-permute-start.9 = (f32[8,128]{1,0:T(8,128)S(1)}, f32[8,128]{1,0:T(8,128)S(1)}, u32[]{:S(2)}, u32[]{:S(2)}) collective-permute-start(f32[8,128]{1,0:T(8,128)S(1)} %get-tuple-element.109), channel_id=1, source_target_pairs={{0,3},{1,2},{2,1},{3,0},{4,7},{5,6},{6,5},{7,4},{8,11},{9,10},{10,... | collective-permute-start | bytes 12296 | tf_op jit(solution)/shard_map/ppermute | solution.py:638
  28.8 0.5 %shard_map.140 = (f32[4,384,128]{2,1,0:T(8,128)S(1)}, f32[5,384,128]{2,1,0:T(8,128)S(1)}) custom-call(s32[384,128]{1,0:T(8,128)S(1)} %get-tuple-element.64.refs_4_.refs_0_, f32[384,128]{1,0:T(8,128)S(1)} %get-tuple-element.68.refs_5_.refs_1_, f32[384,128]{1,0:T(8,128)S(1)} %get-tuple-element.79.refs_2_, ...), custom_call_target="tpu_custom_call" | custom-call | tf_op jit(solution)/shard_map/pallas_call | solution.py:590
  29.3 0.8 %shard_map.141.refs_5_ = f32[4,384,128]{2,1,0:T(8,128)S(1)} custom-call(f32[4,384,128]{2,1,0:T(8,128)S(1)} %get-tuple-element.95.refs_0_.refs_1_, f32[4,8,128]{2,1,0:T(8,128)S(1)} %get-tuple-element.100.refs_1_, f32[4,8,128]{2,1,0:T(8,128)S(1)} %collective-permute-done.refs_0_.refs_2_.refs_4_, ...), custom_call_target="tpu_custom_call" | custom-call | tf_op jit(solution)/shard_map/pallas_call | solution.py:590
  30.0 0.0 collective-permute-done.8.refs_0_.refs_12_
  30.0 0.2 shard_map.142
  30.2 0.5 %collective-permute-done.9.refs_13_ = f32[8,128]{1,0:T(8,128)S(1)} collective-permute-done((f32[8,128]{1,0:T(8,128)S(1)}, f32[8,128]{1,0:T(8,128)S(1)}, u32[]{:S(2)}, u32[]{:S(2)}) %collective-permute-start.9) | collective-permute-done | bytes 4128 | tf_op jit(solution)/shard_map/ppermute | solution.py:638
  30.7 0.0 collective-permute-done.7.refs_4_
  30.7 1.6 %shard_map.143 = (f32[384,128]{1,0:T(8,128)}, f32[384,128]{1,0:T(8,128)}, f32[384,128]{1,0:T(8,128)}, f32[384,128]{1,0:T(8,128)}) custom-call(f32[8,128]{1,0:T(8,128)S(1)} %get-tuple-element.59.refs_6_.refs_0_.refs_5_, f32[4,384,128]{2,1,0:T(8,128)S(1)} %get-tuple-element.95.refs_0_.refs_1_, f32[384,128]{1,0:T(8,128)S(1)} %get-tuple-element.67.refs_6_.refs_2_, ...), custom_call_target="tpu_custom_call" | custom-call | tf_op jit(solution)/shard_map/pallas_call | solution.py:590
Async XLA Ops:
  2.4 12.3 %collective-permute-start.3 = (f32[312,128]{1,0:T(8,128)S(1)}, f32[312,128]{1,0:T(8,128)S(1)}, u32[]{:S(2)}, u32[]{:S(2)}) collective-permute-start(f32[312,128]{1,0:T(8,128)S(1)} %get-tuple-element.83), channel_id=1, source_target_pairs={{0,2},{2,0},{1,3},{3,1},{4,6},{6,4},{5,7},{7,5},{8,10},{10,8},{9,1... | collective-permute-start | bytes 479240 | tf_op jit(solution)/shard_map/ppermute | solution.py:634
  7.2 3.9 %collective-permute-start = (f32[4,8,128]{2,1,0:T(8,128)S(1)}, f32[4,8,128]{2,1,0:T(8,128)S(1)}, u32[]{:S(2)}, u32[]{:S(2)}) collective-permute-start(f32[4,8,128]{2,1,0:T(8,128)S(1)} %get-tuple-element.70), channel_id=1, source_target_pairs={{0,4},{4,0},{8,12},{12,8},{16,20},{20,16},{24,28},{28,24},{1,5},{5... | collective-permute-start | bytes 49160 | tf_op jit(solution)/shard_map/ppermute | solution.py:667
  7.3 4.1 %collective-permute-start.1 = (f32[4,8,128]{2,1,0:T(8,128)S(1)}, f32[4,8,128]{2,1,0:T(8,128)S(1)}, u32[]{:S(2)}, u32[]{:S(2)}) collective-permute-start(f32[4,8,128]{2,1,0:T(8,128)S(1)} %get-tuple-element.71), channel_id=1, source_target_pairs={{0,28},{4,8},{8,4},{12,16},{16,12},{20,24},{24,20},{28,0},{1,29},{... | collective-permute-start | bytes 49160 | tf_op jit(solution)/shard_map/ppermute | solution.py:668
  11.7 7.1 %collective-permute-start.2 = (f32[8,8,128]{2,1,0:T(8,128)S(1)}, f32[8,8,128]{2,1,0:T(8,128)S(1)}, u32[]{:S(2)}, u32[]{:S(2)}) collective-permute-start(f32[8,8,128]{2,1,0:T(8,128)S(1)} %get-tuple-element.77.refs_3_), channel_id=1, source_target_pairs={{0,1},{1,0},{2,3},{3,2},{4,5},{5,4},{6,7},{7,6},{8,9},{9,8},{10,11... | collective-permute-start | bytes 98312 | tf_op jit(solution)/shard_map/ppermute | solution.py:641
  13.3 5.4 %collective-permute-start.4 = (f32[8,128]{1,0:T(8,128)S(1)}, f32[8,128]{1,0:T(8,128)S(1)}, u32[]{:S(2)}, u32[]{:S(2)}) collective-permute-start(f32[8,128]{1,0:T(8,128)S(1)} %get-tuple-element.86), channel_id=1, source_target_pairs={{0,3},{1,2},{2,1},{3,0},{4,7},{5,6},{6,5},{7,4},{8,11},{9,10},{10,... | collective-permute-start | bytes 12296 | tf_op jit(solution)/shard_map/ppermute | solution.py:638
  19.4 10.6 %collective-permute-start.8 = (f32[240,128]{1,0:T(8,128)S(1)}, f32[240,128]{1,0:T(8,128)S(1)}, u32[]{:S(2)}, u32[]{:S(2)}) collective-permute-start(f32[240,128]{1,0:T(8,128)S(1)} %get-tuple-element.103), channel_id=1, source_target_pairs={{0,2},{2,0},{1,3},{3,1},{4,6},{6,4},{5,7},{7,5},{8,10},{10,8},{9,1... | collective-permute-start | bytes 368648 | tf_op jit(solution)/shard_map/ppermute | solution.py:634
  19.9 2.5 %collective-permute-start.5 = (f32[2,8,128]{2,1,0:T(8,128)S(1)}, f32[2,8,128]{2,1,0:T(8,128)S(1)}, u32[]{:S(2)}, u32[]{:S(2)}) collective-permute-start(f32[2,8,128]{2,1,0:T(8,128)S(1)} %get-tuple-element.96), channel_id=1, source_target_pairs={{0,4},{4,0},{8,12},{12,8},{16,20},{20,16},{24,28},{28,24},{1,5},{5... | collective-permute-start | bytes 24584 | tf_op jit(solution)/shard_map/ppermute | solution.py:667
  20.0 4.0 %collective-permute-start.6 = (f32[2,8,128]{2,1,0:T(8,128)S(1)}, f32[2,8,128]{2,1,0:T(8,128)S(1)}, u32[]{:S(2)}, u32[]{:S(2)}) collective-permute-start(f32[2,8,128]{2,1,0:T(8,128)S(1)} %get-tuple-element.97), channel_id=1, source_target_pairs={{0,28},{4,8},{8,4},{12,16},{16,12},{20,24},{24,20},{28,0},{1,29},{... | collective-permute-start | bytes 24584 | tf_op jit(solution)/shard_map/ppermute | solution.py:668
  24.3 6.4 %collective-permute-start.7 = (f32[8,8,128]{2,1,0:T(8,128)S(1)}, f32[8,8,128]{2,1,0:T(8,128)S(1)}, u32[]{:S(2)}, u32[]{:S(2)}) collective-permute-start(f32[8,8,128]{2,1,0:T(8,128)S(1)} %get-tuple-element.99.refs_3_), channel_id=1, source_target_pairs={{0,1},{1,0},{2,3},{3,2},{4,5},{5,4},{6,7},{7,6},{8,9},{9,8},{10,11... | collective-permute-start | bytes 98312 | tf_op jit(solution)/shard_map/ppermute | solution.py:641
  25.3 5.4 %collective-permute-start.9 = (f32[8,128]{1,0:T(8,128)S(1)}, f32[8,128]{1,0:T(8,128)S(1)}, u32[]{:S(2)}, u32[]{:S(2)}) collective-permute-start(f32[8,128]{1,0:T(8,128)S(1)} %get-tuple-element.109), channel_id=1, source_target_pairs={{0,3},{1,2},{2,1},{3,0},{4,7},{5,6},{6,5},{7,4},{8,11},{9,10},{10,... | collective-permute-start | bytes 12296 | tf_op jit(solution)/shard_map/ppermute | solution.py:638

commit v8 on v7

--- a/solution.py
+++ b/solution.py
@@ -316,9 +316,8 @@
             size = block_shape(levels)
             packed = const[h][pl.ds(6 * levels, size), :]
             square = jnp.concatenate([packed[:, :levels], turn(packed, half)[:, :levels]], axis=0)
-            eye = (iota((levels, levels), 0) == iota((levels, levels), 1)).astype(bf16)
             pick = (iota((levels, cols), 0) == ids[2]).astype(bf16)
-            turned = tuple(dot(eye, piece, ((1,), (1,))).astype(bf16) for piece in split(square))
+            turned = split(square.T)
             turned_high[h][...], turned_low[h][...] = turned
             thin[h][...] = dot(turned[0], pick) + dot(turned[1], pick)
         turned = (turned_high[h][...], turned_low[h][...])
@@ -693,14 +692,17 @@
             (near, far, near_const, far_const, planes, corner, spike_packed, p_high, p_low),
         )
         theirs = to_depth(mine)
-        coef, factor, *more = call(
-            functools.partial(coef_kernel, step),
-            dims,
-            [((4, n, cols), f32), ((5, n, cols), f32)] + [((4, n, cols), f32)] * first,
-            (sea, east, north, flags, near_const, far_const, spike, spike_packed),
-        )
         if first:
-            (beside,) = more
+            faces = {}
+            for later in reversed(range(STEPS)):
+                *faces[later], = call(
+                    functools.partial(coef_kernel, later),
+                    dims,
+                    [((4, n, cols), f32), ((5, n, cols), f32)] + [((4, n, cols), f32)] * (later == step),
+                    (sea, east, north, flags, near_const, far_const, spike, spike_packed),
+                )
+            beside = faces[step][2]
+        coef, factor = faces[step][:2]
         (base,) = call(base_kernel, dims, [((4, n, cols), f32)], (proj, side_proj, near_const, far_const, coef))
         block = ((levels, levels), bf16)
         rows_out = call(

time: 32.4 us -> 32.4 us (level)
  no operation moved by 1% of the time
where the time goes in v8:
time: 32.4 us; the launch traced here: 32.3 us
  starting transfers between devices  14.7 us (45%)
  Pallas kernels  10.8 us (33%)
  waiting for transfers between devices  5.94 us (18%)
  between operations  0.76 us (2%)
    pallas_call x15, Pallas kernels, call(): pl.pallas_call(run, out_shape=[jax.ShapeDtypeStruct(shape, kind) for shap...  10.8 us
    ppermute x2, starting transfers between devices, to_lon(): far = lax.ppermute(far, 'lon', apart)  4.22 us
    ppermute x2, starting transfers between devices, to_lat(): return [lax.ppermute(m, 'lat', r) for m, r in zip(msgs, routes)]  4.2 us
    ppermute x2, waiting for transfers between devices, to_lat(): return [lax.ppermute(m, ('lat', 'depth'), r) for m, r in zip(msgs, both)]  4.14 us
    ppermute x2, starting transfers between devices, to_lat(): return [lax.ppermute(m, ('lat', 'depth'), r) for m, r in zip(msgs, both)]  3.63 us
    ppermute x2, starting transfers between devices, to_depth(): lax.ppermute(msg, 'depth', [(d, depths - 1 - d) for d in range(depths)])  2.61 us
    ppermute x2, waiting for transfers between devices, to_lon(): far = lax.ppermute(far, 'lon', apart)  1.79 us
  transfers between devices with their start and end apart: 10, of which 4 were waited for; matrix products, arithmetic and copies ran while one was open for 0% of the time, Pallas kernels for 21%

profile of v8, /device:TPU:0, one launch (start us, length us, event | category | flops | bytes accessed | tf_op | source)
XLA Modules:
  0.0 32.3 jit_solution(14526142185439370300)
XLA Ops:
  0.6 1.8 %shard_map.129 = (f32[48,128]{1,0:T(8,128)S(1)}, f32[8,128]{1,0:T(8,128)S(1)}, f32[312,128]{1,0:T(8,128)S(1)}, f32[384,128]{1,0:T(8,128)S(1)}, f32[384,128]{1,0:...) custom-call(f32[1,8]{1,0:T(1,128)} %bitcast.21, ...), custom_call_target="tpu_custom_call" | custom-call | tf_op jit(solution)/shard_map/pallas_call | solution.py:589
  2.4 4.1 %collective-permute-start.3 = (f32[312,128]{1,0:T(8,128)S(1)}, f32[312,128]{1,0:T(8,128)S(1)}, u32[]{:S(2)}, u32[]{:S(2)}) collective-permute-start(f32[312,128]{1,0:T(8,128)S(1)} %get-tuple-element.83), channel_id=1, source_target_pairs={{0,2},{2,0},{1,3},{3,1},{4,6},{6,4},{5,7},{7,5},{8,10},{10,8},{9,1... | collective-permute-start | bytes 479240 | tf_op jit(solution)/shard_map/ppermute | solution.py:633
  6.6 0.7 %shard_map.131 = (f32[4,8,128]{2,1,0:T(8,128)S(1)}, f32[4,8,128]{2,1,0:T(8,128)S(1)}) custom-call(f32[384,128]{1,0:T(8,128)S(1)} %get-tuple-element.60.refs_0_, f32[384,128]{1,0:T(8,128)S(1)} %get-tuple-element.61.refs_1_, f32[384,128]{1,0:T(8,128)S(1)} %get-tuple-element.62.refs_2_, f32[384,128]{1,0:T(8,128)S(1)} %get-tuple-element.63.refs_3_, ...), custom_call_target="tpu_custom_call" | custom-call | tf_op jit(solution)/shard_map/pallas_call | solution.py:589
  7.2 0.0 collective-permute-start
  7.3 2.6 %collective-permute-start.1 = (f32[4,8,128]{2,1,0:T(8,128)S(1)}, f32[4,8,128]{2,1,0:T(8,128)S(1)}, u32[]{:S(2)}, u32[]{:S(2)}) collective-permute-start(f32[4,8,128]{2,1,0:T(8,128)S(1)} %get-tuple-element.71), channel_id=1, source_target_pairs={{0,28},{4,8},{8,4},{12,16},{16,12},{20,24},{24,20},{28,0},{1,29},{... | collective-permute-start | bytes 49160 | tf_op jit(solution)/shard_map/ppermute | solution.py:667
  9.8 1.3 %shard_map.130 = (f32[4,384,128]{2,1,0:T(8,128)S(1)}, f32[7,8,128]{2,1,0:T(8,128)S(1)}, f32[8,128]{1,0:T(8,128)S(1)}, f32[384,128]{1,0:T(8,128)S(1)}, bf16[384,3...) custom-call(f32[384,128]{1,0:T(8,128)S(1)} %get-tuple-element.60.ref, ...), custom_call_target="tpu_custom_call" | custom-call | tf_op jit(solution)/shard_map/pallas_call | solution.py:589
  11.1 0.0 collective-permute-done.refs_0_.refs_2_.refs_4_
  11.1 0.2 collective-permute-done.1.refs_1_.refs_3_.refs_5_
  11.3 0.3 shard_map.132
  11.7 1.6 %collective-permute-start.2 = (f32[8,8,128]{2,1,0:T(8,128)S(1)}, f32[8,8,128]{2,1,0:T(8,128)S(1)}, u32[]{:S(2)}, u32[]{:S(2)}) collective-permute-start(f32[8,8,128]{2,1,0:T(8,128)S(1)} %get-tuple-element.77.refs_3_), channel_id=1, source_target_pairs={{0,1},{1,0},{2,3},{3,2},{4,5},{5,4},{6,7},{7,6},{8,9},{9,8},{10,11... | collective-permute-start | bytes 98312 | tf_op jit(solution)/shard_map/ppermute | solution.py:640
  13.3 0.1 collective-permute-start.4
  13.5 0.5 %shard_map.133 = (f32[4,384,128]{2,1,0:T(8,128)S(1)}, f32[5,384,128]{2,1,0:T(8,128)S(1)}, f32[4,384,128]{2,1,0:T(8,128)S(1)}) custom-call(s32[384,128]{1,0:T(8,128)S(1)} %get-tuple-element.64.refs_4_.refs_0_, f32[384,128]{1,0:T(8,128)S(1)} %get-tuple-element.68.refs_5_.refs_1_, f32[384,128]{1,0:T(8,128)S(1)} %get-tuple-element.79.refs_2_, ...), custom_call_target="tpu_custom_call" | custom-call | tf_op jit(solution)/shard_map/pallas_call | solution.py:589
  13.9 0.8 %shard_map.134.refs_5_ = f32[4,384,128]{2,1,0:T(8,128)S(1)} custom-call(f32[4,384,128]{2,1,0:T(8,128)S(1)} %get-tuple-element.66.refs_0_.refs_1_, f32[4,8,128]{2,1,0:T(8,128)S(1)} %get-tuple-element.78.refs_1_, f32[4,8,128]{2,1,0:T(8,128)S(1)} %collective-permute-done.refs_0_.refs_2_.refs_4_, ...), custom_call_target="tpu_custom_call" | custom-call | tf_op jit(solution)/shard_map/pallas_call | solution.py:589
  14.7 0.0 collective-permute-done.3.refs_0_.refs_1_.refs_11_.refs_12_
  14.7 0.3 %shard_map.135 = (f32[5,48,128]{2,1,0:T(8,128)S(1)}, f32[8,128]{1,0:T(8,128)S(1)}, bf16[48,48]{1,0:T(8,128)(2,1)S(1)}, bf16[48,48]{1,0:T(8,128)(2,1)S(1)}, f32[48,128]{1,0:T(8,128)S(1)}) custom-call(f32[312,128]{1,0:T(8,128)S(1)} %collective-permute-done.3.refs_0_.refs_1_.refs_11_.refs_12_, ...), custom_call_target="tpu_custom_call" | custom-call | tf_op jit(solution)/shard_map/pallas_call | solution.py:589
  15.1 3.7 %collective-permute-done.4.refs_13_ = f32[8,128]{1,0:T(8,128)S(1)} collective-permute-done((f32[8,128]{1,0:T(8,128)S(1)}, f32[8,128]{1,0:T(8,128)S(1)}, u32[]{:S(2)}, u32[]{:S(2)}) %collective-permute-start.4) | collective-permute-done | bytes 4128 | tf_op jit(solution)/shard_map/ppermute | solution.py:637
  18.7 0.0 collective-permute-done.2.refs_4_
  18.7 0.7 %shard_map.136 = (f32[384,128]{1,0:T(8,128)S(1)}, f32[384,128]{1,0:T(8,128)S(1)}, f32[384,128]{1,0:T(8,128)S(1)}, f32[384,128]{1,0:T(8,128)S(1)}, f32[240,128]{1,0:T(8,128)S(1)}) custom-call(f32[8,128]{1,0:T(8,128)S(1)} %get-tuple-element.59.refs_6_.refs_0_.refs_5_, f32[4,384,128]{2,1,0:T(8,128)S(1)} %get-tuple-element.66.refs_0_.refs_1_, ...), custom_call_target="tpu_custom_call" | custom-call | tf_op jit(solution)/shard_map/pallas_call | solution.py:589
  19.4 0.1 collective-permute-start.8
  19.5 0.4 %shard_map.138 = (f32[2,8,128]{2,1,0:T(8,128)S(1)}, f32[2,8,128]{2,1,0:T(8,128)S(1)}) custom-call(f32[384,128]{1,0:T(8,128)S(1)} %get-tuple-element.88.refs_0_, f32[384,128]{1,0:T(8,128)S(1)} %get-tuple-element.89.refs_1_, f32[384,128]{1,0:T(8,128)S(1)} %get-tuple-element.90.refs_2_, f32[384,128]{1,0:T(8,128)S(1)} %get-tuple-element.91.refs_3_), custom_call_target="tpu_custom_call" | custom-call | tf_op jit(solution)/shard_map/pallas_call | solution.py:589
  19.9 0.1 collective-permute-start.5
  20.0 1.7 %collective-permute-start.6 = (f32[2,8,128]{2,1,0:T(8,128)S(1)}, f32[2,8,128]{2,1,0:T(8,128)S(1)}, u32[]{:S(2)}, u32[]{:S(2)}) collective-permute-start(f32[2,8,128]{2,1,0:T(8,128)S(1)} %get-tuple-element.97), channel_id=1, source_target_pairs={{0,28},{4,8},{8,4},{12,16},{16,12},{20,24},{24,20},{28,0},{1,29},{... | collective-permute-start | bytes 24584 | tf_op jit(solution)/shard_map/ppermute | solution.py:667
  21.6 0.8 %shard_map.137 = (f32[4,384,128]{2,1,0:T(8,128)S(1)}, f32[7,8,128]{2,1,0:T(8,128)S(1)}, f32[8,128]{1,0:T(8,128)S(1)}) custom-call(f32[384,128]{1,0:T(8,128)S(1)} %get-tuple-element.88.refs_0_, f32[384,128]{1,0:T(8,128)S(1)} %get-tuple-element.89.refs_1_, f32[384,128]{1,0:T(8,128)S(1)} %get-tuple-element.90.refs_2_, ...), custom_call_target="tpu_custom_call" | custom-call | tf_op jit(solution)/shard_map/pallas_call | solution.py:589
  22.4 0.0 collective-permute-done.5.refs_0_
  22.4 1.6 %collective-permute-done.6.refs_1_ = f32[2,8,128]{2,1,0:T(8,128)S(1)} collective-permute-done((f32[2,8,128]{2,1,0:T(8,128)S(1)}, f32[2,8,128]{2,1,0:T(8,128)S(1)}, u32[]{:S(2)}, u32[]{:S(2)}) %collective-permute-start.6) | collective-permute-done | bytes 8224 | tf_op jit(solution)/shard_map/ppermute | solution.py:667
  24.0 0.3 shard_map.139
  24.3 1.0 %collective-permute-start.7 = (f32[8,8,128]{2,1,0:T(8,128)S(1)}, f32[8,8,128]{2,1,0:T(8,128)S(1)}, u32[]{:S(2)}, u32[]{:S(2)}) collective-permute-start(f32[8,8,128]{2,1,0:T(8,128)S(1)} %get-tuple-element.99.refs_3_), channel_id=1, source_target_pairs={{0,1},{1,0},{2,3},{3,2},{4,5},{5,4},{6,7},{7,6},{8,9},{9,8},{10,11... | collective-permute-start | bytes 98312 | tf_op jit(solution)/shard_map/ppermute | solution.py:640
  25.3 3.5 %collective-permute-start.9 = (f32[8,128]{1,0:T(8,128)S(1)}, f32[8,128]{1,0:T(8,128)S(1)}, u32[]{:S(2)}, u32[]{:S(2)}) collective-permute-start(f32[8,128]{1,0:T(8,128)S(1)} %get-tuple-element.109), channel_id=1, source_target_pairs={{0,3},{1,2},{2,1},{3,0},{4,7},{5,6},{6,5},{7,4},{8,11},{9,10},{10,... | collective-permute-start | bytes 12296 | tf_op jit(solution)/shard_map/ppermute | solution.py:637
  28.8 0.5 %shard_map.140 = (f32[4,384,128]{2,1,0:T(8,128)S(1)}, f32[5,384,128]{2,1,0:T(8,128)S(1)}) custom-call(s32[384,128]{1,0:T(8,128)S(1)} %get-tuple-element.64.refs_4_.refs_0_, f32[384,128]{1,0:T(8,128)S(1)} %get-tuple-element.68.refs_5_.refs_1_, f32[384,128]{1,0:T(8,128)S(1)} %get-tuple-element.79.refs_2_, ...), custom_call_target="tpu_custom_call" | custom-call | tf_op jit(solution)/shard_map/pallas_call | solution.py:589
  29.3 0.8 %shard_map.141.refs_5_ = f32[4,384,128]{2,1,0:T(8,128)S(1)} custom-call(f32[4,384,128]{2,1,0:T(8,128)S(1)} %get-tuple-element.95.refs_0_.refs_1_, f32[4,8,128]{2,1,0:T(8,128)S(1)} %get-tuple-element.100.refs_1_, f32[4,8,128]{2,1,0:T(8,128)S(1)} %collective-permute-done.refs_0_.refs_2_.refs_4_, ...), custom_call_target="tpu_custom_call" | custom-call | tf_op jit(solution)/shard_map/pallas_call | solution.py:589
  30.0 0.0 collective-permute-done.8.refs_0_.refs_12_
  30.0 0.2 shard_map.142
  30.2 0.5 %collective-permute-done.9.refs_13_ = f32[8,128]{1,0:T(8,128)S(1)} collective-permute-done((f32[8,128]{1,0:T(8,128)S(1)}, f32[8,128]{1,0:T(8,128)S(1)}, u32[]{:S(2)}, u32[]{:S(2)}) %collective-permute-start.9) | collective-permute-done | bytes 4128 | tf_op jit(solution)/shard_map/ppermute | solution.py:637
  30.7 0.0 collective-permute-done.7.refs_4_
  30.7 1.6 %shard_map.143 = (f32[384,128]{1,0:T(8,128)}, f32[384,128]{1,0:T(8,128)}, f32[384,128]{1,0:T(8,128)}, f32[384,128]{1,0:T(8,128)}) custom-call(f32[8,128]{1,0:T(8,128)S(1)} %get-tuple-element.59.refs_6_.refs_0_.refs_5_, f32[4,384,128]{2,1,0:T(8,128)S(1)} %get-tuple-element.95.refs_0_.refs_1_, f32[384,128]{1,0:T(8,128)S(1)} %get-tuple-element.67.refs_6_.refs_2_, ...), custom_call_target="tpu_custom_call" | custom-call | tf_op jit(solution)/shard_map/pallas_call | solution.py:589
Async XLA Ops:
  2.4 12.3 %collective-permute-start.3 = (f32[312,128]{1,0:T(8,128)S(1)}, f32[312,128]{1,0:T(8,128)S(1)}, u32[]{:S(2)}, u32[]{:S(2)}) collective-permute-start(f32[312,128]{1,0:T(8,128)S(1)} %get-tuple-element.83), channel_id=1, source_target_pairs={{0,2},{2,0},{1,3},{3,1},{4,6},{6,4},{5,7},{7,5},{8,10},{10,8},{9,1... | collective-permute-start | bytes 479240 | tf_op jit(solution)/shard_map/ppermute | solution.py:633
  7.2 3.9 %collective-permute-start = (f32[4,8,128]{2,1,0:T(8,128)S(1)}, f32[4,8,128]{2,1,0:T(8,128)S(1)}, u32[]{:S(2)}, u32[]{:S(2)}) collective-permute-start(f32[4,8,128]{2,1,0:T(8,128)S(1)} %get-tuple-element.70), channel_id=1, source_target_pairs={{0,4},{4,0},{8,12},{12,8},{16,20},{20,16},{24,28},{28,24},{1,5},{5... | collective-permute-start | bytes 49160 | tf_op jit(solution)/shard_map/ppermute | solution.py:666
  7.3 4.1 %collective-permute-start.1 = (f32[4,8,128]{2,1,0:T(8,128)S(1)}, f32[4,8,128]{2,1,0:T(8,128)S(1)}, u32[]{:S(2)}, u32[]{:S(2)}) collective-permute-start(f32[4,8,128]{2,1,0:T(8,128)S(1)} %get-tuple-element.71), channel_id=1, source_target_pairs={{0,28},{4,8},{8,4},{12,16},{16,12},{20,24},{24,20},{28,0},{1,29},{... | collective-permute-start | bytes 49160 | tf_op jit(solution)/shard_map/ppermute | solution.py:667
  11.7 7.1 %collective-permute-start.2 = (f32[8,8,128]{2,1,0:T(8,128)S(1)}, f32[8,8,128]{2,1,0:T(8,128)S(1)}, u32[]{:S(2)}, u32[]{:S(2)}) collective-permute-start(f32[8,8,128]{2,1,0:T(8,128)S(1)} %get-tuple-element.77.refs_3_), channel_id=1, source_target_pairs={{0,1},{1,0},{2,3},{3,2},{4,5},{5,4},{6,7},{7,6},{8,9},{9,8},{10,11... | collective-permute-start | bytes 98312 | tf_op jit(solution)/shard_map/ppermute | solution.py:640
  13.3 5.4 %collective-permute-start.4 = (f32[8,128]{1,0:T(8,128)S(1)}, f32[8,128]{1,0:T(8,128)S(1)}, u32[]{:S(2)}, u32[]{:S(2)}) collective-permute-start(f32[8,128]{1,0:T(8,128)S(1)} %get-tuple-element.86), channel_id=1, source_target_pairs={{0,3},{1,2},{2,1},{3,0},{4,7},{5,6},{6,5},{7,4},{8,11},{9,10},{10,... | collective-permute-start | bytes 12296 | tf_op jit(solution)/shard_map/ppermute | solution.py:637
  19.4 10.6 %collective-permute-start.8 = (f32[240,128]{1,0:T(8,128)S(1)}, f32[240,128]{1,0:T(8,128)S(1)}, u32[]{:S(2)}, u32[]{:S(2)}) collective-permute-start(f32[240,128]{1,0:T(8,128)S(1)} %get-tuple-element.103), channel_id=1, source_target_pairs={{0,2},{2,0},{1,3},{3,1},{4,6},{6,4},{5,7},{7,5},{8,10},{10,8},{9,1... | collective-permute-start | bytes 368648 | tf_op jit(solution)/shard_map/ppermute | solution.py:633
  19.9 2.5 %collective-permute-start.5 = (f32[2,8,128]{2,1,0:T(8,128)S(1)}, f32[2,8,128]{2,1,0:T(8,128)S(1)}, u32[]{:S(2)}, u32[]{:S(2)}) collective-permute-start(f32[2,8,128]{2,1,0:T(8,128)S(1)} %get-tuple-element.96), channel_id=1, source_target_pairs={{0,4},{4,0},{8,12},{12,8},{16,20},{20,16},{24,28},{28,24},{1,5},{5... | collective-permute-start | bytes 24584 | tf_op jit(solution)/shard_map/ppermute | solution.py:666
  20.0 4.0 %collective-permute-start.6 = (f32[2,8,128]{2,1,0:T(8,128)S(1)}, f32[2,8,128]{2,1,0:T(8,128)S(1)}, u32[]{:S(2)}, u32[]{:S(2)}) collective-permute-start(f32[2,8,128]{2,1,0:T(8,128)S(1)} %get-tuple-element.97), channel_id=1, source_target_pairs={{0,28},{4,8},{8,4},{12,16},{16,12},{20,24},{24,20},{28,0},{1,29},{... | collective-permute-start | bytes 24584 | tf_op jit(solution)/shard_map/ppermute | solution.py:667
  24.3 6.4 %collective-permute-start.7 = (f32[8,8,128]{2,1,0:T(8,128)S(1)}, f32[8,8,128]{2,1,0:T(8,128)S(1)}, u32[]{:S(2)}, u32[]{:S(2)}) collective-permute-start(f32[8,8,128]{2,1,0:T(8,128)S(1)} %get-tuple-element.99.refs_3_), channel_id=1, source_target_pairs={{0,1},{1,0},{2,3},{3,2},{4,5},{5,4},{6,7},{7,6},{8,9},{9,8},{10,11... | collective-permute-start | bytes 98312 | tf_op jit(solution)/shard_map/ppermute | solution.py:640
  25.3 5.4 %collective-permute-start.9 = (f32[8,128]{1,0:T(8,128)S(1)}, f32[8,128]{1,0:T(8,128)S(1)}, u32[]{:S(2)}, u32[]{:S(2)}) collective-permute-start(f32[8,128]{1,0:T(8,128)S(1)} %get-tuple-element.109), channel_id=1, source_target_pairs={{0,3},{1,2},{2,1},{3,0},{4,7},{5,6},{6,5},{7,4},{8,11},{9,10},{10,... | collective-permute-start | bytes 12296 | tf_op jit(solution)/shard_map/ppermute | solution.py:637

commit v9 on v8

--- a/solution.py
+++ b/solution.py
@@ -105,20 +105,23 @@
 
 def fetch_kernel(dims, ids, *refs):
     levels, rows, cols, half, pair = dims
-    coup, sources, (nn_late, coupled), rest = refs[0], refs[1:10], refs[10:12], refs[12:]
+    coup, inverse, sources, (nn_late, coupled), rest = refs[0], refs[1], refs[2:9], refs[9:11], refs[11:]
     count = 1 if pair else 2
-    lat_msgs, copies, (coup_here, sems) = rest[:count], rest[count : count + 9], rest[count + 9 :]
+    lat_msgs, copies, (coup_here, blocks, sems) = rest[:count], rest[count : count + 7], rest[count + 7 :]
     moves = [pltpu.make_async_copy(a, b, sems.at[i]) for i, (a, b) in enumerate(zip(sources, copies))]
-    moves.append(pltpu.make_async_copy(coup, coup_here, sems.at[9]))
+    moves.append(pltpu.make_async_copy(coup, coup_here, sems.at[7]))
+    choices = row_choices(pair, rows, ids[0])
+    for which, row in enumerate(choices):
+        moves.append(pltpu.make_async_copy(inverse.at[row], blocks.at[which], sems.at[8 + which]))
     for move in moves:
         move.start()
-    t, s, u, v, sea, _, north, flags, inverse = copies
+    t, s, u, v, sea, north, flags = copies
     for move in moves:
         move.wait()
     spot = iota((rows, rows), 0) == iota((rows, rows), 1)
     value = jnp.sum(jnp.where(spot, coup_here[...], 0.0), axis=1, keepdims=True)
     coupled[...] = jnp.broadcast_to(value, (rows, cols))
-    for which, row in enumerate(row_choices(pair, rows, ids[0])):
+    for which, row in enumerate(choices):
         msg = lat_msgs[which]
 
         def put(j, value):
@@ -136,10 +139,7 @@
                 put(5, value)
             elif pair or row:
                 nn_late[...] = value
-        if pair:
-            block = jnp.where(row == 0, inverse[0], inverse[rows - 1])
-        else:
-            block = inverse[row]
+        block = blocks[which]
         size = block_shape(levels)
         last = pl.ds(6 * levels, size)
         msg[last, :] = jnp.zeros((size, cols), f32)
@@ -563,7 +563,7 @@
             there = pl.ds(part * size * rows, size * rows)
             for f in range(4):
                 move = pltpu.make_async_copy(work.at[f, there], outs[f].at[there], sems.at[4 * part + f])
-                move.start()
+                move.start(priority=f % 2)
                 moves.append(move)
     for move in moves:
         move.wait()
@@ -639,8 +639,8 @@
     def to_depth(msg):
         return lax.ppermute(msg, "depth", [(d, depths - 1 - d) for d in range(depths)])
 
-    sources = (*state, sea, east, north, flags, block_inverse)
-    sources = tuple(pltpu.with_memory_space_constraint(x, pltpu.HBM) for x in sources)
+    in_place = lambda x: pltpu.with_memory_space_constraint(x, pltpu.HBM)
+    sources = tuple(in_place(x) for x in (*state, sea, north, flags))
     full = 6 * levels + block_shape(levels)
     late, coupled, *rest = call(
         fetch_kernel,
@@ -648,13 +648,17 @@
         [(grid, f32), (plane, f32)]
         + [((full, cols), f32)] * count
         + [(x.shape, x.dtype) for x in sources],
-        (pltpu.with_memory_space_constraint(coupling.reshape(1, rows), pltpu.HBM), *sources),
+        (in_place(coupling.reshape(1, rows)), in_place(block_inverse), *sources),
         (),
-        (pltpu.VMEM((1, rows), f32), pltpu.SemaphoreType.DMA((10,))),
-        range(10),
+        (
+            pltpu.VMEM((1, rows), f32),
+            pltpu.VMEM((count, levels, levels), f32),
+            pltpu.SemaphoreType.DMA((8 + count,)),
+        ),
+        range(9),
     )
     lat_msgs, rest = rest[:count], rest[count:]
-    state, (sea, east, north, flags, block_inverse) = rest[:4], rest[4:]
+    state, (sea, north, flags) = rest[:4], rest[4:]
 
     def to_lon(step, state, *more):
         near, far = call(

time: 32.4 us -> 32.4 us (level)
  no operation moved by 1% of the time
where the time goes in v9:
time: 32.4 us; the launch traced here: 32.3 us
  starting transfers between devices  14.7 us (45%)
  Pallas kernels  10.8 us (33%)
  waiting for transfers between devices  5.97 us (18%)
  between operations  0.77 us (2%)
    pallas_call x15, Pallas kernels, call(): pl.pallas_call(run, out_shape=[jax.ShapeDtypeStruct(shape, kind) for shap...  10.8 us
    ppermute x2, starting transfers between devices, to_lon(): far = lax.ppermute(far, 'lon', apart)  4.22 us
    ppermute x2, starting transfers between devices, to_lat(): return [lax.ppermute(m, 'lat', r) for m, r in zip(msgs, routes)]  4.2 us
    ppermute x2, waiting for transfers between devices, to_lat(): return [lax.ppermute(m, ('lat', 'depth'), r) for m, r in zip(msgs, both)]  4.14 us
    ppermute x2, starting transfers between devices, to_lat(): return [lax.ppermute(m, ('lat', 'depth'), r) for m, r in zip(msgs, both)]  3.62 us
    ppermute x2, starting transfers between devices, to_depth(): lax.ppermute(msg, 'depth', [(d, depths - 1 - d) for d in range(depths)])  2.6 us
    ppermute x2, waiting for transfers between devices, to_lon(): far = lax.ppermute(far, 'lon', apart)  1.82 us
  transfers between devices with their start and end apart: 10, of which 4 were waited for; matrix products, arithmetic and copies ran while one was open for 0% of the time, Pallas kernels for 21%

profile of v9, /device:TPU:0, one launch (start us, length us, event | category | flops | bytes accessed | tf_op | source)
XLA Modules:
  0.0 32.3 jit_solution(16251956098666059465)
XLA Ops:
  0.6 0.0 copy-start
  0.6 1.7 %shard_map.129 = (f32[48,128]{1,0:T(8,128)S(1)}, f32[8,128]{1,0:T(8,128)S(1)}, f32[312,128]{1,0:T(8,128)S(1)}, f32[384,128]{1,0:T(8,128)S(1)}, f32[384,128]{1,0:...) custom-call(f32[1,8]{1,0:T(1,128)} %bitcast.23, ...), custom_call_target="tpu_custom_call" | custom-call | tf_op jit(solution)/shard_map/pallas_call | solution.py:589
  2.4 4.1 %collective-permute-start.3 = (f32[312,128]{1,0:T(8,128)S(1)}, f32[312,128]{1,0:T(8,128)S(1)}, u32[]{:S(2)}, u32[]{:S(2)}) collective-permute-start(f32[312,128]{1,0:T(8,128)S(1)} %get-tuple-element.79), channel_id=1, source_target_pairs={{0,2},{2,0},{1,3},{3,1},{4,6},{6,4},{5,7},{7,5},{8,10},{10,8},{9,1... | collective-permute-start | bytes 479240 | tf_op jit(solution)/shard_map/ppermute | solution.py:633
  6.5 0.0 copy-done
  6.5 0.0 copy-start.1
  6.5 0.7 %shard_map.131 = (f32[4,8,128]{2,1,0:T(8,128)S(1)}, f32[4,8,128]{2,1,0:T(8,128)S(1)}) custom-call(f32[384,128]{1,0:T(8,128)S(1)} %get-tuple-element.58.refs_0_, f32[384,128]{1,0:T(8,128)S(1)} %get-tuple-element.59.refs_1_, f32[384,128]{1,0:T(8,128)S(1)} %get-tuple-element.60.refs_2_, f32[384,128]{1,0:T(8,128)S(1)} %get-tuple-element.61.refs_3_, ...), custom_call_target="tpu_custom_call" | custom-call | tf_op jit(solution)/shard_map/pallas_call | solution.py:589
  7.2 0.0 collective-permute-start
  7.2 2.6 %collective-permute-start.1 = (f32[4,8,128]{2,1,0:T(8,128)S(1)}, f32[4,8,128]{2,1,0:T(8,128)S(1)}, u32[]{:S(2)}, u32[]{:S(2)}) collective-permute-start(f32[4,8,128]{2,1,0:T(8,128)S(1)} %get-tuple-element.67), channel_id=1, source_target_pairs={{0,28},{4,8},{8,4},{12,16},{16,12},{20,24},{24,20},{28,0},{1,29},{... | collective-permute-start | bytes 49160 | tf_op jit(solution)/shard_map/ppermute | solution.py:671
  9.8 0.0 copy-done.1
  9.8 1.3 %shard_map.130 = (f32[4,384,128]{2,1,0:T(8,128)S(1)}, f32[7,8,128]{2,1,0:T(8,128)S(1)}, f32[8,128]{1,0:T(8,128)S(1)}, f32[384,128]{1,0:T(8,128)S(1)}, bf16[384,3...) custom-call(f32[384,128]{1,0:T(8,128)S(1)} %get-tuple-element.58.ref, ...), custom_call_target="tpu_custom_call" | custom-call | tf_op jit(solution)/shard_map/pallas_call | solution.py:589
  11.0 0.0 collective-permute-done.refs_0_.refs_2_.refs_4_
  11.1 0.2 collective-permute-done.1.refs_1_.refs_3_.refs_5_
  11.3 0.3 shard_map.132
  11.6 1.6 %collective-permute-start.2 = (f32[8,8,128]{2,1,0:T(8,128)S(1)}, f32[8,8,128]{2,1,0:T(8,128)S(1)}, u32[]{:S(2)}, u32[]{:S(2)}) collective-permute-start(f32[8,8,128]{2,1,0:T(8,128)S(1)} %get-tuple-element.73.refs_3_), channel_id=1, source_target_pairs={{0,1},{1,0},{2,3},{3,2},{4,5},{5,4},{6,7},{7,6},{8,9},{9,8},{10,11... | collective-permute-start | bytes 98312 | tf_op jit(solution)/shard_map/ppermute | solution.py:640
  13.3 0.1 collective-permute-start.4
  13.4 0.5 %shard_map.133 = (f32[4,384,128]{2,1,0:T(8,128)S(1)}, f32[5,384,128]{2,1,0:T(8,128)S(1)}, f32[4,384,128]{2,1,0:T(8,128)S(1)}) custom-call(s32[384,128]{1,0:T(8,128)S(1)} %get-tuple-element.62.refs_4_.refs_0_, f32[384,128]{1,0:T(8,128)S(1)} %bitcast.14, f32[384,128]{1,0:T(8,128)S(1)} %get-tuple-element.75.refs_2_, ...), custom_call_target="tpu_custom_call" | custom-call | tf_op jit(solution)/shard_map/pallas_call | solution.py:589
  13.9 0.8 %shard_map.134.refs_5_ = f32[4,384,128]{2,1,0:T(8,128)S(1)} custom-call(f32[4,384,128]{2,1,0:T(8,128)S(1)} %get-tuple-element.63.refs_0_.refs_1_, f32[4,8,128]{2,1,0:T(8,128)S(1)} %get-tuple-element.74.refs_1_, f32[4,8,128]{2,1,0:T(8,128)S(1)} %collective-permute-done.refs_0_.refs_2_.refs_4_, ...), custom_call_target="tpu_custom_call" | custom-call | tf_op jit(solution)/shard_map/pallas_call | solution.py:589
  14.7 0.0 collective-permute-done.3.refs_0_.refs_1_.refs_11_.refs_12_
  14.7 0.3 %shard_map.135 = (f32[5,48,128]{2,1,0:T(8,128)S(1)}, f32[8,128]{1,0:T(8,128)S(1)}, bf16[48,48]{1,0:T(8,128)(2,1)S(1)}, bf16[48,48]{1,0:T(8,128)(2,1)S(1)}, f32[48,128]{1,0:T(8,128)S(1)}) custom-call(f32[312,128]{1,0:T(8,128)S(1)} %collective-permute-done.3.refs_0_.refs_1_.refs_11_.refs_12_, ...), custom_call_target="tpu_custom_call" | custom-call | tf_op jit(solution)/shard_map/pallas_call | solution.py:589
  15.0 3.7 %collective-permute-done.4.refs_13_ = f32[8,128]{1,0:T(8,128)S(1)} collective-permute-done((f32[8,128]{1,0:T(8,128)S(1)}, f32[8,128]{1,0:T(8,128)S(1)}, u32[]{:S(2)}, u32[]{:S(2)}) %collective-permute-start.4) | collective-permute-done | bytes 4128 | tf_op jit(solution)/shard_map/ppermute | solution.py:637
  18.7 0.0 collective-permute-done.2.refs_4_
  18.7 0.7 %shard_map.136 = (f32[384,128]{1,0:T(8,128)S(1)}, f32[384,128]{1,0:T(8,128)S(1)}, f32[384,128]{1,0:T(8,128)S(1)}, f32[384,128]{1,0:T(8,128)S(1)}, f32[240,128]{1,0:T(8,128)S(1)}) custom-call(f32[8,128]{1,0:T(8,128)S(1)} %get-tuple-element.57.refs_6_.refs_0_.refs_5_, f32[4,384,128]{2,1,0:T(8,128)S(1)} %get-tuple-element.63.refs_0_.refs_1_, ...), custom_call_target="tpu_custom_call" | custom-call | tf_op jit(solution)/shard_map/pallas_call | solution.py:589
  19.4 0.1 collective-permute-start.8
  19.5 0.4 %shard_map.138 = (f32[2,8,128]{2,1,0:T(8,128)S(1)}, f32[2,8,128]{2,1,0:T(8,128)S(1)}) custom-call(f32[384,128]{1,0:T(8,128)S(1)} %get-tuple-element.84.refs_0_, f32[384,128]{1,0:T(8,128)S(1)} %get-tuple-element.85.refs_1_, f32[384,128]{1,0:T(8,128)S(1)} %get-tuple-element.86.refs_2_, f32[384,128]{1,0:T(8,128)S(1)} %get-tuple-element.87.refs_3_), custom_call_target="tpu_custom_call" | custom-call | tf_op jit(solution)/shard_map/pallas_call | solution.py:589
  19.8 0.1 collective-permute-start.5
  19.9 1.6 %collective-permute-start.6 = (f32[2,8,128]{2,1,0:T(8,128)S(1)}, f32[2,8,128]{2,1,0:T(8,128)S(1)}, u32[]{:S(2)}, u32[]{:S(2)}) collective-permute-start(f32[2,8,128]{2,1,0:T(8,128)S(1)} %get-tuple-element.93), channel_id=1, source_target_pairs={{0,28},{4,8},{8,4},{12,16},{16,12},{20,24},{24,20},{28,0},{1,29},{... | collective-permute-start | bytes 24584 | tf_op jit(solution)/shard_map/ppermute | solution.py:671
  21.6 0.8 %shard_map.137 = (f32[4,384,128]{2,1,0:T(8,128)S(1)}, f32[7,8,128]{2,1,0:T(8,128)S(1)}, f32[8,128]{1,0:T(8,128)S(1)}) custom-call(f32[384,128]{1,0:T(8,128)S(1)} %get-tuple-element.84.refs_0_, f32[384,128]{1,0:T(8,128)S(1)} %get-tuple-element.85.refs_1_, f32[384,128]{1,0:T(8,128)S(1)} %get-tuple-element.86.refs_2_, ...), custom_call_target="tpu_custom_call" | custom-call | tf_op jit(solution)/shard_map/pallas_call | solution.py:589
  22.4 0.0 collective-permute-done.5.refs_0_
  22.4 1.6 %collective-permute-done.6.refs_1_ = f32[2,8,128]{2,1,0:T(8,128)S(1)} collective-permute-done((f32[2,8,128]{2,1,0:T(8,128)S(1)}, f32[2,8,128]{2,1,0:T(8,128)S(1)}, u32[]{:S(2)}, u32[]{:S(2)}) %collective-permute-start.6) | collective-permute-done | bytes 8224 | tf_op jit(solution)/shard_map/ppermute | solution.py:671
  24.0 0.3 shard_map.139
  24.3 1.0 %collective-permute-start.7 = (f32[8,8,128]{2,1,0:T(8,128)S(1)}, f32[8,8,128]{2,1,0:T(8,128)S(1)}, u32[]{:S(2)}, u32[]{:S(2)}) collective-permute-start(f32[8,8,128]{2,1,0:T(8,128)S(1)} %get-tuple-element.95.refs_3_), channel_id=1, source_target_pairs={{0,1},{1,0},{2,3},{3,2},{4,5},{5,4},{6,7},{7,6},{8,9},{9,8},{10,11... | collective-permute-start | bytes 98312 | tf_op jit(solution)/shard_map/ppermute | solution.py:640
  25.2 3.5 %collective-permute-start.9 = (f32[8,128]{1,0:T(8,128)S(1)}, f32[8,128]{1,0:T(8,128)S(1)}, u32[]{:S(2)}, u32[]{:S(2)}) collective-permute-start(f32[8,128]{1,0:T(8,128)S(1)} %get-tuple-element.105), channel_id=1, source_target_pairs={{0,3},{1,2},{2,1},{3,0},{4,7},{5,6},{6,5},{7,4},{8,11},{9,10},{10,... | collective-permute-start | bytes 12296 | tf_op jit(solution)/shard_map/ppermute | solution.py:637
  28.7 0.5 %shard_map.140 = (f32[4,384,128]{2,1,0:T(8,128)S(1)}, f32[5,384,128]{2,1,0:T(8,128)S(1)}) custom-call(s32[384,128]{1,0:T(8,128)S(1)} %get-tuple-element.62.refs_4_.refs_0_, f32[384,128]{1,0:T(8,128)S(1)} %bitcast.15, f32[384,128]{1,0:T(8,128)S(1)} %get-tuple-element.75.refs_2_, s32[2,384,128]{2,1,0:T(8,128)S(1)} %get-tuple-element.65.refs_6_.refs_3_, ...), custom_call_target="tpu_custom_call" | custom-call | tf_op jit(solution)/shard_map/pallas_call | solution.py:589
  29.2 0.8 %shard_map.141.refs_5_ = f32[4,384,128]{2,1,0:T(8,128)S(1)} custom-call(f32[4,384,128]{2,1,0:T(8,128)S(1)} %get-tuple-element.91.refs_0_.refs_1_, f32[4,8,128]{2,1,0:T(8,128)S(1)} %get-tuple-element.96.refs_1_, f32[4,8,128]{2,1,0:T(8,128)S(1)} %collective-permute-done.refs_0_.refs_2_.refs_4_, ...), custom_call_target="tpu_custom_call" | custom-call | tf_op jit(solution)/shard_map/pallas_call | solution.py:589
  30.0 0.0 collective-permute-done.8.refs_0_.refs_12_
  30.0 0.2 shard_map.142
  30.2 0.5 %collective-permute-done.9.refs_13_ = f32[8,128]{1,0:T(8,128)S(1)} collective-permute-done((f32[8,128]{1,0:T(8,128)S(1)}, f32[8,128]{1,0:T(8,128)S(1)}, u32[]{:S(2)}, u32[]{:S(2)}) %collective-permute-start.9) | collective-permute-done | bytes 4128 | tf_op jit(solution)/shard_map/ppermute | solution.py:637
  30.7 0.0 collective-permute-done.7.refs_4_
  30.7 1.6 %shard_map.143 = (f32[384,128]{1,0:T(8,128)}, f32[384,128]{1,0:T(8,128)}, f32[384,128]{1,0:T(8,128)}, f32[384,128]{1,0:T(8,128)}) custom-call(f32[8,128]{1,0:T(8,128)S(1)} %get-tuple-element.57.refs_6_.refs_0_.refs_5_, f32[4,384,128]{2,1,0:T(8,128)S(1)} %get-tuple-element.91.refs_0_.refs_1_, f32[384,128]{1,0:T(8,128)S(1)} %get-tuple-element.64.refs_6_.refs_2_, ...), custom_call_target="tpu_custom_call" | custom-call | tf_op jit(solution)/shard_map/pallas_call | solution.py:589
Async XLA Ops:
  0.6 5.9 %copy-start = (f32[48,8,128]{2,1,0:T(8,128)S(1)}, f32[48,8,128]{2,1,0:T(8,128)}, u32[]{:S(2)}) copy-start(f32[48,8,128]{2,1,0:T(8,128)} %param.14) | copy-start | bytes 589828
  2.4 12.3 %collective-permute-start.3 = (f32[312,128]{1,0:T(8,128)S(1)}, f32[312,128]{1,0:T(8,128)S(1)}, u32[]{:S(2)}, u32[]{:S(2)}) collective-permute-start(f32[312,128]{1,0:T(8,128)S(1)} %get-tuple-element.79), channel_id=1, source_target_pairs={{0,2},{2,0},{1,3},{3,1},{4,6},{6,4},{5,7},{7,5},{8,10},{10,8},{9,1... | collective-permute-start | bytes 479240 | tf_op jit(solution)/shard_map/ppermute | solution.py:633
  6.5 3.3 %copy-start.1 = (f32[8,48,48]{2,1,0:T(8,128)S(1)}, f32[8,48,48]{2,1,0:T(8,128)}, u32[]{:S(2)}) copy-start(f32[8,48,48]{2,1,0:T(8,128)} %refs_5_.1) | copy-start | bytes 221188
  7.2 3.8 %collective-permute-start = (f32[4,8,128]{2,1,0:T(8,128)S(1)}, f32[4,8,128]{2,1,0:T(8,128)S(1)}, u32[]{:S(2)}, u32[]{:S(2)}) collective-permute-start(f32[4,8,128]{2,1,0:T(8,128)S(1)} %get-tuple-element.66), channel_id=1, source_target_pairs={{0,4},{4,0},{8,12},{12,8},{16,20},{20,16},{24,28},{28,24},{1,5},{5... | collective-permute-start | bytes 49160 | tf_op jit(solution)/shard_map/ppermute | solution.py:670
  7.2 4.1 %collective-permute-start.1 = (f32[4,8,128]{2,1,0:T(8,128)S(1)}, f32[4,8,128]{2,1,0:T(8,128)S(1)}, u32[]{:S(2)}, u32[]{:S(2)}) collective-permute-start(f32[4,8,128]{2,1,0:T(8,128)S(1)} %get-tuple-element.67), channel_id=1, source_target_pairs={{0,28},{4,8},{8,4},{12,16},{16,12},{20,24},{24,20},{28,0},{1,29},{... | collective-permute-start | bytes 49160 | tf_op jit(solution)/shard_map/ppermute | solution.py:671
  11.6 7.1 %collective-permute-start.2 = (f32[8,8,128]{2,1,0:T(8,128)S(1)}, f32[8,8,128]{2,1,0:T(8,128)S(1)}, u32[]{:S(2)}, u32[]{:S(2)}) collective-permute-start(f32[8,8,128]{2,1,0:T(8,128)S(1)} %get-tuple-element.73.refs_3_), channel_id=1, source_target_pairs={{0,1},{1,0},{2,3},{3,2},{4,5},{5,4},{6,7},{7,6},{8,9},{9,8},{10,11... | collective-permute-start | bytes 98312 | tf_op jit(solution)/shard_map/ppermute | solution.py:640
  13.3 5.4 %collective-permute-start.4 = (f32[8,128]{1,0:T(8,128)S(1)}, f32[8,128]{1,0:T(8,128)S(1)}, u32[]{:S(2)}, u32[]{:S(2)}) collective-permute-start(f32[8,128]{1,0:T(8,128)S(1)} %get-tuple-element.82), channel_id=1, source_target_pairs={{0,3},{1,2},{2,1},{3,0},{4,7},{5,6},{6,5},{7,4},{8,11},{9,10},{10,... | collective-permute-start | bytes 12296 | tf_op jit(solution)/shard_map/ppermute | solution.py:637
  19.4 10.6 %collective-permute-start.8 = (f32[240,128]{1,0:T(8,128)S(1)}, f32[240,128]{1,0:T(8,128)S(1)}, u32[]{:S(2)}, u32[]{:S(2)}) collective-permute-start(f32[240,128]{1,0:T(8,128)S(1)} %get-tuple-element.99), channel_id=1, source_target_pairs={{0,2},{2,0},{1,3},{3,1},{4,6},{6,4},{5,7},{7,5},{8,10},{10,8},{9,1... | collective-permute-start | bytes 368648 | tf_op jit(solution)/shard_map/ppermute | solution.py:633
  19.8 2.5 %collective-permute-start.5 = (f32[2,8,128]{2,1,0:T(8,128)S(1)}, f32[2,8,128]{2,1,0:T(8,128)S(1)}, u32[]{:S(2)}, u32[]{:S(2)}) collective-permute-start(f32[2,8,128]{2,1,0:T(8,128)S(1)} %get-tuple-element.92), channel_id=1, source_target_pairs={{0,4},{4,0},{8,12},{12,8},{16,20},{20,16},{24,28},{28,24},{1,5},{5... | collective-permute-start | bytes 24584 | tf_op jit(solution)/shard_map/ppermute | solution.py:670
  19.9 4.0 %collective-permute-start.6 = (f32[2,8,128]{2,1,0:T(8,128)S(1)}, f32[2,8,128]{2,1,0:T(8,128)S(1)}, u32[]{:S(2)}, u32[]{:S(2)}) collective-permute-start(f32[2,8,128]{2,1,0:T(8,128)S(1)} %get-tuple-element.93), channel_id=1, source_target_pairs={{0,28},{4,8},{8,4},{12,16},{16,12},{20,24},{24,20},{28,0},{1,29},{... | collective-permute-start | bytes 24584 | tf_op jit(solution)/shard_map/ppermute | solution.py:671
  24.3 6.4 %collective-permute-start.7 = (f32[8,8,128]{2,1,0:T(8,128)S(1)}, f32[8,8,128]{2,1,0:T(8,128)S(1)}, u32[]{:S(2)}, u32[]{:S(2)}) collective-permute-start(f32[8,8,128]{2,1,0:T(8,128)S(1)} %get-tuple-element.95.refs_3_), channel_id=1, source_target_pairs={{0,1},{1,0},{2,3},{3,2},{4,5},{5,4},{6,7},{7,6},{8,9},{9,8},{10,11... | collective-permute-start | bytes 98312 | tf_op jit(solution)/shard_map/ppermute | solution.py:640
  25.2 5.4 %collective-permute-start.9 = (f32[8,128]{1,0:T(8,128)S(1)}, f32[8,128]{1,0:T(8,128)S(1)}, u32[]{:S(2)}, u32[]{:S(2)}) collective-permute-start(f32[8,128]{1,0:T(8,128)S(1)} %get-tuple-element.105), channel_id=1, source_target_pairs={{0,3},{1,2},{2,1},{3,0},{4,7},{5,6},{6,5},{7,4},{8,11},{9,10},{10,... | collective-permute-start | bytes 12296 | tf_op jit(solution)/shard_map/ppermute | solution.py:637
